TPU v7x, 256 devices: a whole 4x4x8 slice. The times are simulated.
256 devices in a mesh: dp: 4 (over y), expert: 16 (over z, core), ffn: 4 (over x).
Axes of the slice: x: 4, y: 4, z: 8, core: 2. Of those that a mesh axis runs over, the one named last changes fastest.
Arguments:
- tokens: bfloat16 [8192, 7168], P(('dp', 'expert'), 'ffn'), may hold values from -6 to 6
- grad_out: bfloat16 [8192, 7168], P(('dp', 'expert'), 'ffn'), may hold values from -3 to 3
- route_ids: int32 [8192, 2], P(('dp', 'expert')), may hold values from 0 to 15, all different within a row; in each aligned block of 128 rows (0 to 127, 128 to 255, ...) at most 20 rows name the same one
- combine: float32 [8192, 2], P(('dp', 'expert')), may hold values from 0.2 to 1
- gate_weight: bfloat16 [16, 7168, 1024], P('expert', 'dp', 'ffn'), may hold values from -0.0625 to 0.0625
- up_weight: bfloat16 [16, 7168, 1024], P('expert', 'dp', 'ffn'), may hold values from -0.0625 to 0.0625
- down_weight: bfloat16 [16, 1024, 7168], P('expert', 'ffn', 'dp'), may hold values from -0.1875 to 0.1875
Outputs:
- grad_tokens: bfloat16 [8192, 7168], P(('dp', 'expert'), 'ffn')
- grad_gate: float32 [16, 7168, 1024], P('expert', 'dp', 'ffn')
- grad_up: float32 [16, 7168, 1024], P('expert', 'dp', 'ffn')
- grad_down: float32 [16, 1024, 7168], P('expert', 'ffn', 'dp')
Inputs may be any that keep to these rules, and one draw needn't show every extreme that they name: `route_ids`: each row names 2 different experts; every expert is named by some row. In each aligned block of 128 rows (the rows of one device) no expert is named by more than 20 rows, a bound that some block reaches.
All inputs are finite; a program needn't handle non-finite values.
Results may differ from a plain program's by a relative error of at most 0.019.
Values may be sent and summed in bfloat16 or wider, within the bound.
No kernel may reach another device: no remote copies, remote signals or barrier semaphores. Data moves between devices by JAX's collectives and lax.ppermute only.
A program may use at most 128 MiB of HBM per device.

v0:
```python
import jax
import jax.numpy as jnp
from jax import lax
from jax.experimental import pallas as pl
from jax.experimental.pallas import tpu as pltpu
from jax.sharding import PartitionSpec as P


F32 = jnp.float32
BF16 = jnp.bfloat16
N = 4
ANY = pl.BlockSpec(memory_space=pl.ANY)
SMEM = pl.BlockSpec(memory_space=pltpu.SMEM)


def dot(a, b, contract):
    return lax.dot_general(a, b, (contract, ((), ())), preferred_element_type=F32)


NN, NT, TN = ((1,), (0,)), ((1,), (1,)), ((0,), (0,))


def call(body, outs, scratch, args, copies):
    return pl.pallas_call(
        body,
        out_shape=outs,
        in_specs=[SMEM] + [ANY] * (len(args) - 1),
        out_specs=jax.tree.map(lambda _: ANY, outs),
        scratch_shapes=list(scratch) + [pltpu.SemaphoreType.DMA((copies,))],
    )(*args)


def start(src, dst, sem):
    copy = pltpu.make_async_copy(src, dst, sem)
    copy.start()
    return copy


def wrap(x):
    return x & (N - 1)


def vmem(*shape, dtype=BF16):
    return pltpu.VMEM(shape, dtype)


def project(parts, w_in, at, offset, base=None, grads=None):
    _, rows, width = parts[0].shape
    cols = w_in.shape[2]
    units = cols // 2
    last = base is not None

    def body(at_ref, w_ref, *refs):
        x_refs, refs = refs[:N], refs[N:]
        if last:
            (base_ref, grad_ref), refs = refs[:2], refs[2:]
            out_h, out_a, w_buf, x_buf, total, h_buf, a_buf, grad_buf, sems = refs
        else:
            out, w_buf, x_buf, total, sems = refs
        for j in range(N):
            start(w_ref.at[wrap(at_ref[0] + j), pl.ds(offset, 2 * width)], w_buf.at[j], sems.at[j])
            start(x_refs[j], x_buf.at[j], sems.at[N + j])
        if last:
            first = start(base_ref, total, sems.at[2 * N])
            second = start(grad_ref, grad_buf, sems.at[2 * N + 1])
            first.wait()
        else:
            total[...] = jnp.zeros_like(total)

        def step(j, carry):
            pltpu.make_async_copy(w_ref.at[0, pl.ds(offset, 2 * width)], w_buf.at[j], sems.at[j]).wait()
            pltpu.make_async_copy(x_refs[0], x_buf.at[j], sems.at[N + j]).wait()
            total[...] += dot(x_buf[j, 0], w_buf[j, :width], NN) + dot(x_buf[j, 1], w_buf[j, width:], NN)
            return carry

        lax.fori_loop(0, N, step, 0)
        if last:
            second.wait()
            grad = sum(grad_buf[j].astype(F32) for j in range(N))
            gate, up = total[:, :units], total[:, units:]
            sig = jax.nn.sigmoid(gate)
            h_buf[...] = (gate * sig * up).astype(BF16)
            a_buf[:, :units] = (grad * up * sig * (1.0 + gate * (1.0 - sig))).astype(BF16)
            a_buf[:, units:] = (grad * gate * sig).astype(BF16)
            stores = [start(h_buf, out_h, sems.at[0]), start(a_buf, out_a, sems.at[1])]
        else:
            stores = [start(total, out, sems.at[0])]
        for copy in stores:
            copy.wait()

    scratch = [vmem(N, 2 * width, cols), vmem(N, 2, rows, width), vmem(rows, cols, dtype=F32)]
    if not last:
        return call(body, jax.ShapeDtypeStruct((rows, cols), F32), scratch, [at, w_in] + parts, 2 * N)
    outs = (jax.ShapeDtypeStruct((rows, units), BF16), jax.ShapeDtypeStruct((rows, cols), BF16))
    scratch += [vmem(rows, units), vmem(rows, cols), vmem(N, rows, units)]
    return call(body, outs, scratch, [at, w_in] + parts + [base, grads], 2 * N + 2)


def fetch(chunks, x_refs, x_bufs, sems, base):
    for j in range(N):
        for h in range(len(chunks)):
            start(x_refs[h * N + j], x_bufs[h].at[j], sems.at[base + h * N + j])


def arrived(x_refs, x_bufs, sems, base, h, j):
    pltpu.make_async_copy(x_refs[h * N], x_bufs[h].at[j], sems.at[base + h * N + j]).wait()


def flat(chunks):
    return [x for parts in chunks for x in parts]


def buffers(chunks):
    return [vmem(N, *parts[0].shape) for parts in chunks]


def hidden_grads(chunks, w_down, at):
    rows = chunks[0][0].shape[1]
    units, width = w_down.shape
    count = len(chunks)

    def body(at_ref, w_ref, *refs):
        x_refs, (out, w_buf, *x_bufs, out_buf, sems) = refs[: count * N], refs[count * N :]
        first = start(w_ref, w_buf, sems.at[0])
        fetch(chunks, x_refs, x_bufs, sems, 1 + N)
        first.wait()

        def step(j, carry):
            total, lo = None, 0
            for h in range(count):
                w = x_bufs[h].shape[3]
                arrived(x_refs, x_bufs, sems, 1 + N, h, j)
                for c in range(2):
                    term = dot(x_bufs[h][j, c], w_buf[:, lo : lo + w], NT)
                    total = term if total is None else total + term
                    lo += w
            out_buf[j] = total.astype(BF16)
            start(out_buf.at[j], out.at[wrap(at_ref[0] + j)], sems.at[1 + j])
            return carry

        lax.fori_loop(0, N, step, 0)
        for j in range(N):
            pltpu.make_async_copy(out_buf.at[j], out.at[0], sems.at[1 + j]).wait()

    scratch = [vmem(units, width)] + buffers(chunks) + [vmem(N, rows, units)]
    out = jax.ShapeDtypeStruct((N, rows, units), BF16)
    return call(body, out, scratch, [at, w_down] + flat(chunks), 1 + N + count * N)


def weight_grad(chunks, acts, at, lo_col):
    rows, cols = acts.shape
    units = cols // 2
    width = sum(2 * parts[0].shape[2] for parts in chunks)
    count = len(chunks)

    def body(at_ref, a_ref, *refs):
        x_refs, (out, a_buf, *x_bufs, out_buf, sems) = refs[: count * N], refs[count * N :]
        first = start(a_ref, a_buf, sems.at[0])
        fetch(chunks, x_refs, x_bufs, sems, 1 + N)
        first.wait()

        def step(j, carry):
            lo = 0
            for h in range(count):
                w = x_bufs[h].shape[3]
                arrived(x_refs, x_bufs, sems, 1 + N, h, j)
                for c in range(2):
                    grads = dot(x_bufs[h][j, c], a_buf[:, lo_col : lo_col + units], TN)
                    out_buf[j, lo : lo + w] = grads.astype(BF16)
                    lo += w
            start(out_buf.at[j], out.at[wrap(at_ref[0] + j)], sems.at[1 + j])
            return carry

        lax.fori_loop(0, N, step, 0)
        for j in range(N):
            pltpu.make_async_copy(out_buf.at[j], out.at[0], sems.at[1 + j]).wait()

    scratch = [vmem(rows, cols)] + buffers(chunks) + [vmem(N, width, units)]
    out = jax.ShapeDtypeStruct((N, width, units), BF16)
    return call(body, out, scratch, [at, acts] + flat(chunks), 1 + N + count * N)


def down_grad(chunks, hidden, at):
    _, rows, units = hidden.shape
    width = sum(2 * parts[0].shape[2] for parts in chunks)
    count = len(chunks)

    def body(at_ref, h_ref, *refs):
        x_refs, (out, h_buf, *x_bufs, out_buf, sems) = refs[: count * N], refs[count * N :]
        first = start(h_ref, h_buf, sems.at[0])
        fetch(chunks, x_refs, x_bufs, sems, 1)
        out_buf[...] = jnp.zeros_like(out_buf)
        first.wait()

        def step(j, carry):
            lo = 0
            for h in range(count):
                w = x_bufs[h].shape[3]
                arrived(x_refs, x_bufs, sems, 1, h, j)
                for c in range(2):
                    out_buf[:, lo : lo + w] += dot(h_buf[wrap(at_ref[0] + j)], x_bufs[h][j, c], TN)
                    lo += w
            return carry

        lax.fori_loop(0, N, step, 0)
        start(out_buf, out, sems.at[0]).wait()

    scratch = [vmem(N, rows, units)] + buffers(chunks) + [vmem(units, width, dtype=F32)]
    out = jax.ShapeDtypeStruct((units, width), F32)
    return call(body, out, scratch, [at, hidden] + flat(chunks), 1 + count * N)


def input_partials(acts, w_in, at, offset, width):
    rows, cols = acts.shape

    def body(at_ref, a_ref, w_ref, *refs):
        outs, (a_buf, w_buf, out_buf, sems) = refs[: N - 1], refs[N - 1 :]
        first = start(a_ref, a_buf, sems.at[0])
        for j in range(1, N):
            start(w_ref.at[wrap(at_ref[0] + j), pl.ds(offset, 2 * width)], w_buf.at[j - 1], sems.at[j])
        first.wait()

        def step(j, carry):
            pltpu.make_async_copy(w_ref.at[0, pl.ds(offset, 2 * width)], w_buf.at[j], sems.at[1 + j]).wait()
            for c in range(2):
                out_buf[j, c] = dot(a_buf[...], w_buf[j, c * width : (c + 1) * width], NT).astype(BF16)
            return carry

        lax.fori_loop(0, N - 1, step, 0)
        stores = [start(out_buf.at[j], outs[j], sems.at[j]) for j in range(N - 1)]
        for copy in stores:
            copy.wait()

    outs = (jax.ShapeDtypeStruct((2, rows, width), BF16),) * (N - 1)
    scratch = [vmem(rows, cols), vmem(N - 1, 2 * width, cols), vmem(N - 1, 2, rows, width)]
    return call(body, outs, scratch, [at, acts, w_in], N)


def input_totals(acts, w_in, at, offset, received, order):
    rows, cols = acts.shape
    _, _, width = received[0].shape

    def body(at_ref, a_ref, w_ref, order_ref, *refs):
        r_refs, (out, a_buf, w_buf, o_buf, r_buf, t_buf, out_buf, sems) = refs[: N - 1], refs[N - 1 :]
        copies = [
            start(a_ref, a_buf, sems.at[0]),
            start(w_ref.at[at_ref[0], pl.ds(offset, 2 * width)], w_buf, sems.at[1]),
            start(order_ref, o_buf, sems.at[2]),
        ]
        copies += [start(r_refs[j], r_buf.at[j], sems.at[3 + j]) for j in range(N - 1)]
        for copy in copies:
            copy.wait()
        for c in range(2):
            total = dot(a_buf[...], w_buf[c * width : (c + 1) * width], NT)
            for j in range(N - 1):
                total = total + r_buf[j, c].astype(F32)
            t_buf[c * rows : (c + 1) * rows] = total.astype(BF16)

        def step(i, carry):
            block = pl.ds(i * (rows // 2), rows // 2)
            out_buf[block] = dot(o_buf[block], t_buf[...], NN).astype(BF16)
            return carry

        lax.fori_loop(0, 4, step, 0)
        start(out_buf, out, sems.at[0]).wait()

    scratch = [vmem(rows, cols), vmem(2 * width, cols), vmem(2 * rows, 2 * rows), vmem(N - 1, 2, rows, width)]
    scratch += [vmem(2 * rows, width), vmem(2 * rows, width)]
    out = jax.ShapeDtypeStruct((2 * rows, width), BF16)
    return call(body, out, scratch, [at, acts, w_in, order] + list(received), 3 + N - 1)


def slots_of(route, experts, stride):
    rows, top = route.shape
    expert_of = route.reshape(rows * top)
    onehot = (expert_of[:, None] == jnp.arange(experts, dtype=jnp.int32)[None, :]).astype(jnp.int32)
    earlier = jnp.cumsum(onehot, axis=0) - onehot
    position = jnp.sum(earlier * onehot, axis=1)
    return (expert_of * stride + position).reshape(rows, top)


def per_device(tokens, grad_out, route_ids, combine, gate_weight, up_weight, down_weight):
    rows, width = tokens.shape
    top = route_ids.shape[1]
    groups = lax.axis_size("expert")
    experts = gate_weight.shape[0] * groups
    capacity = min(rows, (5 * top * rows + 4 * experts - 1) // (4 * experts))
    slots = experts * capacity
    piece = (width // 4 + 127) // 128 * 128
    pieces = (piece, width // 2 - piece)
    starts = (0, 2 * piece)
    at = lax.axis_index("ffn").astype(jnp.int32)[None]

    def shift(x, by):
        return lax.ppermute(x, "ffn", [(i, (i + by) % N) for i in range(N)])

    def flip(x):
        return lax.ppermute(
            x, ("dp", "ffn"), [(a * N + b, b * N + a) for a in range(N) for b in range(N)]
        )

    def exchange(x):
        return lax.all_to_all(x, "expert", split_axis=0, concat_axis=0, tiled=True)

    def gather_rows(packed):
        received = exchange(packed)
        own = dot(order, received.reshape(2 * slots, -1), NN).astype(BF16).reshape(2, slots, -1)
        return [own, shift(own, -1), shift(own, 2), shift(own, 1)]

    z_local = flip(grad_out)

    to = jnp.arange(2 * slots, dtype=jnp.int32)
    to = to % slots // capacity * (2 * capacity) + to // slots * capacity + to % capacity
    order = (to[:, None] == jnp.arange(2 * slots, dtype=jnp.int32)[None, :]).astype(BF16)
    order_back = (jnp.arange(2 * slots, dtype=jnp.int32)[:, None] == to[None, :]).astype(BF16)

    w_in = jnp.concatenate([gate_weight[0], up_weight[0]], axis=1)
    w_in = lax.all_gather(w_in, "dp", axis=0, tiled=False)

    slot_index = jnp.arange(2 * slots, dtype=jnp.int32)[:, None]

    def hits_of(slot):
        return [[slot_index == (slot[:, k] + c * capacity)[None, :] for k in range(top)] for c in range(2)]

    def one_hot(hits):
        return jnp.concatenate([sum(h.astype(BF16) for h in hit) for hit in hits], axis=1)

    slot = slots_of(route_ids, experts, 2 * capacity)
    x_place = one_hot(hits_of(slot))
    routing = flip(jnp.concatenate([slot.astype(F32), combine], axis=1))
    z_hits = hits_of(routing[:, :top].astype(jnp.int32))
    z_place = one_hot(z_hits)
    z_scale = jnp.zeros((), F32)
    for hit in z_hits:
        for k in range(top):
            z_scale = jnp.where(hit[k], routing[:, top + k][None, :], z_scale)
    z_scale = jnp.sum(z_scale, axis=1)[:, None]

    def stacked(x, h):
        lo, w = starts[h], pieces[h]
        return jnp.concatenate([x[:, lo : lo + w], x[:, lo + w : lo + 2 * w]], axis=0)

    def pack_x(h):
        return dot(x_place, stacked(tokens, h), NN).astype(BF16).reshape(groups, 2 * capacity, -1)

    def pack_z(h):
        packed = dot(z_place, stacked(z_local, h), NN) * z_scale
        return packed.astype(BF16).reshape(groups, 2 * capacity, -1)

    x_0 = gather_rows(pack_x(0))
    z_0 = gather_rows(pack_z(0))
    z_1 = gather_rows(pack_z(1))
    x_1 = gather_rows(pack_x(1))

    partial = hidden_grads((z_0, z_1), down_weight[0], at)
    grads = lax.all_to_all(partial, "dp", split_axis=0, concat_axis=0, tiled=True)
    base = project(x_0, w_in, at, starts[0])
    hidden, acts = project(x_1, w_in, at, starts[1], base, grads)

    part_gate = weight_grad((x_0, x_1), acts, at, 0)
    grad_gate = lax.psum_scatter(part_gate, "dp", scatter_dimension=0, tiled=True)
    grad_gate = grad_gate.astype(F32)
    leads = [input_partials(acts, w_in, at, starts[h], pieces[h]) for h in range(2)]
    received = []
    for h in range(2):
        received.append([shift(leads[h][j - 1], j) for j in range(1, N)])
    part_up = weight_grad((x_0, x_1), acts, at, gate_weight.shape[2])
    grad_up = lax.psum_scatter(part_up, "dp", scatter_dimension=0, tiled=True).astype(F32)

    grad_tokens = []
    for h in range(2):
        total = input_totals(acts, w_in, at, starts[h], received[h], order_back)
        back = exchange(total.reshape(groups, 2 * capacity, -1))
        back = back.reshape(2 * slots, -1)
        back = dot(x_place, back, TN).astype(BF16)
        grad_tokens += [back[:rows], back[rows:]]
    grad_tokens = jnp.concatenate(grad_tokens, axis=1)

    hidden = lax.optimization_barrier((hidden, leads[1][0]))[0]
    hidden_all = lax.all_gather(hidden, "dp", axis=0, tiled=False)
    grad_down = down_grad((z_0, z_1), hidden_all, at)[None]
    return grad_tokens, grad_gate, grad_up, grad_down


def solution(mesh):
    return jax.shard_map(
        per_device,
        mesh=mesh,
        in_specs=(
            P(("dp", "expert"), "ffn"),
            P(("dp", "expert"), "ffn"),
            P(("dp", "expert"), None),
            P(("dp", "expert"), None),
            P("expert", "dp", "ffn"),
            P("expert", "dp", "ffn"),
            P("expert", "ffn", "dp"),
        ),
        out_specs=(
            P(("dp", "expert"), "ffn"),
            P("expert", "dp", "ffn"),
            P("expert", "dp", "ffn"),
            P("expert", "ffn", "dp"),
        ),
        check_vma=False,
    )
```

profile of v0, /device:TPU:1, one launch (start us, length us, event | category | flops | bytes accessed | tf_op | source)
XLA Modules:
  0.0 345.2 jit_solution(16061100436289539866)
XLA Ops:
  7.2 2.8 pad_maximum_fusion
  13.9 1.2 convolution_convert_fusion
  15.0 10.0 %all-to-all-start.1 = ((bf16[16,40,512]{2,1,0:T(8,128)(2,1)}), bf16[16,40,512]{2,1,0:T(8,128)(2,1)S(1)}, u32[]{:S(2)}, u32[]{:S(2)}) async-start(bf16[16,40,512]{2,1,0:T(8,128)(2,1)} %bitcast.10), calls=%async_computation.1 | async-start | bytes 1310720 | tf_op jit(solution)/shard_map/all_to_all | solution.py:303
  25.4 1.1 fusion.8
  26.6 18.4 %all-to-all-done.1 = bf16[16,40,512]{2,1,0:T(8,128)(2,1)S(1)} async-done(((bf16[16,40,512]{2,1,0:T(8,128)(2,1)}), bf16[16,40,512]{2,1,0:T(8,128)(2,1)S(1)}, u32[]{:S(2)}, u32[]{:S(2)}) %all-to-all-start.1) | async-done | bytes 655392 | tf_op jit(solution)/shard_map/all_to_all | solution.py:303
  44.9 3.5 %all-to-all-start.3 = ((bf16[16,40,384]{2,1,0:T(8,128)(2,1)}), bf16[16,40,384]{2,1,0:T(8,128)(2,1)S(1)}, u32[]{:S(2)}, u32[]{:S(2)}) async-start(bf16[16,40,384]{2,1,0:T(8,128)(2,1)} %bitcast.21), calls=%async_computation.3 | async-start | bytes 983040 | tf_op jit(solution)/shard_map/all_to_all | solution.py:303
  48.5 1.2 fusion.7
  49.6 14.9 %all-to-all-done.3 = bf16[16,40,384]{2,1,0:T(8,128)(2,1)S(1)} async-done(((bf16[16,40,384]{2,1,0:T(8,128)(2,1)}), bf16[16,40,384]{2,1,0:T(8,128)(2,1)S(1)}, u32[]{:S(2)}, u32[]{:S(2)}) %all-to-all-start.3) | async-done | bytes 491552 | tf_op jit(solution)/shard_map/all_to_all | solution.py:303
  64.5 3.5 %all-to-all-start.2 = ((bf16[16,40,512]{2,1,0:T(8,128)(2,1)}), bf16[16,40,512]{2,1,0:T(8,128)(2,1)S(1)}, u32[]{:S(2)}, u32[]{:S(2)}) async-start(bf16[16,40,512]{2,1,0:T(8,128)(2,1)} %bitcast.18), calls=%async_computation.2 | async-start | bytes 1310720 | tf_op jit(solution)/shard_map/all_to_all | solution.py:303
  68.7 10.4 %collective-permute-start.11 = (bf16[2,320,384]{2,1,0:T(8,128)(2,1)S(1)}, bf16[2,320,384]{2,1,0:T(8,128)(2,1)S(1)}, u32[]{:S(2)}, u32[]{:S(2)}) collective-permute-start(bf16[2,320,384]{2,1,0:T(8,128)(2,1)S(1)} %bitcast.88), channel_id=1, source_target_pairs={{0,3},{1,0},{2,1},{3,2},{4,7},{5,4},{6,5},{7,6},{8,11},{9,8},{10,9... | collective-permute-start | bytes 1474568 | tf_op jit(solution)/shard_map/ppermute | solution.py:295
  79.1 1.1 convolution_convert_fusion.1
  80.2 7.3 %all-to-all-done.2 = bf16[16,40,512]{2,1,0:T(8,128)(2,1)S(1)} async-done(((bf16[16,40,512]{2,1,0:T(8,128)(2,1)}), bf16[16,40,512]{2,1,0:T(8,128)(2,1)S(1)}, u32[]{:S(2)}, u32[]{:S(2)}) %all-to-all-start.2) | async-done | bytes 655392 | tf_op jit(solution)/shard_map/all_to_all | solution.py:303
  87.5 4.1 %all-to-all-start = ((bf16[16,40,384]{2,1,0:T(8,128)(2,1)}), bf16[16,40,384]{2,1,0:T(8,128)(2,1)}, u32[]{:S(2)}, u32[]{:S(2)}) async-start(bf16[16,40,384]{2,1,0:T(8,128)(2,1)} %bitcast.7), calls=%async_computation | async-start | bytes 983040 | tf_op jit(solution)/shard_map/all_to_all | solution.py:303
  91.6 11.2 %collective-permute-start.12 = (bf16[2,320,384]{2,1,0:T(8,128)(2,1)S(1)}, bf16[2,320,384]{2,1,0:T(8,128)(2,1)S(1)}, u32[]{:S(2)}, u32[]{:S(2)}) collective-permute-start(bf16[2,320,384]{2,1,0:T(8,128)(2,1)S(1)} %bitcast.89), channel_id=1, source_target_pairs={{0,2},{1,3},{2,0},{3,1},{4,6},{5,7},{6,4},{7,5},{8,10},{9,11},{10,... | collective-permute-start | bytes 1474568 | tf_op jit(solution)/shard_map/ppermute | solution.py:295
  102.9 1.6 fusion.6
  104.4 2.7 collective-permute-start.8
  107.1 1.3 collective-permute-start.9
  109.1 5.3 %collective-permute-done.12.refs_6_ = bf16[2,320,384]{2,1,0:T(8,128)(2,1)S(1)} collective-permute-done((bf16[2,320,384]{2,1,0:T(8,128)(2,1)S(1)}, bf16[2,320,384]{2,1,0:T(8,128)(2,1)S(1)}, u32[]{:S(2)}, u32[]{:S(2)}) %collective-permute-start.12) | collective-permute-done | bytes 491552 | tf_op jit(solution)/shard_map/ppermute | solution.py:295
  114.4 0.8 copy-done.7
  115.2 2.1 collective-permute-start.3
  117.3 7.2 %collective-permute-done.13.refs_7_ = bf16[2,320,384]{2,1,0:T(8,128)(2,1)} collective-permute-done((bf16[2,320,384]{2,1,0:T(8,128)(2,1)S(1)}, bf16[2,320,384]{2,1,0:T(8,128)(2,1)}, u32[]{:S(2)}, u32[]{:S(2)}) %collective-permute-start.13) | collective-permute-done | bytes 491552 | tf_op jit(solution)/shard_map/ppermute | solution.py:295
  124.5 2.3 collective-permute-start.4
  126.8 12.4 %collective-permute-done.10.refs_3_ = bf16[2,320,512]{2,1,0:T(8,128)(2,1)} collective-permute-done((bf16[2,320,512]{2,1,0:T(8,128)(2,1)}, bf16[2,320,512]{2,1,0:T(8,128)(2,1)}, u32[]{:S(2)}, u32[]{:S(2)}) %collective-permute-start.10) | collective-permute-done | bytes 655392 | tf_op jit(solution)/shard_map/ppermute | solution.py:295
  139.3 1.6 collective-permute-start.5
  140.8 1.7 fusion.9
  142.6 1.2 collective-permute-start
  143.8 9.6 %collective-permute-done.9.refs_2_ = bf16[2,320,512]{2,1,0:T(8,128)(2,1)} collective-permute-done((bf16[2,320,512]{2,1,0:T(8,128)(2,1)}, bf16[2,320,512]{2,1,0:T(8,128)(2,1)}, u32[]{:S(2)}, u32[]{:S(2)}) %collective-permute-start.9) | collective-permute-done | bytes 655392 | tf_op jit(solution)/shard_map/ppermute | solution.py:295
  153.3 3.0 collective-permute-start.1
  156.3 6.3 %shard_map.103 = bf16[4,320,256]{2,1,0:T(8,128)(2,1)} custom-call(s32[1]{0:T(128)} %bitcast.3.at_ref, bf16[256,1792]{1,0:T(8,128)(2,1)} %bitcast.97, bf16[2,320,512]{2,1,0:T(8,128)(2,1)} %bitcast.20.refs_0_, bf16[2,320,512]{2,1,0:T(8,128)(2,1)} %collective-permute-done.8.refs_1_, bf16[2,320,512]{2,1,0:T(8,128)(2,1)} %collective-permute-done.9.refs_2_, ...), custom_call_target="tpu_custom_call" | custom-call | tf_op jit(solution)/shard_map/pallas_call | solution.py:24
  162.8 4.2 %all-to-all-start.4 = ((bf16[4,320,256]{2,1,0:T(8,128)(2,1)}), bf16[4,320,256]{2,1,0:T(8,128)(2,1)}, u32[]{:S(2)}, u32[]{:S(2)}) async-start(bf16[4,320,256]{2,1,0:T(8,128)(2,1)} %shard_map.103), calls=%async_computation.4 | async-start | bytes 1310720 | tf_op jit(solution)/shard_map/all_to_all | solution.py:356
  167.1 14.2 %collective-permute-done.5.refs_3_ = bf16[2,320,512]{2,1,0:T(8,128)(2,1)S(1)} collective-permute-done((bf16[2,320,512]{2,1,0:T(8,128)(2,1)S(1)}, bf16[2,320,512]{2,1,0:T(8,128)(2,1)S(1)}, u32[]{:S(2)}, u32[]{:S(2)}) %collective-permute-start.5) | collective-permute-done | bytes 655392 | tf_op jit(solution)/shard_map/ppermute | solution.py:295
  181.3 0.8 copy-done.3
  182.1 4.3 %shard_map.102.refs_4_ = f32[320,512]{1,0:T(8,128)} custom-call(s32[1]{0:T(128)} %bitcast.3.at_ref, bf16[4,1792,512]{2,1,0:T(8,128)(2,1)} %bitcast.68, bf16[2,320,512]{2,1,0:T(8,128)(2,1)} %bitcast.77, bf16[2,320,512]{2,1,0:T(8,128)(2,1)} %copy-done.1, bf16[2,320,512]{2,1,0:T(8,128)(2,1)} %copy-done.2, bf16[2,320,512]{2,1,0:T(8,128)(2,1)} %copy-done.3), custom_call_target="tpu_custom_call" | custom-call | tf_op jit(solution)/shard_map/pallas_call | solution.py:24
  186.5 5.3 %collective-permute-done.1.refs_2_.refs_6_ = bf16[2,320,384]{2,1,0:T(8,128)(2,1)} collective-permute-done((bf16[2,320,384]{2,1,0:T(8,128)(2,1)S(1)}, bf16[2,320,384]{2,1,0:T(8,128)(2,1)}, u32[]{:S(2)}, u32[]{:S(2)}) %collective-permute-start.1) | collective-permute-done | bytes 491552 | tf_op jit(solution)/shard_map/ppermute | solution.py:295
  191.8 9.9 %collective-permute-done.2.refs_3_.refs_7_ = bf16[2,320,384]{2,1,0:T(8,128)(2,1)} collective-permute-done((bf16[2,320,384]{2,1,0:T(8,128)(2,1)S(1)}, bf16[2,320,384]{2,1,0:T(8,128)(2,1)}, u32[]{:S(2)}, u32[]{:S(2)}) %collective-permute-start.2) | collective-permute-done | bytes 491552 | tf_op jit(solution)/shard_map/ppermute | solution.py:295
  201.7 5.7 %shard_map.104 = (bf16[320,256]{1,0:T(8,128)(2,1)}, bf16[320,512]{1,0:T(8,128)(2,1)}) custom-call(s32[1]{0:T(128)} %bitcast.3.at_ref, bf16[4,1792,512]{2,1,0:T(8,128)(2,1)} %bitcast.69, bf16[2,320,384]{2,1,0:T(8,128)(2,1)} %bitcast.83, bf16[2,320,384]{2,1,0:T(8,128)(2,1)} %collective-permute-done.refs_1_.refs_5_, ...), custom_call_target="tpu_custom_call" | custom-call | tf_op jit(solution)/shard_map/pallas_call | solution.py:24
  207.4 5.9 %shard_map.110 = bf16[4,1792,256]{2,1,0:T(8,128)(2,1)} custom-call(s32[1]{0:T(128)} %bitcast.3.at_ref, bf16[320,512]{1,0:T(8,128)(2,1)} %get-tuple-element.13.a_ref, bf16[2,320,512]{2,1,0:T(8,128)(2,1)} %bitcast.78, bf16[2,320,512]{2,1,0:T(8,128)(2,1)} %copy-done.1, bf16[2,320,512]{2,1,0:T(8,128)(2,1)} %copy-done.2, bf16[2,320,512]{2,1,0:T(8,128)(2,1)} %copy-done.3, ...), custom_call_target="tpu_custom_call" | custom-call | tf_op jit(solution)/shard_map/pallas_call | solution.py:24
  213.4 5.9 %shard_map.109 = bf16[4,1792,256]{2,1,0:T(8,128)(2,1)} custom-call(s32[1]{0:T(128)} %bitcast.3.at_ref, bf16[320,512]{1,0:T(8,128)(2,1)} %get-tuple-element.13.a_ref, bf16[2,320,512]{2,1,0:T(8,128)(2,1)} %bitcast.79, bf16[2,320,512]{2,1,0:T(8,128)(2,1)} %copy-done.1, bf16[2,320,512]{2,1,0:T(8,128)(2,1)} %copy-done.2, bf16[2,320,512]{2,1,0:T(8,128)(2,1)} %copy-done.3, ...), custom_call_target="tpu_custom_call" | custom-call | tf_op jit(solution)/shard_map/pallas_call | solution.py:24
  219.3 3.9 %shard_map.107 = (bf16[2,320,384]{2,1,0:T(8,128)(2,1)}, bf16[2,320,384]{2,1,0:T(8,128)(2,1)}, bf16[2,320,384]{2,1,0:T(8,128)(2,1)}) custom-call(s32[1]{0:T(128)} %bitcast.3.at_ref, bf16[320,512]{1,0:T(8,128)(2,1)} %get-tuple-element.13.a_ref, bf16[4,1792,512]{2,1,0:T(8,128)(2,1)} %bitcast.70), custom_call_target="tpu_custom_call" | custom-call | tf_op jit(solution)/shard_map/pallas_call | solution.py:24
  223.2 1.7 collective-permute-start.17
  224.9 1.8 collective-permute-start.18
  226.7 2.0 collective-permute-start.19
  228.7 1.1 fusion.4.order_ref
  229.9 7.3 %collective-permute-done.17.refs_0_ = bf16[2,320,384]{2,1,0:T(8,128)(2,1)S(1)} collective-permute-done((bf16[2,320,384]{2,1,0:T(8,128)(2,1)}, bf16[2,320,384]{2,1,0:T(8,128)(2,1)S(1)}, u32[]{:S(2)}, u32[]{:S(2)}) %collective-permute-start.17) | collective-permute-done | bytes 491552 | tf_op jit(solution)/shard_map/ppermute | solution.py:295
  237.1 11.5 %collective-permute-done.18.refs_1_ = bf16[2,320,384]{2,1,0:T(8,128)(2,1)S(1)} collective-permute-done((bf16[2,320,384]{2,1,0:T(8,128)(2,1)}, bf16[2,320,384]{2,1,0:T(8,128)(2,1)S(1)}, u32[]{:S(2)}, u32[]{:S(2)}) %collective-permute-start.18) | collective-permute-done | bytes 491552 | tf_op jit(solution)/shard_map/ppermute | solution.py:295
  249.4 0.8 copy-done.13
  250.2 4.4 %shard_map.108 = bf16[640,384]{1,0:T(8,128)(2,1)} custom-call(s32[1]{0:T(128)} %bitcast.3.at_ref, bf16[320,512]{1,0:T(8,128)(2,1)} %get-tuple-element.13.a_ref, bf16[4,1792,512]{2,1,0:T(8,128)(2,1)} %bitcast.71, bf16[640,640]{1,0:T(8,128)(2,1)} %fusion.4.order_ref, bf16[2,320,384]{2,1,0:T(8,128)(2,1)} %copy-done.11, bf16[2,320,384]{2,1,0:T(8,128)(2,1)} %copy-done.12, ...), custom_call_target="tpu_custom_call" | custom-call | tf_op jit(solution)/shard_map/pallas_call | solution.py:24
  254.5 7.0 %all-to-all-start.6 = ((bf16[16,40,384]{2,1,0:T(8,128)(2,1)}), bf16[16,40,384]{2,1,0:T(8,128)(2,1)S(1)}, u32[]{:S(2)}, u32[]{:S(2)}) async-start(bf16[16,40,384]{2,1,0:T(8,128)(2,1)} %bitcast.93), calls=%async_computation.6 | async-start | bytes 983040 | tf_op jit(solution)/shard_map/all_to_all | solution.py:303
  261.6 4.2 %shard_map.105 = (bf16[2,320,512]{2,1,0:T(8,128)(2,1)}, bf16[2,320,512]{2,1,0:T(8,128)(2,1)}, bf16[2,320,512]{2,1,0:T(8,128)(2,1)}) custom-call(s32[1]{0:T(128)} %bitcast.3.at_ref, bf16[320,512]{1,0:T(8,128)(2,1)} %get-tuple-element.13.a_ref, bf16[4,1792,512]{2,1,0:T(8,128)(2,1)} %bitcast.72), custom_call_target="tpu_custom_call" | custom-call | tf_op jit(solution)/shard_map/pallas_call | solution.py:24
  265.8 1.1 collective-permute-start.14
  266.9 2.1 collective-permute-start.15
  269.0 1.5 collective-permute-start.16
  270.5 13.1 %collective-permute-done.14.refs_0_ = bf16[2,320,512]{2,1,0:T(8,128)(2,1)S(1)} collective-permute-done((bf16[2,320,512]{2,1,0:T(8,128)(2,1)}, bf16[2,320,512]{2,1,0:T(8,128)(2,1)S(1)}, u32[]{:S(2)}, u32[]{:S(2)}) %collective-permute-start.14) | collective-permute-done | bytes 655392 | tf_op jit(solution)/shard_map/ppermute | solution.py:295
  283.6 14.4 %collective-permute-done.15.refs_1_ = bf16[2,320,512]{2,1,0:T(8,128)(2,1)S(1)} collective-permute-done((bf16[2,320,512]{2,1,0:T(8,128)(2,1)}, bf16[2,320,512]{2,1,0:T(8,128)(2,1)S(1)}, u32[]{:S(2)}, u32[]{:S(2)}) %collective-permute-start.15) | collective-permute-done | bytes 655392 | tf_op jit(solution)/shard_map/ppermute | solution.py:295
  298.0 0.8 copy-done.9
  298.8 0.8 copy-done.10
  299.7 4.9 %shard_map.106 = bf16[640,512]{1,0:T(8,128)(2,1)} custom-call(s32[1]{0:T(128)} %bitcast.3.at_ref, bf16[320,512]{1,0:T(8,128)(2,1)} %get-tuple-element.13.a_ref, bf16[4,1792,512]{2,1,0:T(8,128)(2,1)} %bitcast.73, bf16[640,640]{1,0:T(8,128)(2,1)} %fusion.4.order_ref, bf16[2,320,512]{2,1,0:T(8,128)(2,1)} %copy-done.8, bf16[2,320,512]{2,1,0:T(8,128)(2,1)} %copy-done.9, ...), custom_call_target="tpu_custom_call" | custom-call | tf_op jit(solution)/shard_map/pallas_call | solution.py:24
  304.6 7.8 %all-to-all-start.5 = ((bf16[16,40,512]{2,1,0:T(8,128)(2,1)}), bf16[16,40,512]{2,1,0:T(8,128)(2,1)S(1)}, u32[]{:S(2)}, u32[]{:S(2)}) async-start(bf16[16,40,512]{2,1,0:T(8,128)(2,1)} %bitcast.86), calls=%async_computation.5 | async-start | bytes 1310720 | tf_op jit(solution)/shard_map/all_to_all | solution.py:303
  312.4 12.3 %all-gather.1 = bf16[1280,256]{1,0:T(8,128)(2,1)} all-gather(bf16[320,256]{1,0:T(8,128)(2,1)S(1)} %copy-done.15), channel_id=3, replica_groups=mesh['dp'=4,'expert'=16,'ffn'=4] {'dp'}, dimensions={0}, use_global_device_ids=true | all-gather | bytes 819200 | tf_op jit(solution)/shard_map/all_gather | solution.py:380
  324.7 6.2 %shard_map.111 = f32[256,1792]{1,0:T(8,128)} custom-call(s32[1]{0:T(128)} %bitcast.3.at_ref, bf16[4,320,256]{2,1,0:T(8,128)(2,1)} %bitcast.87, bf16[2,320,512]{2,1,0:T(8,128)(2,1)} %bitcast.20.refs_0_, bf16[2,320,512]{2,1,0:T(8,128)(2,1)} %collective-permute-done.8.refs_1_, bf16[2,320,512]{2,1,0:T(8,128)(2,1)} %collective-permute-done.9.refs_2_, ...), custom_call_target="tpu_custom_call" | custom-call | tf_op jit(solution)/shard_map/pallas_call | solution.py:24
  331.3 1.0 all-to-all-done.5
  332.7 0.8 pad_maximum_fusion.1
  333.5 2.5 convert_element_type.103
  336.1 2.5 convert_element_type.102
  (92 shorter events, 7.5 us)
Async XLA Ops:
  7.2 174.1 %all-gather.4.cloned.1.call-start = ((), (), s32[]{:S(2)}) async-start(), calls=%async_computation.11 | async-start | bytes 9175040 | tf_op jit(solution)/shard_map/all_gather | solution.py:318
  10.0 0.7 copy-start.16
  10.0 2.2 copy-start.17
  10.0 2.9 copy-start.18
  10.0 3.8 %copy-start.14 = (bf16[128,1792]{1,0:T(8,128)(2,1)S(1)}, bf16[128,1792]{1,0:T(8,128)(2,1)}, u32[]{:S(2)}) copy-start(bf16[128,1792]{1,0:T(8,128)(2,1)} %param.7) | copy-start | bytes 1376260
  12.3 12.7 %collective-permute-start.6 = (f32[128,4]{0,1:T(4,128)S(1)}, f32[128,4]{0,1:T(4,128)S(1)}, u32[]{:S(2)}, u32[]{:S(2)}) collective-permute-start(f32[128,4]{0,1:T(4,128)S(1)} %pad_maximum_fusion.6), channel_id=1, source_target_pairs={{0,0},{1,64},{2,128},{3,192},{64,1},{65,65},{66,129},{67,193},{128... | collective-permute-start | bytes 6152 | tf_op jit(solution)/shard_map/ppermute | solution.py:298
  13.0 12.4 %collective-permute-start.7 = (bf16[128,1792]{1,0:T(8,128)(2,1)S(1)}, bf16[128,1792]{1,0:T(8,128)(2,1)S(1)}, u32[]{:S(2)}, u32[]{:S(2)}) collective-permute-start(bf16[128,1792]{1,0:T(8,128)(2,1)S(1)} %copy-done.18), channel_id=1, source_target_pairs={{0,0},{1,64},{2,128},{3,192},{64,1},{65,65},{66,129},{67,193},{128... | collective-permute-start | bytes 1376264 | tf_op jit(solution)/shard_map/ppermute | solution.py:298
  15.0 29.9 %all-to-all-start.1 = ((bf16[16,40,512]{2,1,0:T(8,128)(2,1)}), bf16[16,40,512]{2,1,0:T(8,128)(2,1)S(1)}, u32[]{:S(2)}, u32[]{:S(2)}) async-start(bf16[16,40,512]{2,1,0:T(8,128)(2,1)} %bitcast.10), calls=%async_computation.1 | async-start | bytes 1310720 | tf_op jit(solution)/shard_map/all_to_all | solution.py:303
  44.9 19.5 %all-to-all-start.3 = ((bf16[16,40,384]{2,1,0:T(8,128)(2,1)}), bf16[16,40,384]{2,1,0:T(8,128)(2,1)S(1)}, u32[]{:S(2)}, u32[]{:S(2)}) async-start(bf16[16,40,384]{2,1,0:T(8,128)(2,1)} %bitcast.21), calls=%async_computation.3 | async-start | bytes 983040 | tf_op jit(solution)/shard_map/all_to_all | solution.py:303
  64.5 23.0 %all-to-all-start.2 = ((bf16[16,40,512]{2,1,0:T(8,128)(2,1)}), bf16[16,40,512]{2,1,0:T(8,128)(2,1)S(1)}, u32[]{:S(2)}, u32[]{:S(2)}) async-start(bf16[16,40,512]{2,1,0:T(8,128)(2,1)} %bitcast.18), calls=%async_computation.2 | async-start | bytes 1310720 | tf_op jit(solution)/shard_map/all_to_all | solution.py:303
  68.7 35.7 %copy-start.5 = (bf16[640,384]{1,0:T(8,128)(2,1)}, bf16[640,384]{1,0:T(8,128)(2,1)S(1)}, u32[]{:S(2)}) copy-start(bf16[640,384]{1,0:T(8,128)(2,1)S(1)} %fusion.10) | copy-start | bytes 1474564
  68.7 38.4 %collective-permute-start.11 = (bf16[2,320,384]{2,1,0:T(8,128)(2,1)S(1)}, bf16[2,320,384]{2,1,0:T(8,128)(2,1)S(1)}, u32[]{:S(2)}, u32[]{:S(2)}) collective-permute-start(bf16[2,320,384]{2,1,0:T(8,128)(2,1)S(1)} %bitcast.88), channel_id=1, source_target_pairs={{0,3},{1,0},{2,1},{3,2},{4,7},{5,4},{6,5},{7,6},{8,11},{9,8},{10,9... | collective-permute-start | bytes 1474568 | tf_op jit(solution)/shard_map/ppermute | solution.py:295
  87.5 53.3 %all-to-all-start = ((bf16[16,40,384]{2,1,0:T(8,128)(2,1)}), bf16[16,40,384]{2,1,0:T(8,128)(2,1)}, u32[]{:S(2)}, u32[]{:S(2)}) async-start(bf16[16,40,384]{2,1,0:T(8,128)(2,1)} %bitcast.7), calls=%async_computation | async-start | bytes 983040 | tf_op jit(solution)/shard_map/all_to_all | solution.py:303
  91.6 22.8 %collective-permute-start.12 = (bf16[2,320,384]{2,1,0:T(8,128)(2,1)S(1)}, bf16[2,320,384]{2,1,0:T(8,128)(2,1)S(1)}, u32[]{:S(2)}, u32[]{:S(2)}) collective-permute-start(bf16[2,320,384]{2,1,0:T(8,128)(2,1)S(1)} %bitcast.89), channel_id=1, source_target_pairs={{0,2},{1,3},{2,0},{3,1},{4,6},{5,7},{6,4},{7,5},{8,10},{9,11},{10,... | collective-permute-start | bytes 1474568 | tf_op jit(solution)/shard_map/ppermute | solution.py:295
  102.9 21.6 %collective-permute-start.13 = (bf16[2,320,384]{2,1,0:T(8,128)(2,1)S(1)}, bf16[2,320,384]{2,1,0:T(8,128)(2,1)}, u32[]{:S(2)}, u32[]{:S(2)}) collective-permute-start(bf16[2,320,384]{2,1,0:T(8,128)(2,1)S(1)} %bitcast.90), channel_id=1, source_target_pairs={{0,1},{1,2},{2,3},{3,0},{4,5},{5,6},{6,7},{7,4},{8,9},{9,10},{10,1... | collective-permute-start | bytes 1474568 | tf_op jit(solution)/shard_map/ppermute | solution.py:295
  104.4 34.8 %collective-permute-start.10 = (bf16[2,320,512]{2,1,0:T(8,128)(2,1)}, bf16[2,320,512]{2,1,0:T(8,128)(2,1)}, u32[]{:S(2)}, u32[]{:S(2)}) collective-permute-start(bf16[2,320,512]{2,1,0:T(8,128)(2,1)} %bitcast.20.refs_0_), channel_id=1, source_target_pairs={{0,1},{1,2},{2,3},{3,0},{4,5},{5,6},{6,7},{7,4},{8,9},{9,10},{10,1... | collective-permute-start | bytes 1966088 | tf_op jit(solution)/shard_map/ppermute | solution.py:295
  104.4 38.1 %collective-permute-start.8 = (bf16[2,320,512]{2,1,0:T(8,128)(2,1)}, bf16[2,320,512]{2,1,0:T(8,128)(2,1)}, u32[]{:S(2)}, u32[]{:S(2)}) collective-permute-start(bf16[2,320,512]{2,1,0:T(8,128)(2,1)} %bitcast.20.refs_0_), channel_id=1, source_target_pairs={{0,3},{1,0},{2,1},{3,2},{4,7},{5,4},{6,5},{7,6},{8,11},{9,8},{10,9... | collective-permute-start | bytes 1966088 | tf_op jit(solution)/shard_map/ppermute | solution.py:295
  107.1 1.3 copy-start.6
  107.1 46.2 %collective-permute-start.9 = (bf16[2,320,512]{2,1,0:T(8,128)(2,1)}, bf16[2,320,512]{2,1,0:T(8,128)(2,1)}, u32[]{:S(2)}, u32[]{:S(2)}) collective-permute-start(bf16[2,320,512]{2,1,0:T(8,128)(2,1)} %bitcast.20.refs_0_), channel_id=1, source_target_pairs={{0,2},{1,3},{2,0},{3,1},{4,6},{5,7},{6,4},{7,5},{8,10},{9,11},{10,... | collective-permute-start | bytes 1966088 | tf_op jit(solution)/shard_map/ppermute | solution.py:295
  109.1 53.5 %copy-start = (bf16[640,512]{1,0:T(8,128)(2,1)}, bf16[640,512]{1,0:T(8,128)(2,1)S(1)}, u32[]{:S(2)}) copy-start(bf16[640,512]{1,0:T(8,128)(2,1)S(1)} %fusion.5) | copy-start | bytes 1966084
  114.4 0.8 copy-start.7
  115.2 47.5 %collective-permute-start.3 = (bf16[2,320,512]{2,1,0:T(8,128)(2,1)S(1)}, bf16[2,320,512]{2,1,0:T(8,128)(2,1)S(1)}, u32[]{:S(2)}, u32[]{:S(2)}) collective-permute-start(bf16[2,320,512]{2,1,0:T(8,128)(2,1)S(1)} %bitcast.74), channel_id=1, source_target_pairs={{0,3},{1,0},{2,1},{3,2},{4,7},{5,4},{6,5},{7,6},{8,11},{9,8},{10,9... | collective-permute-start | bytes 1966088 | tf_op jit(solution)/shard_map/ppermute | solution.py:295
  124.5 42.6 %collective-permute-start.4 = (bf16[2,320,512]{2,1,0:T(8,128)(2,1)S(1)}, bf16[2,320,512]{2,1,0:T(8,128)(2,1)S(1)}, u32[]{:S(2)}, u32[]{:S(2)}) collective-permute-start(bf16[2,320,512]{2,1,0:T(8,128)(2,1)S(1)} %bitcast.75), channel_id=1, source_target_pairs={{0,2},{1,3},{2,0},{3,1},{4,6},{5,7},{6,4},{7,5},{8,10},{9,11},{10,... | collective-permute-start | bytes 1966088 | tf_op jit(solution)/shard_map/ppermute | solution.py:295
  139.3 42.0 %collective-permute-start.5 = (bf16[2,320,512]{2,1,0:T(8,128)(2,1)S(1)}, bf16[2,320,512]{2,1,0:T(8,128)(2,1)S(1)}, u32[]{:S(2)}, u32[]{:S(2)}) collective-permute-start(bf16[2,320,512]{2,1,0:T(8,128)(2,1)S(1)} %bitcast.76), channel_id=1, source_target_pairs={{0,1},{1,2},{2,3},{3,0},{4,5},{5,6},{6,7},{7,4},{8,9},{9,10},{10,1... | collective-permute-start | bytes 1966088 | tf_op jit(solution)/shard_map/ppermute | solution.py:295
  142.5 20.1 %copy-start.4 = (bf16[640,384]{1,0:T(8,128)(2,1)}, bf16[640,384]{1,0:T(8,128)(2,1)S(1)}, u32[]{:S(2)}) copy-start(bf16[640,384]{1,0:T(8,128)(2,1)S(1)} %fusion.9) | copy-start | bytes 1474564
  142.6 43.9 %collective-permute-start = (bf16[2,320,384]{2,1,0:T(8,128)(2,1)S(1)}, bf16[2,320,384]{2,1,0:T(8,128)(2,1)}, u32[]{:S(2)}, u32[]{:S(2)}) collective-permute-start(bf16[2,320,384]{2,1,0:T(8,128)(2,1)S(1)} %bitcast.80), channel_id=1, source_target_pairs={{0,3},{1,0},{2,1},{3,2},{4,7},{5,4},{6,5},{7,6},{8,11},{9,8},{10,9... | collective-permute-start | bytes 1474568 | tf_op jit(solution)/shard_map/ppermute | solution.py:295
  153.3 38.5 %collective-permute-start.1 = (bf16[2,320,384]{2,1,0:T(8,128)(2,1)S(1)}, bf16[2,320,384]{2,1,0:T(8,128)(2,1)}, u32[]{:S(2)}, u32[]{:S(2)}) collective-permute-start(bf16[2,320,384]{2,1,0:T(8,128)(2,1)S(1)} %bitcast.81), channel_id=1, source_target_pairs={{0,2},{1,3},{2,0},{3,1},{4,6},{5,7},{6,4},{7,5},{8,10},{9,11},{10,... | collective-permute-start | bytes 1474568 | tf_op jit(solution)/shard_map/ppermute | solution.py:295
  162.7 18.6 %copy-start.1 = (bf16[2,320,512]{2,1,0:T(8,128)(2,1)}, bf16[2,320,512]{2,1,0:T(8,128)(2,1)S(1)}, u32[]{:S(2)}) copy-start(bf16[2,320,512]{2,1,0:T(8,128)(2,1)S(1)} %collective-permute-done.3.refs_1_) | copy-start | bytes 1966084
  162.7 39.0 %collective-permute-start.2 = (bf16[2,320,384]{2,1,0:T(8,128)(2,1)S(1)}, bf16[2,320,384]{2,1,0:T(8,128)(2,1)}, u32[]{:S(2)}, u32[]{:S(2)}) collective-permute-start(bf16[2,320,384]{2,1,0:T(8,128)(2,1)S(1)} %bitcast.82), channel_id=1, source_target_pairs={{0,1},{1,2},{2,3},{3,0},{4,5},{5,6},{6,7},{7,4},{8,9},{9,10},{10,1... | collective-permute-start | bytes 1474568 | tf_op jit(solution)/shard_map/ppermute | solution.py:295
  162.8 38.9 %all-to-all-start.4 = ((bf16[4,320,256]{2,1,0:T(8,128)(2,1)}), bf16[4,320,256]{2,1,0:T(8,128)(2,1)}, u32[]{:S(2)}, u32[]{:S(2)}) async-start(bf16[4,320,256]{2,1,0:T(8,128)(2,1)} %shard_map.103), calls=%async_computation.4 | async-start | bytes 1310720 | tf_op jit(solution)/shard_map/all_to_all | solution.py:356
  167.0 166.6 %reduce-scatter.5.cloned.1.call-start = ((), (), s32[]{:S(2)}) async-start(), calls=%async_computation.10 | async-start | bytes 4587520 | tf_op jit(solution)/shard_map/reduce_scatter | solution.py:368
  167.1 14.2 %copy-start.2 = (bf16[2,320,512]{2,1,0:T(8,128)(2,1)}, bf16[2,320,512]{2,1,0:T(8,128)(2,1)S(1)}, u32[]{:S(2)}) copy-start(bf16[2,320,512]{2,1,0:T(8,128)(2,1)S(1)} %collective-permute-done.4.refs_2_) | copy-start | bytes 1966084
  181.3 0.8 copy-start.3
  213.3 122.8 %reduce-scatter.3.cloned.1.call-start = ((), (), s32[]{:S(2)}) async-start(), calls=%async_computation.9 | async-start | bytes 4587520 | tf_op jit(solution)/shard_map/reduce_scatter | solution.py:361
  223.2 13.9 %collective-permute-start.17 = (bf16[2,320,384]{2,1,0:T(8,128)(2,1)}, bf16[2,320,384]{2,1,0:T(8,128)(2,1)S(1)}, u32[]{:S(2)}, u32[]{:S(2)}) collective-permute-start(bf16[2,320,384]{2,1,0:T(8,128)(2,1)} %get-tuple-element.17), channel_id=1, source_target_pairs={{0,1},{1,2},{2,3},{3,0},{4,5},{5,6},{6,7},{7,4},{8,9},{9,10},{10,1... | collective-permute-start | bytes 1474568 | tf_op jit(solution)/shard_map/ppermute | solution.py:295
  224.9 23.6 %collective-permute-start.18 = (bf16[2,320,384]{2,1,0:T(8,128)(2,1)}, bf16[2,320,384]{2,1,0:T(8,128)(2,1)S(1)}, u32[]{:S(2)}, u32[]{:S(2)}) collective-permute-start(bf16[2,320,384]{2,1,0:T(8,128)(2,1)} %get-tuple-element.18), channel_id=1, source_target_pairs={{0,2},{1,3},{2,0},{3,1},{4,6},{5,7},{6,4},{7,5},{8,10},{9,11},{10,... | collective-permute-start | bytes 1474568 | tf_op jit(solution)/shard_map/ppermute | solution.py:295
  226.7 21.9 %collective-permute-start.19 = (bf16[2,320,384]{2,1,0:T(8,128)(2,1)}, bf16[2,320,384]{2,1,0:T(8,128)(2,1)S(1)}, u32[]{:S(2)}, u32[]{:S(2)}) collective-permute-start(bf16[2,320,384]{2,1,0:T(8,128)(2,1)} %get-tuple-element.19), channel_id=1, source_target_pairs={{0,3},{1,0},{2,1},{3,2},{4,7},{5,4},{6,5},{7,6},{8,11},{9,8},{10,9... | collective-permute-start | bytes 1474568 | tf_op jit(solution)/shard_map/ppermute | solution.py:295
  237.1 11.5 %copy-start.11 = (bf16[2,320,384]{2,1,0:T(8,128)(2,1)}, bf16[2,320,384]{2,1,0:T(8,128)(2,1)S(1)}, u32[]{:S(2)}) copy-start(bf16[2,320,384]{2,1,0:T(8,128)(2,1)S(1)} %collective-permute-done.17.refs_0_) | copy-start | bytes 1474564
  248.6 0.8 copy-start.12
  249.4 0.8 copy-start.13
  254.5 50.0 %all-to-all-start.6 = ((bf16[16,40,384]{2,1,0:T(8,128)(2,1)}), bf16[16,40,384]{2,1,0:T(8,128)(2,1)S(1)}, u32[]{:S(2)}, u32[]{:S(2)}) async-start(bf16[16,40,384]{2,1,0:T(8,128)(2,1)} %bitcast.93), calls=%async_computation.6 | async-start | bytes 983040 | tf_op jit(solution)/shard_map/all_to_all | solution.py:303
  265.8 17.8 %collective-permute-start.14 = (bf16[2,320,512]{2,1,0:T(8,128)(2,1)}, bf16[2,320,512]{2,1,0:T(8,128)(2,1)S(1)}, u32[]{:S(2)}, u32[]{:S(2)}) collective-permute-start(bf16[2,320,512]{2,1,0:T(8,128)(2,1)} %get-tuple-element.14), channel_id=1, source_target_pairs={{0,1},{1,2},{2,3},{3,0},{4,5},{5,6},{6,7},{7,4},{8,9},{9,10},{10,1... | collective-permute-start | bytes 1966088 | tf_op jit(solution)/shard_map/ppermute | solution.py:295
  266.9 31.1 %collective-permute-start.15 = (bf16[2,320,512]{2,1,0:T(8,128)(2,1)}, bf16[2,320,512]{2,1,0:T(8,128)(2,1)S(1)}, u32[]{:S(2)}, u32[]{:S(2)}) collective-permute-start(bf16[2,320,512]{2,1,0:T(8,128)(2,1)} %get-tuple-element.15), channel_id=1, source_target_pairs={{0,2},{1,3},{2,0},{3,1},{4,6},{5,7},{6,4},{7,5},{8,10},{9,11},{10,... | collective-permute-start | bytes 1966088 | tf_op jit(solution)/shard_map/ppermute | solution.py:295
  269.0 43.3 %copy-start.15 = (bf16[320,256]{1,0:T(8,128)(2,1)S(1)}, bf16[320,256]{1,0:T(8,128)(2,1)}, u32[]{:S(2)}) copy-start(bf16[320,256]{1,0:T(8,128)(2,1)} %get-tuple-element.21) | copy-start | bytes 491524
  269.0 29.0 %collective-permute-start.16 = (bf16[2,320,512]{2,1,0:T(8,128)(2,1)}, bf16[2,320,512]{2,1,0:T(8,128)(2,1)S(1)}, u32[]{:S(2)}, u32[]{:S(2)}) collective-permute-start(bf16[2,320,512]{2,1,0:T(8,128)(2,1)} %get-tuple-element.16), channel_id=1, source_target_pairs={{0,3},{1,0},{2,1},{3,2},{4,7},{5,4},{6,5},{7,6},{8,11},{9,8},{10,9... | collective-permute-start | bytes 1966088 | tf_op jit(solution)/shard_map/ppermute | solution.py:295
  283.6 14.4 %copy-start.8 = (bf16[2,320,512]{2,1,0:T(8,128)(2,1)}, bf16[2,320,512]{2,1,0:T(8,128)(2,1)S(1)}, u32[]{:S(2)}) copy-start(bf16[2,320,512]{2,1,0:T(8,128)(2,1)S(1)} %collective-permute-done.14.refs_0_) | copy-start | bytes 1966084
  298.0 0.8 copy-start.9
  298.8 0.8 copy-start.10
  304.6 27.7 %all-to-all-start.5 = ((bf16[16,40,512]{2,1,0:T(8,128)(2,1)}), bf16[16,40,512]{2,1,0:T(8,128)(2,1)S(1)}, u32[]{:S(2)}, u32[]{:S(2)}) async-start(bf16[16,40,512]{2,1,0:T(8,128)(2,1)} %bitcast.86), calls=%async_computation.5 | async-start | bytes 1310720 | tf_op jit(solution)/shard_map/all_to_all | solution.py:303
Sparse Core Ops, SparseCore 0:
  10.4 89.0 all-gather.3
  213.4 43.6 reduce-scatter.4
  259.7 44.8 reduce-scatter.2
where the time goes:
time: 346 us; the launch traced here: 345 us
  waiting for transfers between devices  152 us (44%)
  starting transfers between devices  87.6 us (25%)
  Pallas kernels  51.7 us (15%)
  between operations  14.2 us (4%)
  blocking collectives  12.3 us (4%)
  other arithmetic  11.1 us (3%)
  matrix products  10 us (3%)
  local copies, waits for them, and re-layouts  6.43 us (2%)
    ppermute x18, waiting for transfers between devices, shift(): return lax.ppermute(x, 'ffn', [(i, (i + by) % N) for i in range(N)])  110 us
    pallas_call x10, Pallas kernels, call(): pl.pallas_call(body, out_shape=outs, in_specs=[SMEM] + [ANY] * (len(args)...  51.7 us
    ppermute x18, starting transfers between devices, shift(): return lax.ppermute(x, 'ffn', [(i, (i + by) % N) for i in range(N)])  46 us
    all_to_all x6, waiting for transfers between devices, exchange(): return lax.all_to_all(x, 'expert', split_axis=0, concat_axis=0, tiled=True)  41.5 us
    all_to_all x6, starting transfers between devices, exchange(): return lax.all_to_all(x, 'expert', split_axis=0, concat_axis=0, tiled=True)  35.9 us
    all_gather x1, blocking collectives, per_device(): hidden_all = lax.all_gather(hidden, 'dp', axis=0, tiled=False)  12.3 us
    dot_general x10, matrix products, dot(): lax.dot_general(a, b, (contract, ((), ())), preferred_element_type=F32)  10 us
  transfers between devices with their start and end apart: 30, of which 16 were waited for; matrix products, arithmetic and copies ran while one was open for 5% of the time, Pallas kernels for 12%

commit v1 on v0

--- a/solution.py
+++ b/solution.py
@@ -287,8 +287,9 @@
     capacity = min(rows, (5 * top * rows + 4 * experts - 1) // (4 * experts))
     slots = experts * capacity
     piece = (width // 4 + 127) // 128 * 128
-    pieces = (piece, width // 2 - piece)
-    starts = (0, 2 * piece)
+    small = width // 2 - piece
+    pieces, starts = (small, piece), (0, 2 * small)
+    z_pieces, z_starts = (piece, small), (0, 2 * piece)
     at = lax.axis_index("ffn").astype(jnp.int32)[None]
 
     def shift(x, by):
@@ -336,15 +337,14 @@
             z_scale = jnp.where(hit[k], routing[:, top + k][None, :], z_scale)
     z_scale = jnp.sum(z_scale, axis=1)[:, None]
 
-    def stacked(x, h):
-        lo, w = starts[h], pieces[h]
+    def stacked(x, lo, w):
         return jnp.concatenate([x[:, lo : lo + w], x[:, lo + w : lo + 2 * w]], axis=0)
 
     def pack_x(h):
-        return dot(x_place, stacked(tokens, h), NN).astype(BF16).reshape(groups, 2 * capacity, -1)
+        return dot(x_place, stacked(tokens, starts[h], pieces[h]), NN).astype(BF16).reshape(groups, 2 * capacity, -1)
 
     def pack_z(h):
-        packed = dot(z_place, stacked(z_local, h), NN) * z_scale
+        packed = dot(z_place, stacked(z_local, z_starts[h], z_pieces[h]), NN) * z_scale
         return packed.astype(BF16).reshape(groups, 2 * capacity, -1)
 
     x_0 = gather_rows(pack_x(0))
@@ -360,7 +360,9 @@
     part_gate = weight_grad((x_0, x_1), acts, at, 0)
     grad_gate = lax.psum_scatter(part_gate, "dp", scatter_dimension=0, tiled=True)
     grad_gate = grad_gate.astype(F32)
-    leads = [input_partials(acts, w_in, at, starts[h], pieces[h]) for h in range(2)]
+    leads = []
+    for h in range(2):
+        leads.append(input_partials(acts, w_in, at, starts[h], pieces[h]))
     received = []
     for h in range(2):
         received.append([shift(leads[h][j - 1], j) for j in range(1, N)])
@@ -368,6 +370,8 @@
     grad_up = lax.psum_scatter(part_up, "dp", scatter_dimension=0, tiled=True).astype(F32)
 
     grad_tokens = []
+    hidden_all = lax.all_gather(hidden, "dp", axis=0, tiled=False)
+    received[1] = lax.optimization_barrier((received[1], hidden_all))[0]
     for h in range(2):
         total = input_totals(acts, w_in, at, starts[h], received[h], order_back)
         back = exchange(total.reshape(groups, 2 * capacity, -1))
@@ -376,8 +380,6 @@
         grad_tokens += [back[:rows], back[rows:]]
     grad_tokens = jnp.concatenate(grad_tokens, axis=1)
 
-    hidden = lax.optimization_barrier((hidden, leads[1][0]))[0]
-    hidden_all = lax.all_gather(hidden, "dp", axis=0, tiled=False)
     grad_down = down_grad((z_0, z_1), hidden_all, at)[None]
     return grad_tokens, grad_gate, grad_up, grad_down
 

time: 346 us -> 376 us (1.087)
  waiting for transfers between devices: 152 us -> 184 us
  starting transfers between devices: 87.6 us -> 82.2 us
    all_to_all x6, waiting for transfers between devices: 41.5 us -> 60.5 us  [exchange(): return lax.all_to_all(x, 'expert', split_axis=0, concat_axis=0, tiled=True)]
    ppermute x18, waiting for transfers between devices: 110 us -> 123 us  [shift(): return lax.ppermute(x, 'ffn', [(i, (i + by) % N) for i in range(N)])]
    ppermute x18, starting transfers between devices: 46 us -> 41.1 us  [shift(): return lax.ppermute(x, 'ffn', [(i, (i + by) % N) for i in range(N)])]
  transfers between devices with their start and end apart: 30 -> 30, of which waited for: 16 -> 13; matrix products, arithmetic and copies ran while one was open for 5% -> 4% of each run, Pallas kernels for 12% -> 11%
where the time goes in v1:
time: 376 us; the launch traced here: 375 us
  waiting for transfers between devices  184 us (49%)
  starting transfers between devices  82.2 us (22%)
  Pallas kernels  52.1 us (14%)
  blocking collectives  15.5 us (4%)
  between operations  14.3 us (4%)
  other arithmetic  11.1 us (3%)
  matrix products  9.11 us (2%)
  local copies, waits for them, and re-layouts  6.84 us (2%)
    ppermute x18, waiting for transfers between devices, shift(): return lax.ppermute(x, 'ffn', [(i, (i + by) % N) for i in range(N)])  123 us
    all_to_all x6, waiting for transfers between devices, exchange(): return lax.all_to_all(x, 'expert', split_axis=0, concat_axis=0, tiled=True)  60.5 us
    pallas_call x10, Pallas kernels, call(): pl.pallas_call(body, out_shape=outs, in_specs=[SMEM] + [ANY] * (len(args)...  52.1 us
    ppermute x18, starting transfers between devices, shift(): return lax.ppermute(x, 'ffn', [(i, (i + by) % N) for i in range(N)])  41.1 us
    all_to_all x6, starting transfers between devices, exchange(): return lax.all_to_all(x, 'expert', split_axis=0, concat_axis=0, tiled=True)  35.4 us
    all_gather x1, blocking collectives, per_device(): hidden_all = lax.all_gather(hidden, 'dp', axis=0, tiled=False)  15.5 us
    dot_general x10, matrix products, dot(): lax.dot_general(a, b, (contract, ((), ())), preferred_element_type=F32)  9.11 us
  transfers between devices with their start and end apart: 30, of which 13 were waited for; matrix products, arithmetic and copies ran while one was open for 4% of the time, Pallas kernels for 11%

profile of v1, /device:TPU:1, one launch (start us, length us, event | category | flops | bytes accessed | tf_op | source)
XLA Modules:
  0.0 375.3 jit_solution(1837435869200539908)
XLA Ops:
  7.2 2.8 pad_maximum_fusion
  10.1 0.6 copy-done.23
  12.3 0.7 collective-permute-start.6
  13.2 1.1 convolution_convert_fusion.1
  14.3 10.0 %all-to-all-start.1 = ((bf16[16,40,384]{2,1,0:T(8,128)(2,1)}), bf16[16,40,384]{2,1,0:T(8,128)(2,1)S(1)}, u32[]{:S(2)}, u32[]{:S(2)}) async-start(bf16[16,40,384]{2,1,0:T(8,128)(2,1)} %bitcast.10), calls=%async_computation.1 | async-start | bytes 983040 | tf_op jit(solution)/shard_map/all_to_all | solution.py:304
  24.3 0.7 collective-permute-start.7
  25.4 1.2 fusion.8
  26.6 14.2 %all-to-all-done.1 = bf16[16,40,384]{2,1,0:T(8,128)(2,1)S(1)} async-done(((bf16[16,40,384]{2,1,0:T(8,128)(2,1)}), bf16[16,40,384]{2,1,0:T(8,128)(2,1)S(1)}, u32[]{:S(2)}, u32[]{:S(2)}) %all-to-all-start.1) | async-done | bytes 491552 | tf_op jit(solution)/shard_map/all_to_all | solution.py:304
  40.8 3.5 all-to-all-start.3
  44.3 1.2 fusion.7
  45.5 14.8 %all-to-all-done.3 = bf16[16,40,384]{2,1,0:T(8,128)(2,1)S(1)} async-done(((bf16[16,40,384]{2,1,0:T(8,128)(2,1)}), bf16[16,40,384]{2,1,0:T(8,128)(2,1)S(1)}, u32[]{:S(2)}, u32[]{:S(2)}) %all-to-all-start.3) | async-done | bytes 491552 | tf_op jit(solution)/shard_map/all_to_all | solution.py:304
  60.3 3.5 all-to-all-start.2
  63.8 1.2 convolution_convert_fusion
  65.0 18.3 %all-to-all-done.2 = bf16[16,40,512]{2,1,0:T(8,128)(2,1)S(1)} async-done(((bf16[16,40,512]{2,1,0:T(8,128)(2,1)}), bf16[16,40,512]{2,1,0:T(8,128)(2,1)S(1)}, u32[]{:S(2)}, u32[]{:S(2)}) %all-to-all-start.2) | async-done | bytes 655392 | tf_op jit(solution)/shard_map/all_to_all | solution.py:304
  83.2 3.5 all-to-all-start
  86.8 0.7 fusion.9
  87.5 14.7 %collective-permute-start.5 = (bf16[2,320,384]{2,1,0:T(8,128)(2,1)S(1)}, bf16[2,320,384]{2,1,0:T(8,128)(2,1)S(1)}, u32[]{:S(2)}, u32[]{:S(2)}) collective-permute-start(bf16[2,320,384]{2,1,0:T(8,128)(2,1)S(1)} %bitcast.80), channel_id=1, source_target_pairs={{0,1},{1,2},{2,3},{3,0},{4,5},{5,6},{6,7},{7,4},{8,9},{9,10},{10,1... | collective-permute-start | bytes 1474568 | tf_op jit(solution)/shard_map/ppermute | solution.py:296
  102.2 0.7 fusion.10
  102.9 7.1 %collective-permute-start.13 = (bf16[2,320,384]{2,1,0:T(8,128)(2,1)S(1)}, bf16[2,320,384]{2,1,0:T(8,128)(2,1)S(1)}, u32[]{:S(2)}, u32[]{:S(2)}) collective-permute-start(bf16[2,320,384]{2,1,0:T(8,128)(2,1)S(1)} %bitcast.88), channel_id=1, source_target_pairs={{0,1},{1,2},{2,3},{3,0},{4,5},{5,6},{6,7},{7,4},{8,9},{9,10},{10,1... | collective-permute-start | bytes 1474568 | tf_op jit(solution)/shard_map/ppermute | solution.py:296
  110.0 1.6 fusion.6
  111.7 2.4 collective-permute-start.10
  114.4 2.1 collective-permute-start.8
  116.5 6.1 %collective-permute-done.5.refs_3_ = bf16[2,320,384]{2,1,0:T(8,128)(2,1)S(1)} collective-permute-done((bf16[2,320,384]{2,1,0:T(8,128)(2,1)S(1)}, bf16[2,320,384]{2,1,0:T(8,128)(2,1)S(1)}, u32[]{:S(2)}, u32[]{:S(2)}) %collective-permute-start.5) | collective-permute-done | bytes 491552 | tf_op jit(solution)/shard_map/ppermute | solution.py:296
  122.5 0.8 copy-done.5
  123.7 9.4 %collective-permute-done.13.refs_7_ = bf16[2,320,384]{2,1,0:T(8,128)(2,1)S(1)} collective-permute-done((bf16[2,320,384]{2,1,0:T(8,128)(2,1)S(1)}, bf16[2,320,384]{2,1,0:T(8,128)(2,1)S(1)}, u32[]{:S(2)}, u32[]{:S(2)}) %collective-permute-start.13) | collective-permute-done | bytes 491552 | tf_op jit(solution)/shard_map/ppermute | solution.py:296
  133.2 1.4 collective-permute-start.11
  134.6 0.7 fusion.5
  135.3 37.5 %collective-permute-done.12.refs_6_ = bf16[2,320,384]{2,1,0:T(8,128)(2,1)S(1)} collective-permute-done((bf16[2,320,384]{2,1,0:T(8,128)(2,1)S(1)}, bf16[2,320,384]{2,1,0:T(8,128)(2,1)S(1)}, u32[]{:S(2)}, u32[]{:S(2)}) %collective-permute-start.12) | collective-permute-done | bytes 491552 | tf_op jit(solution)/shard_map/ppermute | solution.py:296
  172.8 0.8 copy-done.8
  173.6 2.7 collective-permute-start
  176.3 2.3 collective-permute-start.4
  178.6 0.7 collective-permute-start.3
  179.3 6.3 %shard_map.103 = bf16[4,320,256]{2,1,0:T(8,128)(2,1)} custom-call(s32[1]{0:T(128)} %bitcast.3.at_ref, bf16[256,1792]{1,0:T(8,128)(2,1)} %bitcast.97, bf16[2,320,512]{2,1,0:T(8,128)(2,1)} %bitcast.20.refs_0_, bf16[2,320,512]{2,1,0:T(8,128)(2,1)} %collective-permute-done.8.refs_1_, bf16[2,320,512]{2,1,0:T(8,128)(2,1)} %collective-permute-done.9.refs_2_, ...), custom_call_target="tpu_custom_call" | custom-call | tf_op jit(solution)/shard_map/pallas_call | solution.py:24
  185.6 4.2 %all-to-all-start.4 = ((bf16[4,320,256]{2,1,0:T(8,128)(2,1)}), bf16[4,320,256]{2,1,0:T(8,128)(2,1)}, u32[]{:S(2)}, u32[]{:S(2)}) async-start(bf16[4,320,256]{2,1,0:T(8,128)(2,1)} %shard_map.103), calls=%async_computation.4 | async-start | bytes 1310720 | tf_op jit(solution)/shard_map/all_to_all | solution.py:356
  189.9 22.3 %collective-permute-done.4.refs_2_ = bf16[2,320,384]{2,1,0:T(8,128)(2,1)} collective-permute-done((bf16[2,320,384]{2,1,0:T(8,128)(2,1)S(1)}, bf16[2,320,384]{2,1,0:T(8,128)(2,1)}, u32[]{:S(2)}, u32[]{:S(2)}) %collective-permute-start.4) | collective-permute-done | bytes 491552 | tf_op jit(solution)/shard_map/ppermute | solution.py:296
  212.2 14.1 %collective-permute-done.3.refs_1_ = bf16[2,320,384]{2,1,0:T(8,128)(2,1)} collective-permute-done((bf16[2,320,384]{2,1,0:T(8,128)(2,1)S(1)}, bf16[2,320,384]{2,1,0:T(8,128)(2,1)}, u32[]{:S(2)}, u32[]{:S(2)}) %collective-permute-start.3) | collective-permute-done | bytes 491552 | tf_op jit(solution)/shard_map/ppermute | solution.py:296
  226.3 4.2 %shard_map.102.refs_4_ = f32[320,512]{1,0:T(8,128)} custom-call(s32[1]{0:T(128)} %bitcast.3.at_ref, bf16[4,1792,512]{2,1,0:T(8,128)(2,1)} %bitcast.68, bf16[2,320,384]{2,1,0:T(8,128)(2,1)} %bitcast.83, bf16[2,320,384]{2,1,0:T(8,128)(2,1)} %collective-permute-done.3.refs_1_, bf16[2,320,384]{2,1,0:T(8,128)(2,1)} %collective-permute-done.4.refs_2_, ...), custom_call_target="tpu_custom_call" | custom-call | tf_op jit(solution)/shard_map/pallas_call | solution.py:24
  230.5 0.8 copy-done.1
  231.7 6.2 %shard_map.104 = (bf16[320,256]{1,0:T(8,128)(2,1)}, bf16[320,512]{1,0:T(8,128)(2,1)}) custom-call(s32[1]{0:T(128)} %bitcast.3.at_ref, bf16[4,1792,512]{2,1,0:T(8,128)(2,1)} %bitcast.69, bf16[2,320,512]{2,1,0:T(8,128)(2,1)} %bitcast.77, bf16[2,320,512]{2,1,0:T(8,128)(2,1)} %copy-done.3, bf16[2,320,512]{2,1,0:T(8,128)(2,1)} %copy-done.2, ...), custom_call_target="tpu_custom_call" | custom-call | tf_op jit(solution)/shard_map/pallas_call | solution.py:24
  237.9 5.8 %shard_map.110 = bf16[4,1792,256]{2,1,0:T(8,128)(2,1)} custom-call(s32[1]{0:T(128)} %bitcast.3.at_ref, bf16[320,512]{1,0:T(8,128)(2,1)} %get-tuple-element.15.a_ref, bf16[2,320,384]{2,1,0:T(8,128)(2,1)} %bitcast.84, bf16[2,320,384]{2,1,0:T(8,128)(2,1)} %collective-permute-done.3.refs_1_, bf16[2,320,384]{2,1,0:T(8,128)(2,1)} %collective-permute-done.4.refs_2_, ...), custom_call_target="tpu_custom_call" | custom-call | tf_op jit(solution)/shard_map/pallas_call | solution.py:24
  243.8 5.8 %shard_map.109 = bf16[4,1792,256]{2,1,0:T(8,128)(2,1)} custom-call(s32[1]{0:T(128)} %bitcast.3.at_ref, bf16[320,512]{1,0:T(8,128)(2,1)} %get-tuple-element.15.a_ref, bf16[2,320,384]{2,1,0:T(8,128)(2,1)} %bitcast.85, bf16[2,320,384]{2,1,0:T(8,128)(2,1)} %collective-permute-done.3.refs_1_, bf16[2,320,384]{2,1,0:T(8,128)(2,1)} %collective-permute-done.4.refs_2_, ...), custom_call_target="tpu_custom_call" | custom-call | tf_op jit(solution)/shard_map/pallas_call | solution.py:24
  249.7 3.9 %shard_map.105 = (bf16[2,320,384]{2,1,0:T(8,128)(2,1)}, bf16[2,320,384]{2,1,0:T(8,128)(2,1)}, bf16[2,320,384]{2,1,0:T(8,128)(2,1)}) custom-call(s32[1]{0:T(128)} %bitcast.3.at_ref, bf16[320,512]{1,0:T(8,128)(2,1)} %get-tuple-element.15.a_ref, bf16[4,1792,512]{2,1,0:T(8,128)(2,1)} %bitcast.70), custom_call_target="tpu_custom_call" | custom-call | tf_op jit(solution)/shard_map/pallas_call | solution.py:24
  253.6 1.0 collective-permute-start.14
  254.6 3.2 collective-permute-start.15
  257.8 1.1 fusion.4.order_ref
  259.0 8.1 %collective-permute-done.14.refs_0_ = bf16[2,320,384]{2,1,0:T(8,128)(2,1)S(1)} collective-permute-done((bf16[2,320,384]{2,1,0:T(8,128)(2,1)}, bf16[2,320,384]{2,1,0:T(8,128)(2,1)S(1)}, u32[]{:S(2)}, u32[]{:S(2)}) %collective-permute-start.14) | collective-permute-done | bytes 491552 | tf_op jit(solution)/shard_map/ppermute | solution.py:296
  267.0 12.1 %collective-permute-done.15.refs_1_ = bf16[2,320,384]{2,1,0:T(8,128)(2,1)S(1)} collective-permute-done((bf16[2,320,384]{2,1,0:T(8,128)(2,1)}, bf16[2,320,384]{2,1,0:T(8,128)(2,1)S(1)}, u32[]{:S(2)}, u32[]{:S(2)}) %collective-permute-start.15) | collective-permute-done | bytes 491552 | tf_op jit(solution)/shard_map/ppermute | solution.py:296
  279.2 0.8 copy-done.15
  280.0 0.8 copy-done.16
  280.7 4.4 %shard_map.106 = bf16[640,384]{1,0:T(8,128)(2,1)} custom-call(s32[1]{0:T(128)} %bitcast.3.at_ref, bf16[320,512]{1,0:T(8,128)(2,1)} %get-tuple-element.15.a_ref, bf16[4,1792,512]{2,1,0:T(8,128)(2,1)} %bitcast.71, bf16[640,640]{1,0:T(8,128)(2,1)} %fusion.4.order_ref, bf16[2,320,384]{2,1,0:T(8,128)(2,1)} %copy-done.14, bf16[2,320,384]{2,1,0:T(8,128)(2,1)} %copy-done.15, ...), custom_call_target="tpu_custom_call" | custom-call | tf_op jit(solution)/shard_map/pallas_call | solution.py:24
  285.2 7.0 %all-to-all-start.5 = ((bf16[16,40,384]{2,1,0:T(8,128)(2,1)}), bf16[16,40,384]{2,1,0:T(8,128)(2,1)S(1)}, u32[]{:S(2)}, u32[]{:S(2)}) async-start(bf16[16,40,384]{2,1,0:T(8,128)(2,1)} %bitcast.93), calls=%async_computation.5 | async-start | bytes 983040 | tf_op jit(solution)/shard_map/all_to_all | solution.py:304
  292.2 4.3 %shard_map.107 = (bf16[2,320,512]{2,1,0:T(8,128)(2,1)}, bf16[2,320,512]{2,1,0:T(8,128)(2,1)}, bf16[2,320,512]{2,1,0:T(8,128)(2,1)}) custom-call(s32[1]{0:T(128)} %bitcast.3.at_ref, bf16[320,512]{1,0:T(8,128)(2,1)} %get-tuple-element.15.a_ref, bf16[4,1792,512]{2,1,0:T(8,128)(2,1)} %bitcast.72), custom_call_target="tpu_custom_call" | custom-call | tf_op jit(solution)/shard_map/pallas_call | solution.py:24
  296.6 2.4 collective-permute-start.18
  299.3 15.5 %all-gather.1 = bf16[1280,256]{1,0:T(8,128)(2,1)} all-gather(bf16[320,256]{1,0:T(8,128)(2,1)S(1)} %copy-done.22), channel_id=3, replica_groups=mesh['dp'=4,'expert'=16,'ffn'=4] {'dp'}, dimensions={0}, use_global_device_ids=true | all-gather | bytes 819200 | tf_op jit(solution)/shard_map/all_gather | solution.py:373
  314.8 13.2 %collective-permute-done.18.refs_1_ = bf16[2,320,512]{2,1,0:T(8,128)(2,1)S(1)} collective-permute-done((bf16[2,320,512]{2,1,0:T(8,128)(2,1)}, bf16[2,320,512]{2,1,0:T(8,128)(2,1)S(1)}, u32[]{:S(2)}, u32[]{:S(2)}) %collective-permute-start.18) | collective-permute-done | bytes 655392 | tf_op jit(solution)/shard_map/ppermute | solution.py:296
  328.0 0.7 collective-permute-done.19.refs_2_
  328.9 0.7 copy-done.11
  329.6 4.9 %shard_map.108 = bf16[640,512]{1,0:T(8,128)(2,1)} custom-call(s32[1]{0:T(128)} %bitcast.3.at_ref, bf16[320,512]{1,0:T(8,128)(2,1)} %get-tuple-element.15.a_ref, bf16[4,1792,512]{2,1,0:T(8,128)(2,1)} %bitcast.73, bf16[640,640]{1,0:T(8,128)(2,1)} %fusion.4.order_ref, bf16[2,320,512]{2,1,0:T(8,128)(2,1)} %copy-done.9, bf16[2,320,512]{2,1,0:T(8,128)(2,1)} %copy-done.10, ...), custom_call_target="tpu_custom_call" | custom-call | tf_op jit(solution)/shard_map/pallas_call | solution.py:24
  334.5 8.0 %all-to-all-start.6 = ((bf16[16,40,512]{2,1,0:T(8,128)(2,1)}), bf16[16,40,512]{2,1,0:T(8,128)(2,1)S(1)}, u32[]{:S(2)}, u32[]{:S(2)}) async-start(bf16[16,40,512]{2,1,0:T(8,128)(2,1)} %bitcast.86), calls=%async_computation.6 | async-start | bytes 1310720 | tf_op jit(solution)/shard_map/all_to_all | solution.py:304
  342.5 6.2 %shard_map.111 = f32[256,1792]{1,0:T(8,128)} custom-call(s32[1]{0:T(128)} %bitcast.3.at_ref, bf16[4,320,256]{2,1,0:T(8,128)(2,1)} %bitcast.87, bf16[2,320,512]{2,1,0:T(8,128)(2,1)} %bitcast.20.refs_0_, bf16[2,320,512]{2,1,0:T(8,128)(2,1)} %collective-permute-done.8.refs_1_, bf16[2,320,512]{2,1,0:T(8,128)(2,1)} %collective-permute-done.9.refs_2_, ...), custom_call_target="tpu_custom_call" | custom-call | tf_op jit(solution)/shard_map/pallas_call | solution.py:24
  349.2 13.2 %all-to-all-done.6 = bf16[16,40,512]{2,1,0:T(8,128)(2,1)S(1)} async-done(((bf16[16,40,512]{2,1,0:T(8,128)(2,1)}), bf16[16,40,512]{2,1,0:T(8,128)(2,1)S(1)}, u32[]{:S(2)}, u32[]{:S(2)}) %all-to-all-start.6) | async-done | bytes 655392 | tf_op jit(solution)/shard_map/all_to_all | solution.py:304
  362.8 0.8 pad_maximum_fusion.1
  363.6 2.5 convert_element_type.103
  366.2 2.5 convert_element_type.102
  (106 shorter events, 4.9 us)
Async XLA Ops:
  7.2 219.1 %all-gather.4.cloned.1.call-start = ((), (), s32[]{:S(2)}) async-start(), calls=%async_computation.11 | async-start | bytes 9175040 | tf_op jit(solution)/shard_map/all_gather | solution.py:319
  10.0 0.7 copy-start.23
  10.0 2.2 copy-start.24
  10.0 2.9 copy-start.17
  10.8 13.5 %copy-start.25 = (bf16[128,1792]{1,0:T(8,128)(2,1)S(1)}, bf16[128,1792]{1,0:T(8,128)(2,1)}, u32[]{:S(2)}) copy-start(bf16[128,1792]{1,0:T(8,128)(2,1)} %param.8) | copy-start | bytes 1376260
  12.3 12.7 %collective-permute-start.6 = (f32[128,4]{0,1:T(4,128)S(1)}, f32[128,4]{0,1:T(4,128)S(1)}, u32[]{:S(2)}, u32[]{:S(2)}) collective-permute-start(f32[128,4]{0,1:T(4,128)S(1)} %pad_maximum_fusion.6), channel_id=1, source_target_pairs={{0,0},{1,64},{2,128},{3,192},{64,1},{65,65},{66,129},{67,193},{128... | collective-permute-start | bytes 6152 | tf_op jit(solution)/shard_map/ppermute | solution.py:299
  13.2 50.6 %copy-start.18 = (bf16[640,128]{1,0:T(8,128)(2,1)}, bf16[640,128]{1,0:T(8,128)(2,1)S(1)}, u32[]{:S(2)}) copy-start(bf16[640,128]{1,0:T(8,128)(2,1)S(1)} %get-tuple-element.50) | copy-start | bytes 491524
  13.2 50.6 %copy-start.20 = (bf16[640,128]{1,0:T(8,128)(2,1)}, bf16[640,128]{1,0:T(8,128)(2,1)S(1)}, u32[]{:S(2)}) copy-start(bf16[640,128]{1,0:T(8,128)(2,1)S(1)} %get-tuple-element.51) | copy-start | bytes 491524
  14.3 26.5 %all-to-all-start.1 = ((bf16[16,40,384]{2,1,0:T(8,128)(2,1)}), bf16[16,40,384]{2,1,0:T(8,128)(2,1)S(1)}, u32[]{:S(2)}, u32[]{:S(2)}) async-start(bf16[16,40,384]{2,1,0:T(8,128)(2,1)} %bitcast.10), calls=%async_computation.1 | async-start | bytes 983040 | tf_op jit(solution)/shard_map/all_to_all | solution.py:304
  24.3 1.1 collective-permute-start.7
  40.8 19.4 %all-to-all-start.3 = ((bf16[16,40,384]{2,1,0:T(8,128)(2,1)}), bf16[16,40,384]{2,1,0:T(8,128)(2,1)S(1)}, u32[]{:S(2)}, u32[]{:S(2)}) async-start(bf16[16,40,384]{2,1,0:T(8,128)(2,1)} %bitcast.21), calls=%async_computation.3 | async-start | bytes 983040 | tf_op jit(solution)/shard_map/all_to_all | solution.py:304
  60.3 23.0 %all-to-all-start.2 = ((bf16[16,40,512]{2,1,0:T(8,128)(2,1)}), bf16[16,40,512]{2,1,0:T(8,128)(2,1)S(1)}, u32[]{:S(2)}, u32[]{:S(2)}) async-start(bf16[16,40,512]{2,1,0:T(8,128)(2,1)} %bitcast.18), calls=%async_computation.2 | async-start | bytes 1310720 | tf_op jit(solution)/shard_map/all_to_all | solution.py:304
  83.2 3.5 copy-start.12
  83.2 51.3 %all-to-all-start = ((bf16[16,40,512]{2,1,0:T(8,128)(2,1)}), bf16[16,40,512]{2,1,0:T(8,128)(2,1)S(1)}, u32[]{:S(2)}, u32[]{:S(2)}) async-start(bf16[16,40,512]{2,1,0:T(8,128)(2,1)} %bitcast.7), calls=%async_computation | async-start | bytes 1310720 | tf_op jit(solution)/shard_map/all_to_all | solution.py:304
  86.8 23.3 %copy-start.13 = (bf16[16,40,512]{2,1,0:T(8,128)(2,1)S(1)}, bf16[16,40,512]{2,1,0:T(8,128)(2,1)}, u32[]{:S(2)}) copy-start(bf16[16,40,512]{2,1,0:T(8,128)(2,1)} %copy-done.12) | copy-start | bytes 1966084
  87.5 91.2 %copy-start.4 = (bf16[640,384]{1,0:T(8,128)(2,1)}, bf16[640,384]{1,0:T(8,128)(2,1)S(1)}, u32[]{:S(2)}) copy-start(bf16[640,384]{1,0:T(8,128)(2,1)S(1)} %fusion.9) | copy-start | bytes 1474564
  87.5 35.0 %collective-permute-start.5 = (bf16[2,320,384]{2,1,0:T(8,128)(2,1)S(1)}, bf16[2,320,384]{2,1,0:T(8,128)(2,1)S(1)}, u32[]{:S(2)}, u32[]{:S(2)}) collective-permute-start(bf16[2,320,384]{2,1,0:T(8,128)(2,1)S(1)} %bitcast.80), channel_id=1, source_target_pairs={{0,1},{1,2},{2,3},{3,0},{4,5},{5,6},{6,7},{7,4},{8,9},{9,10},{10,1... | collective-permute-start | bytes 1474568 | tf_op jit(solution)/shard_map/ppermute | solution.py:296
  102.9 32.4 %copy-start.6 = (bf16[640,384]{1,0:T(8,128)(2,1)}, bf16[640,384]{1,0:T(8,128)(2,1)S(1)}, u32[]{:S(2)}) copy-start(bf16[640,384]{1,0:T(8,128)(2,1)S(1)} %fusion.10) | copy-start | bytes 1474564
  102.9 30.2 %collective-permute-start.13 = (bf16[2,320,384]{2,1,0:T(8,128)(2,1)S(1)}, bf16[2,320,384]{2,1,0:T(8,128)(2,1)S(1)}, u32[]{:S(2)}, u32[]{:S(2)}) collective-permute-start(bf16[2,320,384]{2,1,0:T(8,128)(2,1)S(1)} %bitcast.88), channel_id=1, source_target_pairs={{0,1},{1,2},{2,3},{3,0},{4,5},{5,6},{6,7},{7,4},{8,9},{9,10},{10,1... | collective-permute-start | bytes 1474568 | tf_op jit(solution)/shard_map/ppermute | solution.py:296
  111.7 61.9 %collective-permute-start.10 = (bf16[2,320,512]{2,1,0:T(8,128)(2,1)}, bf16[2,320,512]{2,1,0:T(8,128)(2,1)}, u32[]{:S(2)}, u32[]{:S(2)}) collective-permute-start(bf16[2,320,512]{2,1,0:T(8,128)(2,1)} %bitcast.20.refs_0_), channel_id=1, source_target_pairs={{0,1},{1,2},{2,3},{3,0},{4,5},{5,6},{6,7},{7,4},{8,9},{9,10},{10,1... | collective-permute-start | bytes 1966088 | tf_op jit(solution)/shard_map/ppermute | solution.py:296
  114.0 62.3 %collective-permute-start.9 = (bf16[2,320,512]{2,1,0:T(8,128)(2,1)}, bf16[2,320,512]{2,1,0:T(8,128)(2,1)}, u32[]{:S(2)}, u32[]{:S(2)}) collective-permute-start(bf16[2,320,512]{2,1,0:T(8,128)(2,1)} %bitcast.20.refs_0_), channel_id=1, source_target_pairs={{0,2},{1,3},{2,0},{3,1},{4,6},{5,7},{6,4},{7,5},{8,10},{9,11},{10,... | collective-permute-start | bytes 1966088 | tf_op jit(solution)/shard_map/ppermute | solution.py:296
  114.4 64.2 %collective-permute-start.8 = (bf16[2,320,512]{2,1,0:T(8,128)(2,1)}, bf16[2,320,512]{2,1,0:T(8,128)(2,1)}, u32[]{:S(2)}, u32[]{:S(2)}) collective-permute-start(bf16[2,320,512]{2,1,0:T(8,128)(2,1)} %bitcast.20.refs_0_), channel_id=1, source_target_pairs={{0,3},{1,0},{2,1},{3,2},{4,7},{5,4},{6,5},{7,6},{8,11},{9,8},{10,9... | collective-permute-start | bytes 1966088 | tf_op jit(solution)/shard_map/ppermute | solution.py:296
  122.5 0.8 copy-start.5
  123.3 49.4 %collective-permute-start.12 = (bf16[2,320,384]{2,1,0:T(8,128)(2,1)S(1)}, bf16[2,320,384]{2,1,0:T(8,128)(2,1)S(1)}, u32[]{:S(2)}, u32[]{:S(2)}) collective-permute-start(bf16[2,320,384]{2,1,0:T(8,128)(2,1)S(1)} %bitcast.89), channel_id=1, source_target_pairs={{0,2},{1,3},{2,0},{3,1},{4,6},{5,7},{6,4},{7,5},{8,10},{9,11},{10,... | collective-permute-start | bytes 1474568 | tf_op jit(solution)/shard_map/ppermute | solution.py:296
  133.2 1.4 copy-start.7
  133.2 40.4 %collective-permute-start.11 = (bf16[2,320,384]{2,1,0:T(8,128)(2,1)S(1)}, bf16[2,320,384]{2,1,0:T(8,128)(2,1)}, u32[]{:S(2)}, u32[]{:S(2)}) collective-permute-start(bf16[2,320,384]{2,1,0:T(8,128)(2,1)S(1)} %bitcast.90), channel_id=1, source_target_pairs={{0,3},{1,0},{2,1},{3,2},{4,7},{5,4},{6,5},{7,6},{8,11},{9,8},{10,9... | collective-permute-start | bytes 1474568 | tf_op jit(solution)/shard_map/ppermute | solution.py:296
  135.3 50.3 %copy-start = (bf16[640,512]{1,0:T(8,128)(2,1)}, bf16[640,512]{1,0:T(8,128)(2,1)S(1)}, u32[]{:S(2)}) copy-start(bf16[640,512]{1,0:T(8,128)(2,1)S(1)} %fusion.5) | copy-start | bytes 1966084
  172.8 0.8 copy-start.8
  173.6 56.9 %collective-permute-start.2 = (bf16[2,320,512]{2,1,0:T(8,128)(2,1)S(1)}, bf16[2,320,512]{2,1,0:T(8,128)(2,1)S(1)}, u32[]{:S(2)}, u32[]{:S(2)}) collective-permute-start(bf16[2,320,512]{2,1,0:T(8,128)(2,1)S(1)} %bitcast.74), channel_id=1, source_target_pairs={{0,1},{1,2},{2,3},{3,0},{4,5},{5,6},{6,7},{7,4},{8,9},{9,10},{10,1... | collective-permute-start | bytes 1966088 | tf_op jit(solution)/shard_map/ppermute | solution.py:296
  173.6 56.9 %collective-permute-start.1 = (bf16[2,320,512]{2,1,0:T(8,128)(2,1)S(1)}, bf16[2,320,512]{2,1,0:T(8,128)(2,1)S(1)}, u32[]{:S(2)}, u32[]{:S(2)}) collective-permute-start(bf16[2,320,512]{2,1,0:T(8,128)(2,1)S(1)} %bitcast.75), channel_id=1, source_target_pairs={{0,2},{1,3},{2,0},{3,1},{4,6},{5,7},{6,4},{7,5},{8,10},{9,11},{10,... | collective-permute-start | bytes 1966088 | tf_op jit(solution)/shard_map/ppermute | solution.py:296
  173.6 56.9 %collective-permute-start = (bf16[2,320,512]{2,1,0:T(8,128)(2,1)S(1)}, bf16[2,320,512]{2,1,0:T(8,128)(2,1)S(1)}, u32[]{:S(2)}, u32[]{:S(2)}) collective-permute-start(bf16[2,320,512]{2,1,0:T(8,128)(2,1)S(1)} %bitcast.76), channel_id=1, source_target_pairs={{0,3},{1,0},{2,1},{3,2},{4,7},{5,4},{6,5},{7,6},{8,11},{9,8},{10,9... | collective-permute-start | bytes 1966088 | tf_op jit(solution)/shard_map/ppermute | solution.py:296
  176.3 35.9 %collective-permute-start.4 = (bf16[2,320,384]{2,1,0:T(8,128)(2,1)S(1)}, bf16[2,320,384]{2,1,0:T(8,128)(2,1)}, u32[]{:S(2)}, u32[]{:S(2)}) collective-permute-start(bf16[2,320,384]{2,1,0:T(8,128)(2,1)S(1)} %bitcast.81), channel_id=1, source_target_pairs={{0,2},{1,3},{2,0},{3,1},{4,6},{5,7},{6,4},{7,5},{8,10},{9,11},{10,... | collective-permute-start | bytes 1474568 | tf_op jit(solution)/shard_map/ppermute | solution.py:296
  178.6 47.6 %collective-permute-start.3 = (bf16[2,320,384]{2,1,0:T(8,128)(2,1)S(1)}, bf16[2,320,384]{2,1,0:T(8,128)(2,1)}, u32[]{:S(2)}, u32[]{:S(2)}) collective-permute-start(bf16[2,320,384]{2,1,0:T(8,128)(2,1)S(1)} %bitcast.82), channel_id=1, source_target_pairs={{0,3},{1,0},{2,1},{3,2},{4,7},{5,4},{6,5},{7,6},{8,11},{9,8},{10,9... | collective-permute-start | bytes 1474568 | tf_op jit(solution)/shard_map/ppermute | solution.py:296
  185.6 44.9 %all-to-all-start.4 = ((bf16[4,320,256]{2,1,0:T(8,128)(2,1)}), bf16[4,320,256]{2,1,0:T(8,128)(2,1)}, u32[]{:S(2)}, u32[]{:S(2)}) async-start(bf16[4,320,256]{2,1,0:T(8,128)(2,1)} %shard_map.103), calls=%async_computation.4 | async-start | bytes 1310720 | tf_op jit(solution)/shard_map/all_to_all | solution.py:356
  189.8 173.8 %reduce-scatter.5.cloned.1.call-start = ((), (), s32[]{:S(2)}) async-start(), calls=%async_computation.10 | async-start | bytes 4587520 | tf_op jit(solution)/shard_map/reduce_scatter | solution.py:370
  230.5 0.8 copy-start.1
  230.5 1.0 copy-start.2
  230.5 1.2 copy-start.3
  243.8 122.4 %reduce-scatter.3.cloned.1.call-start = ((), (), s32[]{:S(2)}) async-start(), calls=%async_computation.9 | async-start | bytes 4587520 | tf_op jit(solution)/shard_map/reduce_scatter | solution.py:361
  253.6 13.5 %collective-permute-start.14 = (bf16[2,320,384]{2,1,0:T(8,128)(2,1)}, bf16[2,320,384]{2,1,0:T(8,128)(2,1)S(1)}, u32[]{:S(2)}, u32[]{:S(2)}) collective-permute-start(bf16[2,320,384]{2,1,0:T(8,128)(2,1)} %get-tuple-element.16), channel_id=1, source_target_pairs={{0,1},{1,2},{2,3},{3,0},{4,5},{5,6},{6,7},{7,4},{8,9},{9,10},{10,1... | collective-permute-start | bytes 1474568 | tf_op jit(solution)/shard_map/ppermute | solution.py:296
  254.6 24.6 %collective-permute-start.15 = (bf16[2,320,384]{2,1,0:T(8,128)(2,1)}, bf16[2,320,384]{2,1,0:T(8,128)(2,1)S(1)}, u32[]{:S(2)}, u32[]{:S(2)}) collective-permute-start(bf16[2,320,384]{2,1,0:T(8,128)(2,1)} %get-tuple-element.17), channel_id=1, source_target_pairs={{0,2},{1,3},{2,0},{3,1},{4,6},{5,7},{6,4},{7,5},{8,10},{9,11},{10,... | collective-permute-start | bytes 1474568 | tf_op jit(solution)/shard_map/ppermute | solution.py:296
  257.8 21.4 %collective-permute-start.16 = (bf16[2,320,384]{2,1,0:T(8,128)(2,1)}, bf16[2,320,384]{2,1,0:T(8,128)(2,1)S(1)}, u32[]{:S(2)}, u32[]{:S(2)}) collective-permute-start(bf16[2,320,384]{2,1,0:T(8,128)(2,1)} %get-tuple-element.18), channel_id=1, source_target_pairs={{0,3},{1,0},{2,1},{3,2},{4,7},{5,4},{6,5},{7,6},{8,11},{9,8},{10,9... | collective-permute-start | bytes 1474568 | tf_op jit(solution)/shard_map/ppermute | solution.py:296
  267.0 12.2 %copy-start.14 = (bf16[2,320,384]{2,1,0:T(8,128)(2,1)}, bf16[2,320,384]{2,1,0:T(8,128)(2,1)S(1)}, u32[]{:S(2)}) copy-start(bf16[2,320,384]{2,1,0:T(8,128)(2,1)S(1)} %collective-permute-done.14.refs_0_) | copy-start | bytes 1474564
  279.2 0.8 copy-start.15
  280.0 0.8 copy-start.16
  285.2 49.3 %all-to-all-start.5 = ((bf16[16,40,384]{2,1,0:T(8,128)(2,1)}), bf16[16,40,384]{2,1,0:T(8,128)(2,1)S(1)}, u32[]{:S(2)}, u32[]{:S(2)}) async-start(bf16[16,40,384]{2,1,0:T(8,128)(2,1)} %bitcast.93), calls=%async_computation.5 | async-start | bytes 983040 | tf_op jit(solution)/shard_map/all_to_all | solution.py:304
  292.2 7.1 %copy-start.22 = (bf16[320,256]{1,0:T(8,128)(2,1)S(1)}, bf16[320,256]{1,0:T(8,128)(2,1)}, u32[]{:S(2)}) copy-start(bf16[320,256]{1,0:T(8,128)(2,1)} %get-tuple-element.22) | copy-start | bytes 491524
  296.6 18.3 %collective-permute-start.17 = (bf16[2,320,512]{2,1,0:T(8,128)(2,1)}, bf16[2,320,512]{2,1,0:T(8,128)(2,1)S(1)}, u32[]{:S(2)}, u32[]{:S(2)}) collective-permute-start(bf16[2,320,512]{2,1,0:T(8,128)(2,1)} %get-tuple-element.19), channel_id=1, source_target_pairs={{0,1},{1,2},{2,3},{3,0},{4,5},{5,6},{6,7},{7,4},{8,9},{9,10},{10,1... | collective-permute-start | bytes 1966088 | tf_op jit(solution)/shard_map/ppermute | solution.py:296
  296.6 31.4 %collective-permute-start.18 = (bf16[2,320,512]{2,1,0:T(8,128)(2,1)}, bf16[2,320,512]{2,1,0:T(8,128)(2,1)S(1)}, u32[]{:S(2)}, u32[]{:S(2)}) collective-permute-start(bf16[2,320,512]{2,1,0:T(8,128)(2,1)} %get-tuple-element.20), channel_id=1, source_target_pairs={{0,2},{1,3},{2,0},{3,1},{4,6},{5,7},{6,4},{7,5},{8,10},{9,11},{10,... | collective-permute-start | bytes 1966088 | tf_op jit(solution)/shard_map/ppermute | solution.py:296
  299.0 29.7 %collective-permute-start.19 = (bf16[2,320,512]{2,1,0:T(8,128)(2,1)}, bf16[2,320,512]{2,1,0:T(8,128)(2,1)S(1)}, u32[]{:S(2)}, u32[]{:S(2)}) collective-permute-start(bf16[2,320,512]{2,1,0:T(8,128)(2,1)} %get-tuple-element.21), channel_id=1, source_target_pairs={{0,3},{1,0},{2,1},{3,2},{4,7},{5,4},{6,5},{7,6},{8,11},{9,8},{10,9... | collective-permute-start | bytes 1966088 | tf_op jit(solution)/shard_map/ppermute | solution.py:296
  314.8 13.9 %copy-start.9 = (bf16[2,320,512]{2,1,0:T(8,128)(2,1)}, bf16[2,320,512]{2,1,0:T(8,128)(2,1)S(1)}, u32[]{:S(2)}) copy-start(bf16[2,320,512]{2,1,0:T(8,128)(2,1)S(1)} %collective-permute-done.17.refs_0_) | copy-start | bytes 1966084
  328.0 0.8 copy-start.10
  328.7 0.9 copy-start.11
  334.5 27.9 %all-to-all-start.6 = ((bf16[16,40,512]{2,1,0:T(8,128)(2,1)}), bf16[16,40,512]{2,1,0:T(8,128)(2,1)S(1)}, u32[]{:S(2)}, u32[]{:S(2)}) async-start(bf16[16,40,512]{2,1,0:T(8,128)(2,1)} %bitcast.86), calls=%async_computation.6 | async-start | bytes 1310720 | tf_op jit(solution)/shard_map/all_to_all | solution.py:304
  342.5 6.3 %copy-start.19 = (bf16[640,128]{1,0:T(8,128)(2,1)S(1)}, bf16[640,128]{1,0:T(8,128)(2,1)}, u32[]{:S(2)}) copy-start(bf16[640,128]{1,0:T(8,128)(2,1)} %copy-done.18) | copy-start | bytes 491524
  342.5 6.3 %copy-start.21 = (bf16[640,128]{1,0:T(8,128)(2,1)S(1)}, bf16[640,128]{1,0:T(8,128)(2,1)}, u32[]{:S(2)}) copy-start(bf16[640,128]{1,0:T(8,128)(2,1)} %copy-done.20) | copy-start | bytes 491524
Sparse Core Ops, SparseCore 0:
  10.4 96.1 all-gather.3
  243.9 42.7 reduce-scatter.4
  289.2 50.1 reduce-scatter.2

commit v2 on v1

--- a/solution.py
+++ b/solution.py
@@ -36,8 +36,19 @@
     return copy
 
 
-def wrap(x):
-    return x & (N - 1)
+def place(part, buf, sem):
+    if len(part) == 1:
+        start(part[0], buf, sem)
+    else:
+        for c in range(2):
+            start(part[c], buf.at[c], sem)
+
+
+def grouped(refs):
+    return [[refs[0]], [refs[1]], [refs[2], refs[3]], [refs[4]]]
+
+
+PER = N + 1
 
 
 def vmem(*shape, dtype=BF16):
@@ -51,15 +62,15 @@
     last = base is not None
 
     def body(at_ref, w_ref, *refs):
-        x_refs, refs = refs[:N], refs[N:]
+        x_refs, refs = refs[:PER], refs[PER:]
         if last:
             (base_ref, grad_ref), refs = refs[:2], refs[2:]
             out_h, out_a, w_buf, x_buf, total, h_buf, a_buf, grad_buf, sems = refs
         else:
             out, w_buf, x_buf, total, sems = refs
         for j in range(N):
-            start(w_ref.at[wrap(at_ref[0] + j), pl.ds(offset, 2 * width)], w_buf.at[j], sems.at[j])
-            start(x_refs[j], x_buf.at[j], sems.at[N + j])
+            start(w_ref.at[at_ref[0] ^ j, pl.ds(offset, 2 * width)], w_buf.at[j], sems.at[j])
+            place(grouped(x_refs)[j], x_buf.at[j], sems.at[N + j])
         if last:
             first = start(base_ref, total, sems.at[2 * N])
             second = start(grad_ref, grad_buf, sems.at[2 * N + 1])
@@ -99,11 +110,11 @@
 def fetch(chunks, x_refs, x_bufs, sems, base):
     for j in range(N):
         for h in range(len(chunks)):
-            start(x_refs[h * N + j], x_bufs[h].at[j], sems.at[base + h * N + j])
+            place(grouped(x_refs[h * PER :])[j], x_bufs[h].at[j], sems.at[base + h * N + j])
 
 
 def arrived(x_refs, x_bufs, sems, base, h, j):
-    pltpu.make_async_copy(x_refs[h * N], x_bufs[h].at[j], sems.at[base + h * N + j]).wait()
+    pltpu.make_async_copy(x_refs[h * PER], x_bufs[h].at[j], sems.at[base + h * N + j]).wait()
 
 
 def flat(chunks):
@@ -120,7 +131,7 @@
     count = len(chunks)
 
     def body(at_ref, w_ref, *refs):
-        x_refs, (out, w_buf, *x_bufs, out_buf, sems) = refs[: count * N], refs[count * N :]
+        x_refs, (out, w_buf, *x_bufs, out_buf, sems) = refs[: count * PER], refs[count * PER :]
         first = start(w_ref, w_buf, sems.at[0])
         fetch(chunks, x_refs, x_bufs, sems, 1 + N)
         first.wait()
@@ -135,7 +146,7 @@
                     total = term if total is None else total + term
                     lo += w
             out_buf[j] = total.astype(BF16)
-            start(out_buf.at[j], out.at[wrap(at_ref[0] + j)], sems.at[1 + j])
+            start(out_buf.at[j], out.at[at_ref[0] ^ j], sems.at[1 + j])
             return carry
 
         lax.fori_loop(0, N, step, 0)
@@ -154,7 +165,7 @@
     count = len(chunks)
 
     def body(at_ref, a_ref, *refs):
-        x_refs, (out, a_buf, *x_bufs, out_buf, sems) = refs[: count * N], refs[count * N :]
+        x_refs, (out, a_buf, *x_bufs, out_buf, sems) = refs[: count * PER], refs[count * PER :]
         first = start(a_ref, a_buf, sems.at[0])
         fetch(chunks, x_refs, x_bufs, sems, 1 + N)
         first.wait()
@@ -168,7 +179,7 @@
                     grads = dot(x_bufs[h][j, c], a_buf[:, lo_col : lo_col + units], TN)
                     out_buf[j, lo : lo + w] = grads.astype(BF16)
                     lo += w
-            start(out_buf.at[j], out.at[wrap(at_ref[0] + j)], sems.at[1 + j])
+            start(out_buf.at[j], out.at[at_ref[0] ^ j], sems.at[1 + j])
             return carry
 
         lax.fori_loop(0, N, step, 0)
@@ -186,7 +197,7 @@
     count = len(chunks)
 
     def body(at_ref, h_ref, *refs):
-        x_refs, (out, h_buf, *x_bufs, out_buf, sems) = refs[: count * N], refs[count * N :]
+        x_refs, (out, h_buf, *x_bufs, out_buf, sems) = refs[: count * PER], refs[count * PER :]
         first = start(h_ref, h_buf, sems.at[0])
         fetch(chunks, x_refs, x_bufs, sems, 1)
         out_buf[...] = jnp.zeros_like(out_buf)
@@ -198,7 +209,7 @@
                 w = x_bufs[h].shape[3]
                 arrived(x_refs, x_bufs, sems, 1, h, j)
                 for c in range(2):
-                    out_buf[:, lo : lo + w] += dot(h_buf[wrap(at_ref[0] + j)], x_bufs[h][j, c], TN)
+                    out_buf[:, lo : lo + w] += dot(h_buf[at_ref[0] ^ j], x_bufs[h][j, c], TN)
                     lo += w
             return carry
 
@@ -217,7 +228,7 @@
         outs, (a_buf, w_buf, out_buf, sems) = refs[: N - 1], refs[N - 1 :]
         first = start(a_ref, a_buf, sems.at[0])
         for j in range(1, N):
-            start(w_ref.at[wrap(at_ref[0] + j), pl.ds(offset, 2 * width)], w_buf.at[j - 1], sems.at[j])
+            start(w_ref.at[at_ref[0] ^ j, pl.ds(offset, 2 * width)], w_buf.at[j - 1], sems.at[j])
         first.wait()
 
         def step(j, carry):
@@ -292,8 +303,8 @@
     z_pieces, z_starts = (piece, small), (0, 2 * piece)
     at = lax.axis_index("ffn").astype(jnp.int32)[None]
 
-    def shift(x, by):
-        return lax.ppermute(x, "ffn", [(i, (i + by) % N) for i in range(N)])
+    def swap(x, by):
+        return lax.ppermute(x, "ffn", [(i, i ^ by) for i in range(N)])
 
     def flip(x):
         return lax.ppermute(
@@ -306,7 +317,8 @@
     def gather_rows(packed):
         received = exchange(packed)
         own = dot(order, received.reshape(2 * slots, -1), NN).astype(BF16).reshape(2, slots, -1)
-        return [own, shift(own, -1), shift(own, 2), shift(own, 1)]
+        near, other = swap(own, 1), swap(own, 3)
+        return [own, near, swap(near[0], 3), swap(other[1], 1), other]
 
     z_local = flip(grad_out)
 
@@ -365,13 +377,13 @@
         leads.append(input_partials(acts, w_in, at, starts[h], pieces[h]))
     received = []
     for h in range(2):
-        received.append([shift(leads[h][j - 1], j) for j in range(1, N)])
+        received.append([swap(leads[h][j - 1], j) for j in range(1, N)])
     part_up = weight_grad((x_0, x_1), acts, at, gate_weight.shape[2])
     grad_up = lax.psum_scatter(part_up, "dp", scatter_dimension=0, tiled=True).astype(F32)
 
     grad_tokens = []
     hidden_all = lax.all_gather(hidden, "dp", axis=0, tiled=False)
-    received[1] = lax.optimization_barrier((received[1], hidden_all))[0]
+    received[1], hidden_all, grad_gate = lax.optimization_barrier((received[1], hidden_all, grad_gate))
     for h in range(2):
         total = input_totals(acts, w_in, at, starts[h], received[h], order_back)
         back = exchange(total.reshape(groups, 2 * capacity, -1))

time: 376 us -> 341 us (0.907)
  waiting for transfers between devices: 184 us -> 126 us
  starting transfers between devices: 82.2 us -> 101 us
    ppermute x18 -> x22, waiting for transfers between devices: 123 us -> 67.5 us  [swap(): return lax.ppermute(x, 'ffn', [(i, i ^ by) for i in range(N)])]
    ppermute x18 -> x22, starting transfers between devices: 41.1 us -> 60.9 us  [swap(): return lax.ppermute(x, 'ffn', [(i, i ^ by) for i in range(N)])]
  transfers between devices with their start and end apart: 30 -> 34, of which waited for: 13 -> 16; matrix products, arithmetic and copies ran while one was open for 4% -> 6% of each run, Pallas kernels for 11% -> 12%
where the time goes in v2:
time: 341 us; the launch traced here: 340 us
  waiting for transfers between devices  126 us (37%)
  starting transfers between devices  101 us (30%)
  Pallas kernels  52.3 us (15%)
  blocking collectives  15.9 us (5%)
  between operations  14.4 us (4%)
  other arithmetic  11.1 us (3%)
  matrix products  11 us (3%)
  local copies, waits for them, and re-layouts  8.24 us (2%)
    ppermute x22, waiting for transfers between devices, swap(): return lax.ppermute(x, 'ffn', [(i, i ^ by) for i in range(N)])  67.5 us
    ppermute x22, starting transfers between devices, swap(): return lax.ppermute(x, 'ffn', [(i, i ^ by) for i in range(N)])  60.9 us
    all_to_all x6, waiting for transfers between devices, exchange(): return lax.all_to_all(x, 'expert', split_axis=0, concat_axis=0, tiled=True)  58.8 us
    pallas_call x10, Pallas kernels, call(): pl.pallas_call(body, out_shape=outs, in_specs=[SMEM] + [ANY] * (len(args)...  52.3 us
    all_to_all x6, starting transfers between devices, exchange(): return lax.all_to_all(x, 'expert', split_axis=0, concat_axis=0, tiled=True)  35.3 us
    all_gather x1, blocking collectives, per_device(): hidden_all = lax.all_gather(hidden, 'dp', axis=0, tiled=False)  15.9 us
    dot_general x10, matrix products, dot(): lax.dot_general(a, b, (contract, ((), ())), preferred_element_type=F32)  11 us
  transfers between devices with their start and end apart: 34, of which 16 were waited for; matrix products, arithmetic and copies ran while one was open for 6% of the time, Pallas kernels for 12%

profile of v2, /device:TPU:1, one launch (start us, length us, event | category | flops | bytes accessed | tf_op | source)
XLA Modules:
  0.0 340.4 jit_solution(15238446460516751123)
XLA Ops:
  7.2 2.8 pad_maximum_fusion
  13.9 1.1 convolution_convert_fusion.1
  15.0 10.0 %all-to-all-start.1 = ((bf16[16,40,384]{2,1,0:T(8,128)(2,1)}), bf16[16,40,384]{2,1,0:T(8,128)(2,1)S(1)}, u32[]{:S(2)}, u32[]{:S(2)}) async-start(bf16[16,40,384]{2,1,0:T(8,128)(2,1)} %bitcast.12), calls=%async_computation.1 | async-start | bytes 983040 | tf_op jit(solution)/shard_map/all_to_all | solution.py:315
  25.4 1.2 fusion.8
  26.6 14.9 %all-to-all-done.1 = bf16[16,40,384]{2,1,0:T(8,128)(2,1)S(1)} async-done(((bf16[16,40,384]{2,1,0:T(8,128)(2,1)}), bf16[16,40,384]{2,1,0:T(8,128)(2,1)S(1)}, u32[]{:S(2)}, u32[]{:S(2)}) %all-to-all-start.1) | async-done | bytes 491552 | tf_op jit(solution)/shard_map/all_to_all | solution.py:315
  41.5 3.5 %all-to-all-start.3 = ((bf16[16,40,384]{2,1,0:T(8,128)(2,1)}), bf16[16,40,384]{2,1,0:T(8,128)(2,1)S(1)}, u32[]{:S(2)}, u32[]{:S(2)}) async-start(bf16[16,40,384]{2,1,0:T(8,128)(2,1)} %bitcast.27), calls=%async_computation.3 | async-start | bytes 983040 | tf_op jit(solution)/shard_map/all_to_all | solution.py:315
  45.0 1.2 fusion.7
  46.2 14.8 %all-to-all-done.3 = bf16[16,40,384]{2,1,0:T(8,128)(2,1)S(1)} async-done(((bf16[16,40,384]{2,1,0:T(8,128)(2,1)}), bf16[16,40,384]{2,1,0:T(8,128)(2,1)S(1)}, u32[]{:S(2)}, u32[]{:S(2)}) %all-to-all-start.3) | async-done | bytes 491552 | tf_op jit(solution)/shard_map/all_to_all | solution.py:315
  61.0 3.5 %all-to-all-start.2 = ((bf16[16,40,512]{2,1,0:T(8,128)(2,1)}), bf16[16,40,512]{2,1,0:T(8,128)(2,1)S(1)}, u32[]{:S(2)}, u32[]{:S(2)}) async-start(bf16[16,40,512]{2,1,0:T(8,128)(2,1)} %bitcast.22), calls=%async_computation.2 | async-start | bytes 1310720 | tf_op jit(solution)/shard_map/all_to_all | solution.py:315
  64.5 1.2 convolution_convert_fusion
  65.7 18.3 %all-to-all-done.2 = bf16[16,40,512]{2,1,0:T(8,128)(2,1)S(1)} async-done(((bf16[16,40,512]{2,1,0:T(8,128)(2,1)}), bf16[16,40,512]{2,1,0:T(8,128)(2,1)S(1)}, u32[]{:S(2)}, u32[]{:S(2)}) %all-to-all-start.2) | async-done | bytes 655392 | tf_op jit(solution)/shard_map/all_to_all | solution.py:315
  83.9 4.2 %all-to-all-start = ((bf16[16,40,512]{2,1,0:T(8,128)(2,1)}), bf16[16,40,512]{2,1,0:T(8,128)(2,1)}, u32[]{:S(2)}, u32[]{:S(2)}) async-start(bf16[16,40,512]{2,1,0:T(8,128)(2,1)} %bitcast.7), calls=%async_computation | async-start | bytes 1310720 | tf_op jit(solution)/shard_map/all_to_all | solution.py:315
  88.8 6.7 %collective-permute-start.4 = (bf16[2,320,384]{2,1,0:T(8,128)(2,1)S(1)}, bf16[2,320,384]{2,1,0:T(8,128)(2,1)S(1)}, u32[]{:S(2)}, u32[]{:S(2)}) collective-permute-start(bf16[2,320,384]{2,1,0:T(8,128)(2,1)S(1)} %bitcast.95), channel_id=1, source_target_pairs={{0,1},{1,0},{2,3},{3,2},{4,5},{5,4},{6,7},{7,6},{8,9},{9,8},{10,11... | collective-permute-start | bytes 1474568 | tf_op jit(solution)/shard_map/ppermute | solution.py:307
  95.5 6.9 %collective-permute-start.6 = (bf16[2,320,384]{2,1,0:T(8,128)(2,1)S(1)}, bf16[2,320,384]{2,1,0:T(8,128)(2,1)S(1)}, u32[]{:S(2)}, u32[]{:S(2)}) collective-permute-start(bf16[2,320,384]{2,1,0:T(8,128)(2,1)S(1)} %bitcast.96), channel_id=1, source_target_pairs={{0,3},{1,2},{2,1},{3,0},{4,7},{5,6},{6,5},{7,4},{8,11},{9,10},{10,... | collective-permute-start | bytes 1474568 | tf_op jit(solution)/shard_map/ppermute | solution.py:307
  102.4 1.5 fusion.10
  103.8 0.8 collective-permute-start.14
  105.2 1.6 fusion.6
  107.1 1.8 fusion.5
  108.9 8.5 %collective-permute-done.14.refs_6_ = bf16[2,320,384]{2,1,0:T(8,128)(2,1)S(1)} collective-permute-done((bf16[2,320,384]{2,1,0:T(8,128)(2,1)}, bf16[2,320,384]{2,1,0:T(8,128)(2,1)S(1)}, u32[]{:S(2)}, u32[]{:S(2)}) %collective-permute-start.14) | collective-permute-done | bytes 491552 | tf_op jit(solution)/shard_map/ppermute | solution.py:307
  117.4 8.8 %collective-permute-start.12 = (bf16[2,320,512]{2,1,0:T(8,128)(2,1)}, bf16[2,320,512]{2,1,0:T(8,128)(2,1)S(1)}, u32[]{:S(2)}, u32[]{:S(2)}) collective-permute-start(bf16[2,320,512]{2,1,0:T(8,128)(2,1)} %bitcast.24.refs_0_), channel_id=1, source_target_pairs={{0,3},{1,2},{2,1},{3,0},{4,7},{5,6},{6,5},{7,4},{8,11},{9,10},{10,... | collective-permute-start | bytes 1966088 | tf_op jit(solution)/shard_map/ppermute | solution.py:307
  126.3 1.0 slice_bitcast_fusion.4
  127.3 4.0 %collective-permute-done.10.refs_1_ = bf16[2,320,512]{2,1,0:T(8,128)(2,1)S(1)} collective-permute-done((bf16[2,320,512]{2,1,0:T(8,128)(2,1)}, bf16[2,320,512]{2,1,0:T(8,128)(2,1)S(1)}, u32[]{:S(2)}, u32[]{:S(2)}) %collective-permute-start.10) | collective-permute-done | bytes 655392 | tf_op jit(solution)/shard_map/ppermute | solution.py:307
  131.3 8.8 %collective-permute-start.15 = (bf16[320,384]{1,0:T(8,128)(2,1)S(1)}, bf16[320,384]{1,0:T(8,128)(2,1)S(1)}, u32[]{:S(2)}, u32[]{:S(2)}) collective-permute-start(bf16[320,384]{1,0:T(8,128)(2,1)S(1)} %slice_bitcast_fusion.5), channel_id=1, source_target_pairs={{0,3},{1,2},{2,1},{3,0},{4,7},{5,6},{6,5},{7,4},{8,11},{9,10},{10,... | collective-permute-start | bytes 737288 | tf_op jit(solution)/shard_map/ppermute | solution.py:307
  140.1 1.1 collective-permute-done.12.refs_4_
  141.2 3.0 collective-permute-start.2
  144.3 0.8 collective-permute-done.refs_1_.refs_6_
  145.1 9.0 %collective-permute-start.11 = (bf16[320,512]{1,0:T(8,128)(2,1)S(1)}, bf16[320,512]{1,0:T(8,128)(2,1)}, u32[]{:S(2)}, u32[]{:S(2)}) collective-permute-start(bf16[320,512]{1,0:T(8,128)(2,1)S(1)} %slice_bitcast_fusion.1), channel_id=1, source_target_pairs={{0,3},{1,2},{2,1},{3,0},{4,7},{5,6},{6,5},{7,4},{8,11},{9,10},{10,... | collective-permute-start | bytes 983048 | tf_op jit(solution)/shard_map/ppermute | solution.py:307
  154.2 0.8 slice_bitcast_fusion.7
  155.0 0.7 slice_bitcast_fusion.3
  155.8 3.8 %collective-permute-start.5 = (bf16[320,384]{1,0:T(8,128)(2,1)}, bf16[320,384]{1,0:T(8,128)(2,1)}, u32[]{:S(2)}, u32[]{:S(2)}) collective-permute-start(bf16[320,384]{1,0:T(8,128)(2,1)} %slice_bitcast_fusion.7), channel_id=1, source_target_pairs={{0,3},{1,2},{2,1},{3,0},{4,7},{5,6},{6,5},{7,4},{8,11},{9,10},{10,... | collective-permute-start | bytes 737288 | tf_op jit(solution)/shard_map/ppermute | solution.py:307
  159.5 8.3 %collective-permute-done.11.refs_2_ = bf16[320,512]{1,0:T(8,128)(2,1)} collective-permute-done((bf16[320,512]{1,0:T(8,128)(2,1)S(1)}, bf16[320,512]{1,0:T(8,128)(2,1)}, u32[]{:S(2)}, u32[]{:S(2)}) %collective-permute-start.11) | collective-permute-done | bytes 327712 | tf_op jit(solution)/shard_map/ppermute | solution.py:307
  167.8 2.8 collective-permute-start.1
  170.6 6.3 %shard_map.103 = bf16[4,320,256]{2,1,0:T(8,128)(2,1)} custom-call(s32[1]{0:T(128)} %bitcast.3.at_ref, bf16[256,1792]{1,0:T(8,128)(2,1)} %bitcast.106, bf16[2,320,512]{2,1,0:T(8,128)(2,1)} %bitcast.24.refs_0_, bf16[2,320,512]{2,1,0:T(8,128)(2,1)} %copy-done.6, bf16[320,512]{1,0:T(8,128)(2,1)} %collective-permute-done.11.refs_2_, ...), custom_call_target="tpu_custom_call" | custom-call | tf_op jit(solution)/shard_map/pallas_call | solution.py:24
  177.0 3.5 %all-to-all-start.4 = ((bf16[4,320,256]{2,1,0:T(8,128)(2,1)}), bf16[4,320,256]{2,1,0:T(8,128)(2,1)S(1)}, u32[]{:S(2)}, u32[]{:S(2)}) async-start(bf16[4,320,256]{2,1,0:T(8,128)(2,1)} %shard_map.103), calls=%async_computation.4 | async-start | bytes 1310720 | tf_op jit(solution)/shard_map/all_to_all | solution.py:368
  180.7 1.5 collective-permute-start.7
  182.2 12.7 %collective-permute-done.7.refs_3_ = bf16[320,384]{1,0:T(8,128)(2,1)S(1)} collective-permute-done((bf16[320,384]{1,0:T(8,128)(2,1)S(1)}, bf16[320,384]{1,0:T(8,128)(2,1)S(1)}, u32[]{:S(2)}, u32[]{:S(2)}) %collective-permute-start.7) | collective-permute-done | bytes 245792 | tf_op jit(solution)/shard_map/ppermute | solution.py:307
  195.7 4.2 %shard_map.102.refs_5_ = f32[320,512]{1,0:T(8,128)} custom-call(s32[1]{0:T(128)} %bitcast.3.at_ref, bf16[4,1792,512]{2,1,0:T(8,128)(2,1)} %bitcast.84, bf16[2,320,384]{2,1,0:T(8,128)(2,1)} %bitcast.97, bf16[2,320,384]{2,1,0:T(8,128)(2,1)} %copy-done.2, bf16[320,384]{1,0:T(8,128)(2,1)} %collective-permute-done.5.refs_2_, bf16[320,384]{1,0:T(8,128)(2,1)} %copy-done.11, ...), custom_call_target="tpu_custom_call" | custom-call | tf_op jit(solution)/shard_map/pallas_call | solution.py:24
  200.6 0.8 copy-done.10
  201.5 6.2 %shard_map.104 = (bf16[320,256]{1,0:T(8,128)(2,1)}, bf16[320,512]{1,0:T(8,128)(2,1)}) custom-call(s32[1]{0:T(128)} %bitcast.3.at_ref, bf16[4,1792,512]{2,1,0:T(8,128)(2,1)} %bitcast.85, bf16[2,320,512]{2,1,0:T(8,128)(2,1)} %bitcast.92, bf16[2,320,512]{2,1,0:T(8,128)(2,1)} %copy-done, bf16[320,512]{1,0:T(8,128)(2,1)} %collective-permute-done.1.refs_2_.refs_7_, ...), custom_call_target="tpu_custom_call" | custom-call | tf_op jit(solution)/shard_map/pallas_call | solution.py:24
  207.7 5.8 %shard_map.108 = bf16[4,1792,256]{2,1,0:T(8,128)(2,1)} custom-call(s32[1]{0:T(128)} %bitcast.3.at_ref, bf16[320,512]{1,0:T(8,128)(2,1)} %get-tuple-element.17.a_ref, bf16[2,320,384]{2,1,0:T(8,128)(2,1)} %bitcast.98, bf16[2,320,384]{2,1,0:T(8,128)(2,1)} %copy-done.2, bf16[320,384]{1,0:T(8,128)(2,1)} %collective-permute-done.5.refs_2_, ...), custom_call_target="tpu_custom_call" | custom-call | tf_op jit(solution)/shard_map/pallas_call | solution.py:24
  213.6 5.8 %shard_map.110 = bf16[4,1792,256]{2,1,0:T(8,128)(2,1)} custom-call(s32[1]{0:T(128)} %bitcast.3.at_ref, bf16[320,512]{1,0:T(8,128)(2,1)} %get-tuple-element.17.a_ref, bf16[2,320,384]{2,1,0:T(8,128)(2,1)} %bitcast.99, bf16[2,320,384]{2,1,0:T(8,128)(2,1)} %copy-done.2, bf16[320,384]{1,0:T(8,128)(2,1)} %collective-permute-done.5.refs_2_, ...), custom_call_target="tpu_custom_call" | custom-call | tf_op jit(solution)/shard_map/pallas_call | solution.py:24
  219.4 4.2 %shard_map.105 = (bf16[2,320,384]{2,1,0:T(8,128)(2,1)}, bf16[2,320,384]{2,1,0:T(8,128)(2,1)}, bf16[2,320,384]{2,1,0:T(8,128)(2,1)}) custom-call(s32[1]{0:T(128)} %bitcast.3.at_ref, bf16[320,512]{1,0:T(8,128)(2,1)} %get-tuple-element.17.a_ref, bf16[4,1792,512]{2,1,0:T(8,128)(2,1)} %bitcast.86), custom_call_target="tpu_custom_call" | custom-call | tf_op jit(solution)/shard_map/pallas_call | solution.py:24
  223.8 0.8 collective-permute-start.19
  224.5 3.1 collective-permute-start.20
  227.6 1.1 fusion.4.order_ref
  228.8 6.9 %collective-permute-done.18.refs_0_ = bf16[2,320,384]{2,1,0:T(8,128)(2,1)S(1)} collective-permute-done((bf16[2,320,384]{2,1,0:T(8,128)(2,1)}, bf16[2,320,384]{2,1,0:T(8,128)(2,1)S(1)}, u32[]{:S(2)}, u32[]{:S(2)}) %collective-permute-start.18) | collective-permute-done | bytes 491552 | tf_op jit(solution)/shard_map/ppermute | solution.py:307
  235.7 9.6 %collective-permute-done.19.refs_1_ = bf16[2,320,384]{2,1,0:T(8,128)(2,1)S(1)} collective-permute-done((bf16[2,320,384]{2,1,0:T(8,128)(2,1)}, bf16[2,320,384]{2,1,0:T(8,128)(2,1)S(1)}, u32[]{:S(2)}, u32[]{:S(2)}) %collective-permute-start.19) | collective-permute-done | bytes 491552 | tf_op jit(solution)/shard_map/ppermute | solution.py:307
  245.3 3.0 collective-permute-done.20.refs_2_
  248.3 0.8 copy-done.19
  249.1 4.4 %shard_map.106 = bf16[640,384]{1,0:T(8,128)(2,1)} custom-call(s32[1]{0:T(128)} %bitcast.3.at_ref, bf16[320,512]{1,0:T(8,128)(2,1)} %get-tuple-element.17.a_ref, bf16[4,1792,512]{2,1,0:T(8,128)(2,1)} %bitcast.87, bf16[640,640]{1,0:T(8,128)(2,1)} %fusion.4.order_ref, bf16[2,320,384]{2,1,0:T(8,128)(2,1)} %copy-done.17, bf16[2,320,384]{2,1,0:T(8,128)(2,1)} %copy-done.18, ...), custom_call_target="tpu_custom_call" | custom-call | tf_op jit(solution)/shard_map/pallas_call | solution.py:24
  253.5 5.7 %all-to-all-start.5 = ((bf16[16,40,384]{2,1,0:T(8,128)(2,1)}), bf16[16,40,384]{2,1,0:T(8,128)(2,1)S(1)}, u32[]{:S(2)}, u32[]{:S(2)}) async-start(bf16[16,40,384]{2,1,0:T(8,128)(2,1)} %bitcast.102), calls=%async_computation.5 | async-start | bytes 983040 | tf_op jit(solution)/shard_map/all_to_all | solution.py:315
  259.2 4.3 %shard_map.107 = (bf16[2,320,512]{2,1,0:T(8,128)(2,1)}, bf16[2,320,512]{2,1,0:T(8,128)(2,1)}, bf16[2,320,512]{2,1,0:T(8,128)(2,1)}) custom-call(s32[1]{0:T(128)} %bitcast.3.at_ref, bf16[320,512]{1,0:T(8,128)(2,1)} %get-tuple-element.17.a_ref, bf16[4,1792,512]{2,1,0:T(8,128)(2,1)} %bitcast.88), custom_call_target="tpu_custom_call" | custom-call | tf_op jit(solution)/shard_map/pallas_call | solution.py:24
  263.6 3.8 %collective-permute-start.22 = (bf16[2,320,512]{2,1,0:T(8,128)(2,1)}, bf16[2,320,512]{2,1,0:T(8,128)(2,1)S(1)}, u32[]{:S(2)}, u32[]{:S(2)}) collective-permute-start(bf16[2,320,512]{2,1,0:T(8,128)(2,1)} %get-tuple-element.22), channel_id=1, source_target_pairs={{0,2},{1,3},{2,0},{3,1},{4,6},{5,7},{6,4},{7,5},{8,10},{9,11},{10,... | collective-permute-start | bytes 1966088 | tf_op jit(solution)/shard_map/ppermute | solution.py:307
  267.4 15.9 %all-gather.1 = bf16[1280,256]{1,0:T(8,128)(2,1)} all-gather(bf16[320,256]{1,0:T(8,128)(2,1)S(1)} %copy-done.25), channel_id=3, replica_groups=mesh['dp'=4,'expert'=16,'ffn'=4] {'dp'}, dimensions={0}, use_global_device_ids=true | all-gather | bytes 819200 | tf_op jit(solution)/shard_map/all_gather | solution.py:385
  283.3 2.5 convert_element_type.101
  285.9 10.4 %collective-permute-done.22.refs_1_ = bf16[2,320,512]{2,1,0:T(8,128)(2,1)S(1)} collective-permute-done((bf16[2,320,512]{2,1,0:T(8,128)(2,1)}, bf16[2,320,512]{2,1,0:T(8,128)(2,1)S(1)}, u32[]{:S(2)}, u32[]{:S(2)}) %collective-permute-start.22) | collective-permute-done | bytes 655392 | tf_op jit(solution)/shard_map/ppermute | solution.py:307
  296.3 2.2 collective-permute-done.23.refs_2_
  298.5 0.8 copy-done.16
  299.4 4.9 %shard_map.109 = bf16[640,512]{1,0:T(8,128)(2,1)} custom-call(s32[1]{0:T(128)} %bitcast.3.at_ref, bf16[320,512]{1,0:T(8,128)(2,1)} %get-tuple-element.17.a_ref, bf16[4,1792,512]{2,1,0:T(8,128)(2,1)} %bitcast.89, bf16[640,640]{1,0:T(8,128)(2,1)} %fusion.4.order_ref, bf16[2,320,512]{2,1,0:T(8,128)(2,1)} %copy-done.14, bf16[2,320,512]{2,1,0:T(8,128)(2,1)} %copy-done.15, ...), custom_call_target="tpu_custom_call" | custom-call | tf_op jit(solution)/shard_map/pallas_call | solution.py:24
  304.3 8.4 %all-to-all-start.6 = ((bf16[16,40,512]{2,1,0:T(8,128)(2,1)}), bf16[16,40,512]{2,1,0:T(8,128)(2,1)S(1)}, u32[]{:S(2)}, u32[]{:S(2)}) async-start(bf16[16,40,512]{2,1,0:T(8,128)(2,1)} %bitcast.100), calls=%async_computation.7 | async-start | bytes 1310720 | tf_op jit(solution)/shard_map/all_to_all | solution.py:315
  313.2 6.2 %shard_map.111 = f32[256,1792]{1,0:T(8,128)} custom-call(s32[1]{0:T(128)} %bitcast.3.at_ref, bf16[4,320,256]{2,1,0:T(8,128)(2,1)} %bitcast.101, bf16[2,320,512]{2,1,0:T(8,128)(2,1)} %bitcast.24.refs_0_, bf16[2,320,512]{2,1,0:T(8,128)(2,1)} %copy-done.6, bf16[320,512]{1,0:T(8,128)(2,1)} %collective-permute-done.11.refs_2_, ...), custom_call_target="tpu_custom_call" | custom-call | tf_op jit(solution)/shard_map/pallas_call | solution.py:24
  319.4 2.5 convert_element_type.103
  322.0 10.7 %all-to-all-done.6 = bf16[16,40,512]{2,1,0:T(8,128)(2,1)S(1)} async-done(((bf16[16,40,512]{2,1,0:T(8,128)(2,1)}), bf16[16,40,512]{2,1,0:T(8,128)(2,1)S(1)}, u32[]{:S(2)}, u32[]{:S(2)}) %all-to-all-start.6) | async-done | bytes 655392 | tf_op jit(solution)/shard_map/all_to_all | solution.py:315
  333.1 0.8 pad_maximum_fusion.1
  (128 shorter events, 8.8 us)
Async XLA Ops:
  7.2 187.8 %all-gather.4.cloned.1.call-start = ((), (), s32[]{:S(2)}) async-start(), calls=%async_computation.11 | async-start | bytes 9175040 | tf_op jit(solution)/shard_map/all_gather | solution.py:331
  10.0 0.7 copy-start.26
  10.0 2.2 copy-start.27
  10.0 2.9 copy-start.28
  10.0 3.7 %copy-start.20 = (bf16[128,1792]{1,0:T(8,128)(2,1)S(1)}, bf16[128,1792]{1,0:T(8,128)(2,1)}, u32[]{:S(2)}) copy-start(bf16[128,1792]{1,0:T(8,128)(2,1)} %param.7) | copy-start | bytes 1376260
  12.3 12.7 %collective-permute-start.8 = (f32[128,4]{0,1:T(4,128)S(1)}, f32[128,4]{0,1:T(4,128)S(1)}, u32[]{:S(2)}, u32[]{:S(2)}) collective-permute-start(f32[128,4]{0,1:T(4,128)S(1)} %pad_maximum_fusion.6), channel_id=1, source_target_pairs={{0,0},{1,64},{2,128},{3,192},{64,1},{65,65},{66,129},{67,193},{128... | collective-permute-start | bytes 6152 | tf_op jit(solution)/shard_map/ppermute | solution.py:310
  13.0 12.4 %collective-permute-start.9 = (bf16[128,1792]{1,0:T(8,128)(2,1)S(1)}, bf16[128,1792]{1,0:T(8,128)(2,1)S(1)}, u32[]{:S(2)}, u32[]{:S(2)}) collective-permute-start(bf16[128,1792]{1,0:T(8,128)(2,1)S(1)} %copy-done.28), channel_id=1, source_target_pairs={{0,0},{1,64},{2,128},{3,192},{64,1},{65,65},{66,129},{67,193},{128... | collective-permute-start | bytes 1376264 | tf_op jit(solution)/shard_map/ppermute | solution.py:310
  13.9 50.6 %copy-start.21 = (bf16[640,128]{1,0:T(8,128)(2,1)}, bf16[640,128]{1,0:T(8,128)(2,1)S(1)}, u32[]{:S(2)}) copy-start(bf16[640,128]{1,0:T(8,128)(2,1)S(1)} %get-tuple-element.54) | copy-start | bytes 491524
  13.9 50.6 %copy-start.23 = (bf16[640,128]{1,0:T(8,128)(2,1)}, bf16[640,128]{1,0:T(8,128)(2,1)S(1)}, u32[]{:S(2)}) copy-start(bf16[640,128]{1,0:T(8,128)(2,1)S(1)} %get-tuple-element.55) | copy-start | bytes 491524
  15.0 26.5 %all-to-all-start.1 = ((bf16[16,40,384]{2,1,0:T(8,128)(2,1)}), bf16[16,40,384]{2,1,0:T(8,128)(2,1)S(1)}, u32[]{:S(2)}, u32[]{:S(2)}) async-start(bf16[16,40,384]{2,1,0:T(8,128)(2,1)} %bitcast.12), calls=%async_computation.1 | async-start | bytes 983040 | tf_op jit(solution)/shard_map/all_to_all | solution.py:315
  41.5 19.4 %all-to-all-start.3 = ((bf16[16,40,384]{2,1,0:T(8,128)(2,1)}), bf16[16,40,384]{2,1,0:T(8,128)(2,1)S(1)}, u32[]{:S(2)}, u32[]{:S(2)}) async-start(bf16[16,40,384]{2,1,0:T(8,128)(2,1)} %bitcast.27), calls=%async_computation.3 | async-start | bytes 983040 | tf_op jit(solution)/shard_map/all_to_all | solution.py:315
  61.0 23.0 %all-to-all-start.2 = ((bf16[16,40,512]{2,1,0:T(8,128)(2,1)}), bf16[16,40,512]{2,1,0:T(8,128)(2,1)S(1)}, u32[]{:S(2)}, u32[]{:S(2)}) async-start(bf16[16,40,512]{2,1,0:T(8,128)(2,1)} %bitcast.22), calls=%async_computation.2 | async-start | bytes 1310720 | tf_op jit(solution)/shard_map/all_to_all | solution.py:315
  83.9 23.1 %all-to-all-start = ((bf16[16,40,512]{2,1,0:T(8,128)(2,1)}), bf16[16,40,512]{2,1,0:T(8,128)(2,1)}, u32[]{:S(2)}, u32[]{:S(2)}) async-start(bf16[16,40,512]{2,1,0:T(8,128)(2,1)} %bitcast.7), calls=%async_computation | async-start | bytes 1310720 | tf_op jit(solution)/shard_map/all_to_all | solution.py:315
  88.8 18.0 %copy-start.5 = (bf16[640,384]{1,0:T(8,128)(2,1)}, bf16[640,384]{1,0:T(8,128)(2,1)S(1)}, u32[]{:S(2)}) copy-start(bf16[640,384]{1,0:T(8,128)(2,1)S(1)} %fusion.9) | copy-start | bytes 1474564
  88.8 55.4 %collective-permute-start.4 = (bf16[2,320,384]{2,1,0:T(8,128)(2,1)S(1)}, bf16[2,320,384]{2,1,0:T(8,128)(2,1)S(1)}, u32[]{:S(2)}, u32[]{:S(2)}) collective-permute-start(bf16[2,320,384]{2,1,0:T(8,128)(2,1)S(1)} %bitcast.95), channel_id=1, source_target_pairs={{0,1},{1,0},{2,3},{3,2},{4,5},{5,4},{6,7},{7,6},{8,9},{9,8},{10,11... | collective-permute-start | bytes 1474568 | tf_op jit(solution)/shard_map/ppermute | solution.py:307
  95.5 85.1 %collective-permute-start.6 = (bf16[2,320,384]{2,1,0:T(8,128)(2,1)S(1)}, bf16[2,320,384]{2,1,0:T(8,128)(2,1)S(1)}, u32[]{:S(2)}, u32[]{:S(2)}) collective-permute-start(bf16[2,320,384]{2,1,0:T(8,128)(2,1)S(1)} %bitcast.96), channel_id=1, source_target_pairs={{0,3},{1,2},{2,1},{3,0},{4,7},{5,6},{6,5},{7,4},{8,11},{9,10},{10,... | collective-permute-start | bytes 1474568 | tf_op jit(solution)/shard_map/ppermute | solution.py:307
  103.8 13.6 %collective-permute-start.14 = (bf16[2,320,384]{2,1,0:T(8,128)(2,1)}, bf16[2,320,384]{2,1,0:T(8,128)(2,1)S(1)}, u32[]{:S(2)}, u32[]{:S(2)}) collective-permute-start(bf16[2,320,384]{2,1,0:T(8,128)(2,1)} %bitcast.29.refs_5_), channel_id=1, source_target_pairs={{0,1},{1,0},{2,3},{3,2},{4,5},{5,4},{6,7},{7,6},{8,9},{9,8},{10,11... | collective-permute-start | bytes 1474568 | tf_op jit(solution)/shard_map/ppermute | solution.py:307
  104.6 21.6 %collective-permute-start.16 = (bf16[2,320,384]{2,1,0:T(8,128)(2,1)}, bf16[2,320,384]{2,1,0:T(8,128)(2,1)}, u32[]{:S(2)}, u32[]{:S(2)}) collective-permute-start(bf16[2,320,384]{2,1,0:T(8,128)(2,1)} %bitcast.29.refs_5_), channel_id=1, source_target_pairs={{0,3},{1,2},{2,1},{3,0},{4,7},{5,6},{6,5},{7,4},{8,11},{9,10},{10,... | collective-permute-start | bytes 1474568 | tf_op jit(solution)/shard_map/ppermute | solution.py:307
  106.8 24.5 %collective-permute-start.10 = (bf16[2,320,512]{2,1,0:T(8,128)(2,1)}, bf16[2,320,512]{2,1,0:T(8,128)(2,1)S(1)}, u32[]{:S(2)}, u32[]{:S(2)}) collective-permute-start(bf16[2,320,512]{2,1,0:T(8,128)(2,1)} %bitcast.24.refs_0_), channel_id=1, source_target_pairs={{0,1},{1,0},{2,3},{3,2},{4,5},{5,4},{6,7},{7,6},{8,9},{9,8},{10,11... | collective-permute-start | bytes 1966088 | tf_op jit(solution)/shard_map/ppermute | solution.py:307
  108.9 46.9 %copy-start.4 = (bf16[640,512]{1,0:T(8,128)(2,1)}, bf16[640,512]{1,0:T(8,128)(2,1)S(1)}, u32[]{:S(2)}) copy-start(bf16[640,512]{1,0:T(8,128)(2,1)S(1)} %fusion.5) | copy-start | bytes 1966084
  117.4 8.8 %copy-start.8 = (bf16[2,320,384]{2,1,0:T(8,128)(2,1)}, bf16[2,320,384]{2,1,0:T(8,128)(2,1)S(1)}, u32[]{:S(2)}) copy-start(bf16[2,320,384]{2,1,0:T(8,128)(2,1)S(1)} %collective-permute-done.14.refs_6_) | copy-start | bytes 1474564
  117.4 23.8 %collective-permute-start.12 = (bf16[2,320,512]{2,1,0:T(8,128)(2,1)}, bf16[2,320,512]{2,1,0:T(8,128)(2,1)S(1)}, u32[]{:S(2)}, u32[]{:S(2)}) collective-permute-start(bf16[2,320,512]{2,1,0:T(8,128)(2,1)} %bitcast.24.refs_0_), channel_id=1, source_target_pairs={{0,3},{1,2},{2,1},{3,0},{4,7},{5,6},{6,5},{7,4},{8,11},{9,10},{10,... | collective-permute-start | bytes 1966088 | tf_op jit(solution)/shard_map/ppermute | solution.py:307
  126.2 18.9 %collective-permute-start = (bf16[2,320,512]{2,1,0:T(8,128)(2,1)S(1)}, bf16[2,320,512]{2,1,0:T(8,128)(2,1)S(1)}, u32[]{:S(2)}, u32[]{:S(2)}) collective-permute-start(bf16[2,320,512]{2,1,0:T(8,128)(2,1)S(1)} %bitcast.90), channel_id=1, source_target_pairs={{0,1},{1,0},{2,3},{3,2},{4,5},{5,4},{6,7},{7,6},{8,9},{9,8},{10,11... | collective-permute-start | bytes 1966088 | tf_op jit(solution)/shard_map/ppermute | solution.py:307
  131.3 8.8 %copy-start.6 = (bf16[2,320,512]{2,1,0:T(8,128)(2,1)}, bf16[2,320,512]{2,1,0:T(8,128)(2,1)S(1)}, u32[]{:S(2)}) copy-start(bf16[2,320,512]{2,1,0:T(8,128)(2,1)S(1)} %collective-permute-done.10.refs_1_) | copy-start | bytes 1966084
  131.3 22.8 %collective-permute-start.15 = (bf16[320,384]{1,0:T(8,128)(2,1)S(1)}, bf16[320,384]{1,0:T(8,128)(2,1)S(1)}, u32[]{:S(2)}, u32[]{:S(2)}) collective-permute-start(bf16[320,384]{1,0:T(8,128)(2,1)S(1)} %slice_bitcast_fusion.5), channel_id=1, source_target_pairs={{0,3},{1,2},{2,1},{3,0},{4,7},{5,6},{6,5},{7,4},{8,11},{9,10},{10,... | collective-permute-start | bytes 737288 | tf_op jit(solution)/shard_map/ppermute | solution.py:307
  141.2 14.5 %copy-start.7 = (bf16[2,320,512]{2,1,0:T(8,128)(2,1)}, bf16[2,320,512]{2,1,0:T(8,128)(2,1)S(1)}, u32[]{:S(2)}) copy-start(bf16[2,320,512]{2,1,0:T(8,128)(2,1)S(1)} %collective-permute-done.12.refs_4_) | copy-start | bytes 1966084
  141.2 39.3 %collective-permute-start.2 = (bf16[2,320,512]{2,1,0:T(8,128)(2,1)S(1)}, bf16[2,320,512]{2,1,0:T(8,128)(2,1)S(1)}, u32[]{:S(2)}, u32[]{:S(2)}) collective-permute-start(bf16[2,320,512]{2,1,0:T(8,128)(2,1)S(1)} %bitcast.91), channel_id=1, source_target_pairs={{0,3},{1,2},{2,1},{3,0},{4,7},{5,6},{6,5},{7,4},{8,11},{9,10},{10,... | collective-permute-start | bytes 1966088 | tf_op jit(solution)/shard_map/ppermute | solution.py:307
  144.2 32.7 %copy-start.2 = (bf16[2,320,384]{2,1,0:T(8,128)(2,1)}, bf16[2,320,384]{2,1,0:T(8,128)(2,1)S(1)}, u32[]{:S(2)}) copy-start(bf16[2,320,384]{2,1,0:T(8,128)(2,1)S(1)} %collective-permute-done.4.refs_1_) | copy-start | bytes 1474564
  144.2 11.5 %collective-permute-start.17 = (bf16[320,384]{1,0:T(8,128)(2,1)S(1)}, bf16[320,384]{1,0:T(8,128)(2,1)S(1)}, u32[]{:S(2)}, u32[]{:S(2)}) collective-permute-start(bf16[320,384]{1,0:T(8,128)(2,1)S(1)} %slice_bitcast_fusion.4), channel_id=1, source_target_pairs={{0,1},{1,0},{2,3},{3,2},{4,5},{5,4},{6,7},{7,6},{8,9},{9,8},{10,11... | collective-permute-start | bytes 737288 | tf_op jit(solution)/shard_map/ppermute | solution.py:307
  145.1 31.8 %copy-start = (bf16[2,320,512]{2,1,0:T(8,128)(2,1)}, bf16[2,320,512]{2,1,0:T(8,128)(2,1)S(1)}, u32[]{:S(2)}) copy-start(bf16[2,320,512]{2,1,0:T(8,128)(2,1)S(1)} %collective-permute-done.refs_1_.refs_6_) | copy-start | bytes 1966084
  145.1 22.7 %collective-permute-start.11 = (bf16[320,512]{1,0:T(8,128)(2,1)S(1)}, bf16[320,512]{1,0:T(8,128)(2,1)}, u32[]{:S(2)}, u32[]{:S(2)}) collective-permute-start(bf16[320,512]{1,0:T(8,128)(2,1)S(1)} %slice_bitcast_fusion.1), channel_id=1, source_target_pairs={{0,3},{1,2},{2,1},{3,0},{4,7},{5,6},{6,5},{7,4},{8,11},{9,10},{10,... | collective-permute-start | bytes 983048 | tf_op jit(solution)/shard_map/ppermute | solution.py:307
  154.2 5.4 %copy-start.12 = (bf16[320,384]{1,0:T(8,128)(2,1)}, bf16[320,384]{1,0:T(8,128)(2,1)S(1)}, u32[]{:S(2)}) copy-start(bf16[320,384]{1,0:T(8,128)(2,1)S(1)} %collective-permute-done.15.refs_7_) | copy-start | bytes 737284
  154.2 16.5 %collective-permute-start.13 = (bf16[320,512]{1,0:T(8,128)(2,1)S(1)}, bf16[320,512]{1,0:T(8,128)(2,1)}, u32[]{:S(2)}, u32[]{:S(2)}) collective-permute-start(bf16[320,512]{1,0:T(8,128)(2,1)S(1)} %slice_bitcast_fusion), channel_id=1, source_target_pairs={{0,1},{1,0},{2,3},{3,2},{4,5},{5,4},{6,7},{7,6},{8,9},{9,8},{10,11... | collective-permute-start | bytes 983048 | tf_op jit(solution)/shard_map/ppermute | solution.py:307
  155.7 12.1 %copy-start.13 = (bf16[320,384]{1,0:T(8,128)(2,1)}, bf16[320,384]{1,0:T(8,128)(2,1)S(1)}, u32[]{:S(2)}) copy-start(bf16[320,384]{1,0:T(8,128)(2,1)S(1)} %collective-permute-done.17.refs_8_) | copy-start | bytes 737284
  155.8 26.5 %collective-permute-start.5 = (bf16[320,384]{1,0:T(8,128)(2,1)}, bf16[320,384]{1,0:T(8,128)(2,1)}, u32[]{:S(2)}, u32[]{:S(2)}) collective-permute-start(bf16[320,384]{1,0:T(8,128)(2,1)} %slice_bitcast_fusion.7), channel_id=1, source_target_pairs={{0,3},{1,2},{2,1},{3,0},{4,7},{5,6},{6,5},{7,4},{8,11},{9,10},{10,... | collective-permute-start | bytes 737288 | tf_op jit(solution)/shard_map/ppermute | solution.py:307
  167.8 32.1 %collective-permute-start.1 = (bf16[320,512]{1,0:T(8,128)(2,1)}, bf16[320,512]{1,0:T(8,128)(2,1)}, u32[]{:S(2)}, u32[]{:S(2)}) collective-permute-start(bf16[320,512]{1,0:T(8,128)(2,1)} %slice_bitcast_fusion.3), channel_id=1, source_target_pairs={{0,3},{1,2},{2,1},{3,0},{4,7},{5,6},{6,5},{7,4},{8,11},{9,10},{10,... | collective-permute-start | bytes 983048 | tf_op jit(solution)/shard_map/ppermute | solution.py:307
  177.0 23.0 %all-to-all-start.4 = ((bf16[4,320,256]{2,1,0:T(8,128)(2,1)}), bf16[4,320,256]{2,1,0:T(8,128)(2,1)S(1)}, u32[]{:S(2)}, u32[]{:S(2)}) async-start(bf16[4,320,256]{2,1,0:T(8,128)(2,1)} %shard_map.103), calls=%async_computation.4 | async-start | bytes 1310720 | tf_op jit(solution)/shard_map/all_to_all | solution.py:368
  180.5 102.9 %reduce-scatter.3.cloned.1.call-start = ((), (), s32[]{:S(2)}) async-start(), calls=%async_computation.9 | async-start | bytes 4587520 | tf_op jit(solution)/shard_map/reduce_scatter | solution.py:373
  180.5 19.4 %copy-start.1 = (bf16[2,320,512]{2,1,0:T(8,128)(2,1)}, bf16[2,320,512]{2,1,0:T(8,128)(2,1)S(1)}, u32[]{:S(2)}) copy-start(bf16[2,320,512]{2,1,0:T(8,128)(2,1)S(1)} %collective-permute-done.2.refs_4_.refs_9_) | copy-start | bytes 1966084
  180.6 19.3 %collective-permute-start.3 = (bf16[320,512]{1,0:T(8,128)(2,1)S(1)}, bf16[320,512]{1,0:T(8,128)(2,1)S(1)}, u32[]{:S(2)}, u32[]{:S(2)}) collective-permute-start(bf16[320,512]{1,0:T(8,128)(2,1)S(1)} %slice_bitcast_fusion.2), channel_id=1, source_target_pairs={{0,1},{1,0},{2,3},{3,2},{4,5},{5,4},{6,7},{7,6},{8,9},{9,8},{10,11... | collective-permute-start | bytes 983048 | tf_op jit(solution)/shard_map/ppermute | solution.py:307
  180.7 14.3 %copy-start.3 = (bf16[2,320,384]{2,1,0:T(8,128)(2,1)}, bf16[2,320,384]{2,1,0:T(8,128)(2,1)S(1)}, u32[]{:S(2)}) copy-start(bf16[2,320,384]{2,1,0:T(8,128)(2,1)S(1)} %collective-permute-done.6.refs_4_) | copy-start | bytes 1474564
  180.7 14.2 %collective-permute-start.7 = (bf16[320,384]{1,0:T(8,128)(2,1)S(1)}, bf16[320,384]{1,0:T(8,128)(2,1)S(1)}, u32[]{:S(2)}, u32[]{:S(2)}) collective-permute-start(bf16[320,384]{1,0:T(8,128)(2,1)S(1)} %slice_bitcast_fusion.6), channel_id=1, source_target_pairs={{0,1},{1,0},{2,3},{3,2},{4,5},{5,4},{6,7},{7,6},{8,9},{9,8},{10,11... | collective-permute-start | bytes 737288 | tf_op jit(solution)/shard_map/ppermute | solution.py:307
  194.9 0.7 copy-start.11
  199.9 0.7 copy-start.9
  200.6 0.8 copy-start.10
  213.5 105.9 %reduce-scatter.5.cloned.1.call-start = ((), (), s32[]{:S(2)}) async-start(), calls=%async_computation.10 | async-start | bytes 4587520 | tf_op jit(solution)/shard_map/reduce_scatter | solution.py:382
  223.7 12.0 %collective-permute-start.18 = (bf16[2,320,384]{2,1,0:T(8,128)(2,1)}, bf16[2,320,384]{2,1,0:T(8,128)(2,1)S(1)}, u32[]{:S(2)}, u32[]{:S(2)}) collective-permute-start(bf16[2,320,384]{2,1,0:T(8,128)(2,1)} %get-tuple-element.18), channel_id=1, source_target_pairs={{0,1},{1,0},{2,3},{3,2},{4,5},{5,4},{6,7},{7,6},{8,9},{9,8},{10,11... | collective-permute-start | bytes 1474568 | tf_op jit(solution)/shard_map/ppermute | solution.py:307
  223.8 21.5 %collective-permute-start.19 = (bf16[2,320,384]{2,1,0:T(8,128)(2,1)}, bf16[2,320,384]{2,1,0:T(8,128)(2,1)S(1)}, u32[]{:S(2)}, u32[]{:S(2)}) collective-permute-start(bf16[2,320,384]{2,1,0:T(8,128)(2,1)} %get-tuple-element.19), channel_id=1, source_target_pairs={{0,2},{1,3},{2,0},{3,1},{4,6},{5,7},{6,4},{7,5},{8,10},{9,11},{10,... | collective-permute-start | bytes 1474568 | tf_op jit(solution)/shard_map/ppermute | solution.py:307
  224.5 23.7 %collective-permute-start.20 = (bf16[2,320,384]{2,1,0:T(8,128)(2,1)}, bf16[2,320,384]{2,1,0:T(8,128)(2,1)S(1)}, u32[]{:S(2)}, u32[]{:S(2)}) collective-permute-start(bf16[2,320,384]{2,1,0:T(8,128)(2,1)} %get-tuple-element.20), channel_id=1, source_target_pairs={{0,3},{1,2},{2,1},{3,0},{4,7},{5,6},{6,5},{7,4},{8,11},{9,10},{10,... | collective-permute-start | bytes 1474568 | tf_op jit(solution)/shard_map/ppermute | solution.py:307
  235.7 12.5 %copy-start.17 = (bf16[2,320,384]{2,1,0:T(8,128)(2,1)}, bf16[2,320,384]{2,1,0:T(8,128)(2,1)S(1)}, u32[]{:S(2)}) copy-start(bf16[2,320,384]{2,1,0:T(8,128)(2,1)S(1)} %collective-permute-done.18.refs_0_) | copy-start | bytes 1474564
  245.3 3.0 copy-start.18
  248.2 0.8 copy-start.19
  253.5 50.8 %all-to-all-start.5 = ((bf16[16,40,384]{2,1,0:T(8,128)(2,1)}), bf16[16,40,384]{2,1,0:T(8,128)(2,1)S(1)}, u32[]{:S(2)}, u32[]{:S(2)}) async-start(bf16[16,40,384]{2,1,0:T(8,128)(2,1)} %bitcast.102), calls=%async_computation.5 | async-start | bytes 983040 | tf_op jit(solution)/shard_map/all_to_all | solution.py:315
  259.2 8.2 %copy-start.25 = (bf16[320,256]{1,0:T(8,128)(2,1)S(1)}, bf16[320,256]{1,0:T(8,128)(2,1)}, u32[]{:S(2)}) copy-start(bf16[320,256]{1,0:T(8,128)(2,1)} %get-tuple-element.24) | copy-start | bytes 491524
  263.5 22.4 %collective-permute-start.21 = (bf16[2,320,512]{2,1,0:T(8,128)(2,1)}, bf16[2,320,512]{2,1,0:T(8,128)(2,1)S(1)}, u32[]{:S(2)}, u32[]{:S(2)}) collective-permute-start(bf16[2,320,512]{2,1,0:T(8,128)(2,1)} %get-tuple-element.21), channel_id=1, source_target_pairs={{0,1},{1,0},{2,3},{3,2},{4,5},{5,4},{6,7},{7,6},{8,9},{9,8},{10,11... | collective-permute-start | bytes 1966088 | tf_op jit(solution)/shard_map/ppermute | solution.py:307
  263.6 32.7 %collective-permute-start.22 = (bf16[2,320,512]{2,1,0:T(8,128)(2,1)}, bf16[2,320,512]{2,1,0:T(8,128)(2,1)S(1)}, u32[]{:S(2)}, u32[]{:S(2)}) collective-permute-start(bf16[2,320,512]{2,1,0:T(8,128)(2,1)} %get-tuple-element.22), channel_id=1, source_target_pairs={{0,2},{1,3},{2,0},{3,1},{4,6},{5,7},{6,4},{7,5},{8,10},{9,11},{10,... | collective-permute-start | bytes 1966088 | tf_op jit(solution)/shard_map/ppermute | solution.py:307
  267.4 31.1 %collective-permute-start.23 = (bf16[2,320,512]{2,1,0:T(8,128)(2,1)}, bf16[2,320,512]{2,1,0:T(8,128)(2,1)S(1)}, u32[]{:S(2)}, u32[]{:S(2)}) collective-permute-start(bf16[2,320,512]{2,1,0:T(8,128)(2,1)} %get-tuple-element.23), channel_id=1, source_target_pairs={{0,3},{1,2},{2,1},{3,0},{4,7},{5,6},{6,5},{7,4},{8,11},{9,10},{10,... | collective-permute-start | bytes 1966088 | tf_op jit(solution)/shard_map/ppermute | solution.py:307
  285.9 12.6 %copy-start.14 = (bf16[2,320,512]{2,1,0:T(8,128)(2,1)}, bf16[2,320,512]{2,1,0:T(8,128)(2,1)S(1)}, u32[]{:S(2)}) copy-start(bf16[2,320,512]{2,1,0:T(8,128)(2,1)S(1)} %collective-permute-done.21.refs_0_) | copy-start | bytes 1966084
  296.3 2.2 copy-start.15
  298.5 0.8 copy-start.16
  299.3 13.4 %copy-start.22 = (bf16[640,128]{1,0:T(8,128)(2,1)S(1)}, bf16[640,128]{1,0:T(8,128)(2,1)}, u32[]{:S(2)}) copy-start(bf16[640,128]{1,0:T(8,128)(2,1)} %copy-done.21) | copy-start | bytes 491524
  299.4 13.4 %copy-start.24 = (bf16[640,128]{1,0:T(8,128)(2,1)S(1)}, bf16[640,128]{1,0:T(8,128)(2,1)}, u32[]{:S(2)}) copy-start(bf16[640,128]{1,0:T(8,128)(2,1)} %copy-done.23) | copy-start | bytes 491524
  304.3 28.4 %all-to-all-start.6 = ((bf16[16,40,512]{2,1,0:T(8,128)(2,1)}), bf16[16,40,512]{2,1,0:T(8,128)(2,1)S(1)}, u32[]{:S(2)}, u32[]{:S(2)}) async-start(bf16[16,40,512]{2,1,0:T(8,128)(2,1)} %bitcast.100), calls=%async_computation.7 | async-start | bytes 1310720 | tf_op jit(solution)/shard_map/all_to_all | solution.py:315
Sparse Core Ops, SparseCore 0:
  10.4 89.0 all-gather.3
  213.7 40.2 reduce-scatter.2
  256.5 50.1 reduce-scatter.4

commit v3 on v2

--- a/solution.py
+++ b/solution.py
@@ -55,36 +55,49 @@
     return pltpu.VMEM(shape, dtype)
 
 
-def project(parts, w_in, at, offset, base=None, grads=None):
-    _, rows, width = parts[0].shape
+def project(groups, w_in, at, base=None, grads=None):
+    rows = groups[0][2][0].shape[1]
     cols = w_in.shape[2]
     units = cols // 2
     last = base is not None
+    arrays = [x for _, js, parts in groups for j in js for x in grouped(parts)[j]]
+    widths = [parts[0].shape[2] for _, _, parts in groups]
+    count = sum(len(js) for _, js, _ in groups)
 
     def body(at_ref, w_ref, *refs):
-        x_refs, refs = refs[:PER], refs[PER:]
+        x_refs, refs = refs[: len(arrays)], refs[len(arrays) :]
         if last:
-            (base_ref, grad_ref), refs = refs[:2], refs[2:]
-            out_h, out_a, w_buf, x_buf, total, h_buf, a_buf, grad_buf, sems = refs
+            (base_ref, grad_ref, out_h, out_a), refs = refs[:4], refs[4:]
         else:
-            out, w_buf, x_buf, total, sems = refs
-        for j in range(N):
-            start(w_ref.at[at_ref[0] ^ j, pl.ds(offset, 2 * width)], w_buf.at[j], sems.at[j])
-            place(grouped(x_refs)[j], x_buf.at[j], sems.at[N + j])
+            (out,), refs = refs[:1], refs[1:]
+        w_bufs, x_bufs, refs = refs[: len(groups)], refs[len(groups) : 2 * len(groups)], refs[2 * len(groups) :]
+        total, sems = refs[0], refs[-1]
+        array, sem = 0, 0
+        for g, (offset, js, parts) in enumerate(groups):
+            for i, j in enumerate(js):
+                size = len(grouped(parts)[j])
+                start(w_ref.at[at_ref[0] ^ j, pl.ds(offset, 2 * widths[g])], w_bufs[g].at[i], sems.at[sem])
+                place(x_refs[array : array + size], x_bufs[g].at[i], sems.at[count + sem])
+                array, sem = array + size, sem + 1
         if last:
-            first = start(base_ref, total, sems.at[2 * N])
-            second = start(grad_ref, grad_buf, sems.at[2 * N + 1])
+            h_buf, a_buf, grad_buf = refs[1:4]
+            first = start(base_ref, total, sems.at[2 * count])
+            second = start(grad_ref, grad_buf, sems.at[2 * count + 1])
             first.wait()
         else:
             total[...] = jnp.zeros_like(total)
-
-        def step(j, carry):
-            pltpu.make_async_copy(w_ref.at[0, pl.ds(offset, 2 * width)], w_buf.at[j], sems.at[j]).wait()
-            pltpu.make_async_copy(x_refs[0], x_buf.at[j], sems.at[N + j]).wait()
-            total[...] += dot(x_buf[j, 0], w_buf[j, :width], NN) + dot(x_buf[j, 1], w_buf[j, width:], NN)
-            return carry
-
-        lax.fori_loop(0, N, step, 0)
+        sem = 0
+        for g, (offset, js, _) in enumerate(groups):
+            width, w_buf, x_buf, lo = widths[g], w_bufs[g], x_bufs[g], sem
+
+            def step(i, carry, width=width, w_buf=w_buf, x_buf=x_buf, lo=lo, offset=offset):
+                pltpu.make_async_copy(w_ref.at[0, pl.ds(offset, 2 * width)], w_buf.at[i], sems.at[lo + i]).wait()
+                pltpu.make_async_copy(x_buf.at[i], x_buf.at[i], sems.at[count + lo + i]).wait()
+                total[...] += dot(x_buf[i, 0], w_buf[i, :width], NN) + dot(x_buf[i, 1], w_buf[i, width:], NN)
+                return carry
+
+            lax.fori_loop(0, len(js), step, 0)
+            sem += len(js)
         if last:
             second.wait()
             grad = sum(grad_buf[j].astype(F32) for j in range(N))
@@ -99,12 +112,13 @@
         for copy in stores:
             copy.wait()
 
-    scratch = [vmem(N, 2 * width, cols), vmem(N, 2, rows, width), vmem(rows, cols, dtype=F32)]
+    scratch = [vmem(len(js), 2 * w, cols) for (_, js, _), w in zip(groups, widths)]
+    scratch += [vmem(len(js), 2, rows, w) for (_, js, _), w in zip(groups, widths)] + [vmem(rows, cols, dtype=F32)]
     if not last:
-        return call(body, jax.ShapeDtypeStruct((rows, cols), F32), scratch, [at, w_in] + parts, 2 * N)
+        return call(body, jax.ShapeDtypeStruct((rows, cols), F32), scratch, [at, w_in] + arrays, 2 * count)
     outs = (jax.ShapeDtypeStruct((rows, units), BF16), jax.ShapeDtypeStruct((rows, cols), BF16))
     scratch += [vmem(rows, units), vmem(rows, cols), vmem(N, rows, units)]
-    return call(body, outs, scratch, [at, w_in] + parts + [base, grads], 2 * N + 2)
+    return call(body, outs, scratch, [at, w_in] + arrays + [base, grads], 2 * count + 2)
 
 
 def fetch(chunks, x_refs, x_bufs, sems, base):
@@ -158,7 +172,7 @@
     return call(body, out, scratch, [at, w_down] + flat(chunks), 1 + N + count * N)
 
 
-def weight_grad(chunks, acts, at, lo_col):
+def weight_grad(chunks, acts, at, lo_col, relative=False):
     rows, cols = acts.shape
     units = cols // 2
     width = sum(2 * parts[0].shape[2] for parts in chunks)
@@ -175,11 +189,16 @@
             for h in range(count):
                 w = x_bufs[h].shape[3]
                 arrived(x_refs, x_bufs, sems, 1 + N, h, j)
-                for c in range(2):
+
+                def piece(c, carry, h=h, lo=lo, w=w):
                     grads = dot(x_bufs[h][j, c], a_buf[:, lo_col : lo_col + units], TN)
-                    out_buf[j, lo : lo + w] = grads.astype(BF16)
-                    lo += w
-            start(out_buf.at[j], out.at[at_ref[0] ^ j], sems.at[1 + j])
+                    out_buf[j, pl.ds(pl.multiple_of(lo + c * w, 128), w)] = grads.astype(BF16)
+                    return carry
+
+                lax.fori_loop(0, 2, piece, 0)
+                lo += 2 * w
+            to = at_ref[0] ^ j ^ at_ref[1] if relative else at_ref[0] ^ j
+            start(out_buf.at[j], out.at[to], sems.at[1 + j])
             return carry
 
         lax.fori_loop(0, N, step, 0)
@@ -208,9 +227,15 @@
             for h in range(count):
                 w = x_bufs[h].shape[3]
                 arrived(x_refs, x_bufs, sems, 1, h, j)
-                for c in range(2):
-                    out_buf[:, lo : lo + w] += dot(h_buf[at_ref[0] ^ j], x_bufs[h][j, c], TN)
-                    lo += w
+
+                def piece(c, carry, h=h, lo=lo, w=w):
+                    out_buf[:, pl.ds(pl.multiple_of(lo + c * w, 128), w)] += dot(
+                        h_buf[at_ref[0] ^ j], x_bufs[h][j, c], TN
+                    )
+                    return carry
+
+                lax.fori_loop(0, 2, piece, 0)
+                lo += 2 * w
             return carry
 
         lax.fori_loop(0, N, step, 0)
@@ -233,9 +258,13 @@
 
         def step(j, carry):
             pltpu.make_async_copy(w_ref.at[0, pl.ds(offset, 2 * width)], w_buf.at[j], sems.at[1 + j]).wait()
-            for c in range(2):
-                out_buf[j, c] = dot(a_buf[...], w_buf[j, c * width : (c + 1) * width], NT).astype(BF16)
-            return carry
+
+            def piece(c, carry):
+                w = w_buf[j, pl.ds(pl.multiple_of(c * width, 128), width)]
+                out_buf[j, c] = dot(a_buf[...], w, NT).astype(BF16)
+                return carry
+
+            return lax.fori_loop(0, 2, piece, carry)
 
         lax.fori_loop(0, N - 1, step, 0)
         stores = [start(out_buf.at[j], outs[j], sems.at[j]) for j in range(N - 1)]
@@ -261,11 +290,15 @@
         copies += [start(r_refs[j], r_buf.at[j], sems.at[3 + j]) for j in range(N - 1)]
         for copy in copies:
             copy.wait()
-        for c in range(2):
-            total = dot(a_buf[...], w_buf[c * width : (c + 1) * width], NT)
+
+        def piece(c, carry):
+            total = dot(a_buf[...], w_buf[pl.ds(pl.multiple_of(c * width, 128), width)], NT)
             for j in range(N - 1):
                 total = total + r_buf[j, c].astype(F32)
-            t_buf[c * rows : (c + 1) * rows] = total.astype(BF16)
+            t_buf[pl.ds(pl.multiple_of(c * rows, rows), rows)] = total.astype(BF16)
+            return carry
+
+        lax.fori_loop(0, 2, piece, 0)
 
         def step(i, carry):
             block = pl.ds(i * (rows // 2), rows // 2)
@@ -301,10 +334,10 @@
     small = width // 2 - piece
     pieces, starts = (small, piece), (0, 2 * small)
     z_pieces, z_starts = (piece, small), (0, 2 * piece)
-    at = lax.axis_index("ffn").astype(jnp.int32)[None]
-
-    def swap(x, by):
-        return lax.ppermute(x, "ffn", [(i, i ^ by) for i in range(N)])
+    at = jnp.stack([lax.axis_index("ffn"), lax.axis_index("dp")]).astype(jnp.int32)
+
+    def swap(x, by, axis="ffn"):
+        return lax.ppermute(x, axis, [(i, i ^ by) for i in range(N)])
 
     def flip(x):
         return lax.ppermute(
@@ -366,8 +399,8 @@
 
     partial = hidden_grads((z_0, z_1), down_weight[0], at)
     grads = lax.all_to_all(partial, "dp", split_axis=0, concat_axis=0, tiled=True)
-    base = project(x_0, w_in, at, starts[0])
-    hidden, acts = project(x_1, w_in, at, starts[1], base, grads)
+    base = project([(starts[0], (0, 1, 2, 3), x_0), (starts[1], (0, 1, 3), x_1)], w_in, at)
+    hidden, acts = project([(starts[1], (2,), x_1)], w_in, at, base, grads)
 
     part_gate = weight_grad((x_0, x_1), acts, at, 0)
     grad_gate = lax.psum_scatter(part_gate, "dp", scatter_dimension=0, tiled=True)
@@ -378,8 +411,12 @@
     received = []
     for h in range(2):
         received.append([swap(leads[h][j - 1], j) for j in range(1, N)])
-    part_up = weight_grad((x_0, x_1), acts, at, gate_weight.shape[2])
-    grad_up = lax.psum_scatter(part_up, "dp", scatter_dimension=0, tiled=True).astype(F32)
+    direct = weight_grad((x_0,), acts, at, gate_weight.shape[2], relative=True)
+    scattered = weight_grad((x_1,), acts, at, gate_weight.shape[2])
+    scattered = lax.psum_scatter(scattered, "dp", scatter_dimension=0, tiled=True)
+    direct = [direct[0]] + [swap(direct[j], j, "dp") for j in range(1, N)]
+    direct = sum(d.astype(F32) for d in direct)
+    grad_up = jnp.concatenate([direct[None], scattered.astype(F32)], axis=1)
 
     grad_tokens = []
     hidden_all = lax.all_gather(hidden, "dp", axis=0, tiled=False)

time: 341 us -> 374 us (1.097)
  Pallas kernels: 52.3 us -> 66.2 us
  waiting for transfers between devices: 126 us -> 137 us
  blocking collectives: 15.9 us -> 25.8 us
  starting transfers between devices: 101 us -> 93.7 us
    ppermute x22 -> x25, waiting for transfers between devices: 67.5 us -> 82.7 us  [swap(): return lax.ppermute(x, axis, [(i, i ^ by) for i in range(N)])]
    pallas_call x10 -> x11, Pallas kernels: 52.3 us -> 66.2 us  [call(): pl.pallas_call(body, out_shape=outs, in_specs=[SMEM] + [ANY] * (len(args)...]
    all_gather x1, blocking collectives: 15.9 us -> 25.8 us  [per_device(): hidden_all = lax.all_gather(hidden, 'dp', axis=0, tiled=False)]
    ppermute x22 -> x25, starting transfers between devices: 60.9 us -> 51.3 us  [swap(): return lax.ppermute(x, axis, [(i, i ^ by) for i in range(N)])]
    all_to_all x6, waiting for transfers between devices: 58.8 us -> 54.3 us  [exchange(): return lax.all_to_all(x, 'expert', split_axis=0, concat_axis=0, tiled=True)]
  transfers between devices with their start and end apart: 34 -> 37, of which waited for: 16 -> 16; matrix products, arithmetic and copies ran while one was open for 6% -> 7% of each run, Pallas kernels for 12% -> 15%
where the time goes in v3:
time: 374 us; the launch traced here: 372 us
  waiting for transfers between devices  137 us (37%)
  starting transfers between devices  93.7 us (25%)
  Pallas kernels  66.2 us (18%)
  blocking collectives  25.8 us (7%)
  between operations  14.4 us (4%)
  other arithmetic  13.1 us (4%)
  local copies, waits for them, and re-layouts  11.3 us (3%)
  matrix products  10.9 us (3%)
    ppermute x25, waiting for transfers between devices, swap(): return lax.ppermute(x, axis, [(i, i ^ by) for i in range(N)])  82.7 us
    pallas_call x11, Pallas kernels, call(): pl.pallas_call(body, out_shape=outs, in_specs=[SMEM] + [ANY] * (len(args)...  66.2 us
    all_to_all x6, waiting for transfers between devices, exchange(): return lax.all_to_all(x, 'expert', split_axis=0, concat_axis=0, tiled=True)  54.3 us
    ppermute x25, starting transfers between devices, swap(): return lax.ppermute(x, axis, [(i, i ^ by) for i in range(N)])  51.3 us
    all_to_all x6, starting transfers between devices, exchange(): return lax.all_to_all(x, 'expert', split_axis=0, concat_axis=0, tiled=True)  37 us
    all_gather x1, blocking collectives, per_device(): hidden_all = lax.all_gather(hidden, 'dp', axis=0, tiled=False)  25.8 us
    dot_general x10, matrix products, dot(): lax.dot_general(a, b, (contract, ((), ())), preferred_element_type=F32)  10.9 us
  transfers between devices with their start and end apart: 37, of which 16 were waited for; matrix products, arithmetic and copies ran while one was open for 7% of the time, Pallas kernels for 15%

profile of v3, /device:TPU:1, one launch (start us, length us, event | category | flops | bytes accessed | tf_op | source)
XLA Modules:
  0.0 372.4 jit_solution(10879600337582649991)
XLA Ops:
  7.2 2.8 pad_maximum_fusion
  13.2 1.1 convolution_convert_fusion.1
  14.3 10.0 %all-to-all-start.1 = ((bf16[16,40,384]{2,1,0:T(8,128)(2,1)}), bf16[16,40,384]{2,1,0:T(8,128)(2,1)S(1)}, u32[]{:S(2)}, u32[]{:S(2)}) async-start(bf16[16,40,384]{2,1,0:T(8,128)(2,1)} %bitcast.13), calls=%async_computation.1 | async-start | bytes 983040 | tf_op jit(solution)/shard_map/all_to_all | solution.py:348
  25.4 1.1 fusion.8
  26.5 14.3 %all-to-all-done.1 = bf16[16,40,384]{2,1,0:T(8,128)(2,1)S(1)} async-done(((bf16[16,40,384]{2,1,0:T(8,128)(2,1)}), bf16[16,40,384]{2,1,0:T(8,128)(2,1)S(1)}, u32[]{:S(2)}, u32[]{:S(2)}) %all-to-all-start.1) | async-done | bytes 491552 | tf_op jit(solution)/shard_map/all_to_all | solution.py:348
  40.8 3.5 all-to-all-start.3
  44.3 1.2 fusion.7
  45.5 14.8 %all-to-all-done.3 = bf16[16,40,384]{2,1,0:T(8,128)(2,1)S(1)} async-done(((bf16[16,40,384]{2,1,0:T(8,128)(2,1)}), bf16[16,40,384]{2,1,0:T(8,128)(2,1)S(1)}, u32[]{:S(2)}, u32[]{:S(2)}) %all-to-all-start.3) | async-done | bytes 491552 | tf_op jit(solution)/shard_map/all_to_all | solution.py:348
  60.3 3.5 all-to-all-start.2
  63.8 1.2 convolution_convert_fusion
  65.0 18.3 %all-to-all-done.2 = bf16[16,40,512]{2,1,0:T(8,128)(2,1)S(1)} async-done(((bf16[16,40,512]{2,1,0:T(8,128)(2,1)}), bf16[16,40,512]{2,1,0:T(8,128)(2,1)S(1)}, u32[]{:S(2)}, u32[]{:S(2)}) %all-to-all-start.2) | async-done | bytes 655392 | tf_op jit(solution)/shard_map/all_to_all | solution.py:348
  83.2 4.2 %all-to-all-start = ((bf16[16,40,512]{2,1,0:T(8,128)(2,1)}), bf16[16,40,512]{2,1,0:T(8,128)(2,1)}, u32[]{:S(2)}, u32[]{:S(2)}) async-start(bf16[16,40,512]{2,1,0:T(8,128)(2,1)} %bitcast.8), calls=%async_computation | async-start | bytes 1310720 | tf_op jit(solution)/shard_map/all_to_all | solution.py:348
  88.7 23.2 %collective-permute-start.6 = (bf16[2,320,384]{2,1,0:T(8,128)(2,1)S(1)}, bf16[2,320,384]{2,1,0:T(8,128)(2,1)S(1)}, u32[]{:S(2)}, u32[]{:S(2)}) collective-permute-start(bf16[2,320,384]{2,1,0:T(8,128)(2,1)S(1)} %bitcast.109), channel_id=1, source_target_pairs={{0,3},{1,2},{2,1},{3,0},{4,7},{5,6},{6,5},{7,4},{8,11},{9,10},{10,... | collective-permute-start | bytes 1474568 | tf_op jit(solution)/shard_map/ppermute | solution.py:340
  112.0 1.5 fusion.10
  113.6 1.4 collective-permute-start.14
  114.9 1.6 fusion.6
  116.5 2.1 collective-permute-start.12
  118.6 1.8 fusion.5
  120.4 13.9 %collective-permute-done.16.refs_9_ = bf16[2,320,384]{2,1,0:T(8,128)(2,1)S(1)} collective-permute-done((bf16[2,320,384]{2,1,0:T(8,128)(2,1)}, bf16[2,320,384]{2,1,0:T(8,128)(2,1)S(1)}, u32[]{:S(2)}, u32[]{:S(2)}) %collective-permute-start.16) | collective-permute-done | bytes 491552 | tf_op jit(solution)/shard_map/ppermute | solution.py:340
  134.3 1.2 collective-permute-done.14.refs_6_
  135.5 2.3 collective-permute-start.2
  137.8 1.0 slice_bitcast_fusion.9
  138.7 9.6 %collective-permute-done.12.refs_4_ = bf16[2,320,512]{2,1,0:T(8,128)(2,1)S(1)} collective-permute-done((bf16[2,320,512]{2,1,0:T(8,128)(2,1)}, bf16[2,320,512]{2,1,0:T(8,128)(2,1)S(1)}, u32[]{:S(2)}, u32[]{:S(2)}) %collective-permute-start.12) | collective-permute-done | bytes 655392 | tf_op jit(solution)/shard_map/ppermute | solution.py:340
  149.2 1.5 collective-permute-done.10.refs_1_
  150.7 3.3 collective-permute-start.15
  154.0 8.4 %collective-permute-done.2.refs_7_.refs_9_.refs_4_ = bf16[2,320,512]{2,1,0:T(8,128)(2,1)S(1)} collective-permute-done((bf16[2,320,512]{2,1,0:T(8,128)(2,1)S(1)}, bf16[2,320,512]{2,1,0:T(8,128)(2,1)S(1)}, u32[]{:S(2)}, u32[]{:S(2)}) %collective-permute-start.2) | collective-permute-done | bytes 655392 | tf_op jit(solution)/shard_map/ppermute | solution.py:340
  162.4 2.8 collective-permute-start.11
  166.6 1.1 collective-permute-done.15.refs_7_
  167.8 9.7 %collective-permute-done.13.refs_3_ = bf16[320,512]{1,0:T(8,128)(2,1)} collective-permute-done((bf16[320,512]{1,0:T(8,128)(2,1)S(1)}, bf16[320,512]{1,0:T(8,128)(2,1)}, u32[]{:S(2)}, u32[]{:S(2)}) %collective-permute-start.13) | collective-permute-done | bytes 327712 | tf_op jit(solution)/shard_map/ppermute | solution.py:340
  177.5 7.0 %shard_map.103 = bf16[4,320,256]{2,1,0:T(8,128)(2,1)} custom-call(s32[2]{0:T(128)} %pad_add_fusion.at_ref, bf16[256,1792]{1,0:T(8,128)(2,1)} %bitcast.120, bf16[2,320,512]{2,1,0:T(8,128)(2,1)} %bitcast.25.refs_0_, bf16[2,320,512]{2,1,0:T(8,128)(2,1)} %copy-done.7, bf16[320,512]{1,0:T(8,128)(2,1)} %collective-permute-done.11.refs_2_, ...), custom_call_target="tpu_custom_call" | custom-call | tf_op jit(solution)/shard_map/pallas_call | solution.py:24
  184.5 3.9 %all-to-all-start.4 = ((bf16[4,320,256]{2,1,0:T(8,128)(2,1)}), bf16[4,320,256]{2,1,0:T(8,128)(2,1)S(1)}, u32[]{:S(2)}, u32[]{:S(2)}) async-start(bf16[4,320,256]{2,1,0:T(8,128)(2,1)} %shard_map.103), calls=%async_computation.4 | async-start | bytes 1310720 | tf_op jit(solution)/shard_map/all_to_all | solution.py:401
  188.4 2.6 collective-permute-start.1
  191.3 12.7 %collective-permute-done.5.refs_2_ = bf16[320,384]{1,0:T(8,128)(2,1)S(1)} collective-permute-done((bf16[320,384]{1,0:T(8,128)(2,1)S(1)}, bf16[320,384]{1,0:T(8,128)(2,1)S(1)}, u32[]{:S(2)}, u32[]{:S(2)}) %collective-permute-start.5) | collective-permute-done | bytes 245792 | tf_op jit(solution)/shard_map/ppermute | solution.py:340
  204.7 6.4 %shard_map.102.refs_2_ = f32[320,512]{1,0:T(8,128)} custom-call(s32[2]{0:T(128)} %pad_add_fusion.at_ref, bf16[4,1792,512]{2,1,0:T(8,128)(2,1)} %bitcast.98, bf16[2,320,384]{2,1,0:T(8,128)(2,1)} %bitcast.111, bf16[2,320,384]{2,1,0:T(8,128)(2,1)} %copy-done.3, bf16[320,384]{1,0:T(8,128)(2,1)} %copy-done.11, bf16[320,384]{1,0:T(8,128)(2,1)} %collective-permute-done.7.refs_3_, ...), custom_call_target="tpu_custom_call" | custom-call | tf_op jit(solution)/shard_map/pallas_call | solution.py:24
  212.7 3.8 %shard_map.104 = (bf16[320,256]{1,0:T(8,128)(2,1)}, bf16[320,512]{1,0:T(8,128)(2,1)}) custom-call(s32[2]{0:T(128)} %pad_add_fusion.at_ref, bf16[4,1792,512]{2,1,0:T(8,128)(2,1)} %bitcast.99, bf16[320,512]{1,0:T(8,128)(2,1)} %copy-done.9, bf16[320,512]{1,0:T(8,128)(2,1)} %collective-permute-done.3.refs_1_.refs_8_.refs_3_, f32[320,512]{1,0:T(8,128)} %shard_map.102.refs_2_, ...), custom_call_target="tpu_custom_call" | custom-call | tf_op jit(solution)/shard_map/pallas_call | solution.py:24
  216.5 8.0 %shard_map.108 = bf16[4,1792,256]{2,1,0:T(8,128)(2,1)} custom-call(s32[2]{0:T(128)} %pad_add_fusion.at_ref, bf16[320,512]{1,0:T(8,128)(2,1)} %get-tuple-element.17.a_ref, bf16[2,320,384]{2,1,0:T(8,128)(2,1)} %bitcast.112, bf16[2,320,384]{2,1,0:T(8,128)(2,1)} %copy-done.3, bf16[320,384]{1,0:T(8,128)(2,1)} %copy-done.11, ...), custom_call_target="tpu_custom_call" | custom-call | tf_op jit(solution)/shard_map/pallas_call | solution.py:24
  224.7 5.5 %shard_map.111 = bf16[4,1024,256]{2,1,0:T(8,128)(2,1)} custom-call(s32[2]{0:T(128)} %pad_add_fusion.at_ref, bf16[320,512]{1,0:T(8,128)(2,1)} %get-tuple-element.17.a_ref, bf16[2,320,512]{2,1,0:T(8,128)(2,1)} %bitcast.108, bf16[2,320,512]{2,1,0:T(8,128)(2,1)} %copy-done.1, bf16[320,512]{1,0:T(8,128)(2,1)} %copy-done.9, ...), custom_call_target="tpu_custom_call" | custom-call | tf_op jit(solution)/shard_map/pallas_call | solution.py:24
  230.2 5.2 %shard_map.105 = (bf16[2,320,384]{2,1,0:T(8,128)(2,1)}, bf16[2,320,384]{2,1,0:T(8,128)(2,1)}, bf16[2,320,384]{2,1,0:T(8,128)(2,1)}) custom-call(s32[2]{0:T(128)} %pad_add_fusion.at_ref, bf16[320,512]{1,0:T(8,128)(2,1)} %get-tuple-element.17.a_ref, bf16[4,1792,512]{2,1,0:T(8,128)(2,1)} %bitcast.100), custom_call_target="tpu_custom_call" | custom-call | tf_op jit(solution)/shard_map/pallas_call | solution.py:24
  235.4 1.0 collective-permute-start.18
  236.4 3.0 collective-permute-start.19
  239.4 1.1 fusion.4.order_ref
  240.6 6.9 %collective-permute-done.18.refs_0_ = bf16[2,320,384]{2,1,0:T(8,128)(2,1)S(1)} collective-permute-done((bf16[2,320,384]{2,1,0:T(8,128)(2,1)}, bf16[2,320,384]{2,1,0:T(8,128)(2,1)S(1)}, u32[]{:S(2)}, u32[]{:S(2)}) %collective-permute-start.18) | collective-permute-done | bytes 491552 | tf_op jit(solution)/shard_map/ppermute | solution.py:340
  247.5 13.2 %collective-permute-done.19.refs_1_ = bf16[2,320,384]{2,1,0:T(8,128)(2,1)S(1)} collective-permute-done((bf16[2,320,384]{2,1,0:T(8,128)(2,1)}, bf16[2,320,384]{2,1,0:T(8,128)(2,1)S(1)}, u32[]{:S(2)}, u32[]{:S(2)}) %collective-permute-start.19) | collective-permute-done | bytes 491552 | tf_op jit(solution)/shard_map/ppermute | solution.py:340
  260.7 2.2 collective-permute-done.20.refs_2_
  263.7 5.3 %shard_map.106 = bf16[640,384]{1,0:T(8,128)(2,1)} custom-call(s32[2]{0:T(128)} %pad_add_fusion.at_ref, bf16[320,512]{1,0:T(8,128)(2,1)} %get-tuple-element.17.a_ref, bf16[4,1792,512]{2,1,0:T(8,128)(2,1)} %bitcast.101, bf16[640,640]{1,0:T(8,128)(2,1)} %fusion.4.order_ref, bf16[2,320,384]{2,1,0:T(8,128)(2,1)} %copy-done.17, bf16[2,320,384]{2,1,0:T(8,128)(2,1)} %copy-done.18, ...), custom_call_target="tpu_custom_call" | custom-call | tf_op jit(solution)/shard_map/pallas_call | solution.py:24
  269.0 5.5 %all-to-all-start.5 = ((bf16[16,40,384]{2,1,0:T(8,128)(2,1)}), bf16[16,40,384]{2,1,0:T(8,128)(2,1)S(1)}, u32[]{:S(2)}, u32[]{:S(2)}) async-start(bf16[16,40,384]{2,1,0:T(8,128)(2,1)} %bitcast.116), calls=%async_computation.5 | async-start | bytes 983040 | tf_op jit(solution)/shard_map/all_to_all | solution.py:348
  274.5 5.5 %shard_map.107 = (bf16[2,320,512]{2,1,0:T(8,128)(2,1)}, bf16[2,320,512]{2,1,0:T(8,128)(2,1)}, bf16[2,320,512]{2,1,0:T(8,128)(2,1)}) custom-call(s32[2]{0:T(128)} %pad_add_fusion.at_ref, bf16[320,512]{1,0:T(8,128)(2,1)} %get-tuple-element.17.a_ref, bf16[4,1792,512]{2,1,0:T(8,128)(2,1)} %bitcast.102), custom_call_target="tpu_custom_call" | custom-call | tf_op jit(solution)/shard_map/pallas_call | solution.py:24
  280.1 1.1 collective-permute-start.22
  281.3 2.7 collective-permute-start.23
  284.0 5.1 %shard_map.110 = bf16[4,768,256]{2,1,0:T(8,128)(2,1)} custom-call(s32[2]{0:T(128)} %pad_add_fusion.at_ref, bf16[320,512]{1,0:T(8,128)(2,1)} %get-tuple-element.17.a_ref, bf16[2,320,384]{2,1,0:T(8,128)(2,1)} %bitcast.113, bf16[2,320,384]{2,1,0:T(8,128)(2,1)} %copy-done.3, bf16[320,384]{1,0:T(8,128)(2,1)} %copy-done.11, ...), custom_call_target="tpu_custom_call" | custom-call | tf_op jit(solution)/shard_map/pallas_call | solution.py:24
  289.1 2.3 slice_bitcast_fusion.2
  291.3 1.1 collective-permute-start.24
  292.4 1.8 collective-permute-start.26
  294.2 2.3 collective-permute-done.21.refs_0_
  296.5 2.5 collective-permute-start.25
  299.1 25.8 %all-gather.1 = bf16[1280,256]{1,0:T(8,128)(2,1)} all-gather(bf16[320,256]{1,0:T(8,128)(2,1)S(1)} %copy-done.26), channel_id=3, replica_groups=mesh['dp'=4,'expert'=16,'ffn'=4] {'dp'}, dimensions={0}, use_global_device_ids=true | all-gather | bytes 819200 | tf_op jit(solution)/shard_map/all_gather | solution.py:422
  324.9 2.5 convert_element_type.116
  328.5 5.8 %shard_map.109 = bf16[640,512]{1,0:T(8,128)(2,1)} custom-call(s32[2]{0:T(128)} %pad_add_fusion.at_ref, bf16[320,512]{1,0:T(8,128)(2,1)} %get-tuple-element.17.a_ref, bf16[4,1792,512]{2,1,0:T(8,128)(2,1)} %bitcast.103, bf16[640,640]{1,0:T(8,128)(2,1)} %fusion.4.order_ref, bf16[2,320,512]{2,1,0:T(8,128)(2,1)} %copy-done.14, bf16[2,320,512]{2,1,0:T(8,128)(2,1)} %copy-done.15, ...), custom_call_target="tpu_custom_call" | custom-call | tf_op jit(solution)/shard_map/pallas_call | solution.py:24
  334.3 10.4 %all-to-all-start.6 = ((bf16[16,40,512]{2,1,0:T(8,128)(2,1)}), bf16[16,40,512]{2,1,0:T(8,128)(2,1)S(1)}, u32[]{:S(2)}, u32[]{:S(2)}) async-start(bf16[16,40,512]{2,1,0:T(8,128)(2,1)} %bitcast.114), calls=%async_computation.7 | async-start | bytes 1310720 | tf_op jit(solution)/shard_map/all_to_all | solution.py:348
  344.7 1.4 fusion.17
  346.6 1.1 convert_element_type.123
  347.7 1.3 pad_maximum_fusion.1
  349.1 8.5 %shard_map.112 = f32[256,1792]{1,0:T(8,128)} custom-call(s32[2]{0:T(128)} %pad_add_fusion.at_ref, bf16[4,320,256]{2,1,0:T(8,128)(2,1)} %bitcast.115, bf16[2,320,512]{2,1,0:T(8,128)(2,1)} %bitcast.25.refs_0_, bf16[2,320,512]{2,1,0:T(8,128)(2,1)} %copy-done.7, bf16[320,512]{1,0:T(8,128)(2,1)} %collective-permute-done.11.refs_2_, ...), custom_call_target="tpu_custom_call" | custom-call | tf_op jit(solution)/shard_map/pallas_call | solution.py:24
  357.6 7.0 %all-to-all-done.6 = bf16[16,40,512]{2,1,0:T(8,128)(2,1)S(1)} async-done(((bf16[16,40,512]{2,1,0:T(8,128)(2,1)}), bf16[16,40,512]{2,1,0:T(8,128)(2,1)S(1)}, u32[]{:S(2)}, u32[]{:S(2)}) %all-to-all-start.6) | async-done | bytes 655392 | tf_op jit(solution)/shard_map/all_to_all | solution.py:348
  (141 shorter events, 14.3 us)
Async XLA Ops:
  7.2 196.8 %all-gather.4.cloned.1.call-start = ((), (), s32[]{:S(2)}) async-start(), calls=%async_computation.11 | async-start | bytes 9175040 | tf_op jit(solution)/shard_map/all_gather | solution.py:364
  10.0 2.2 copy-start.28
  10.0 2.9 copy-start.20
  10.8 13.5 %copy-start.29 = (bf16[128,1792]{1,0:T(8,128)(2,1)S(1)}, bf16[128,1792]{1,0:T(8,128)(2,1)}, u32[]{:S(2)}) copy-start(bf16[128,1792]{1,0:T(8,128)(2,1)} %param.8) | copy-start | bytes 1376260
  12.3 12.7 %collective-permute-start.8 = (f32[128,4]{0,1:T(4,128)S(1)}, f32[128,4]{0,1:T(4,128)S(1)}, u32[]{:S(2)}, u32[]{:S(2)}) collective-permute-start(f32[128,4]{0,1:T(4,128)S(1)} %pad_maximum_fusion.7), channel_id=1, source_target_pairs={{0,0},{1,64},{2,128},{3,192},{64,1},{65,65},{66,129},{67,193},{128... | collective-permute-start | bytes 6152 | tf_op jit(solution)/shard_map/ppermute | solution.py:343
  13.2 50.6 %copy-start.21 = (bf16[640,128]{1,0:T(8,128)(2,1)}, bf16[640,128]{1,0:T(8,128)(2,1)S(1)}, u32[]{:S(2)}) copy-start(bf16[640,128]{1,0:T(8,128)(2,1)S(1)} %get-tuple-element.57) | copy-start | bytes 491524
  13.2 50.6 %copy-start.23 = (bf16[640,128]{1,0:T(8,128)(2,1)}, bf16[640,128]{1,0:T(8,128)(2,1)S(1)}, u32[]{:S(2)}) copy-start(bf16[640,128]{1,0:T(8,128)(2,1)S(1)} %get-tuple-element.58) | copy-start | bytes 491524
  14.3 26.5 %all-to-all-start.1 = ((bf16[16,40,384]{2,1,0:T(8,128)(2,1)}), bf16[16,40,384]{2,1,0:T(8,128)(2,1)S(1)}, u32[]{:S(2)}, u32[]{:S(2)}) async-start(bf16[16,40,384]{2,1,0:T(8,128)(2,1)} %bitcast.13), calls=%async_computation.1 | async-start | bytes 983040 | tf_op jit(solution)/shard_map/all_to_all | solution.py:348
  24.3 1.1 collective-permute-start.9
  40.8 19.4 %all-to-all-start.3 = ((bf16[16,40,384]{2,1,0:T(8,128)(2,1)}), bf16[16,40,384]{2,1,0:T(8,128)(2,1)S(1)}, u32[]{:S(2)}, u32[]{:S(2)}) async-start(bf16[16,40,384]{2,1,0:T(8,128)(2,1)} %bitcast.28), calls=%async_computation.3 | async-start | bytes 983040 | tf_op jit(solution)/shard_map/all_to_all | solution.py:348
  60.3 23.0 %all-to-all-start.2 = ((bf16[16,40,512]{2,1,0:T(8,128)(2,1)}), bf16[16,40,512]{2,1,0:T(8,128)(2,1)S(1)}, u32[]{:S(2)}, u32[]{:S(2)}) async-start(bf16[16,40,512]{2,1,0:T(8,128)(2,1)} %bitcast.23), calls=%async_computation.2 | async-start | bytes 1310720 | tf_op jit(solution)/shard_map/all_to_all | solution.py:348
  83.2 35.3 %all-to-all-start = ((bf16[16,40,512]{2,1,0:T(8,128)(2,1)}), bf16[16,40,512]{2,1,0:T(8,128)(2,1)}, u32[]{:S(2)}, u32[]{:S(2)}) async-start(bf16[16,40,512]{2,1,0:T(8,128)(2,1)} %bitcast.8), calls=%async_computation | async-start | bytes 1310720 | tf_op jit(solution)/shard_map/all_to_all | solution.py:348
  88.7 27.8 %copy-start.5 = (bf16[640,384]{1,0:T(8,128)(2,1)}, bf16[640,384]{1,0:T(8,128)(2,1)S(1)}, u32[]{:S(2)}) copy-start(bf16[640,384]{1,0:T(8,128)(2,1)S(1)} %fusion.9) | copy-start | bytes 1474564
  88.7 61.9 %collective-permute-start.6 = (bf16[2,320,384]{2,1,0:T(8,128)(2,1)S(1)}, bf16[2,320,384]{2,1,0:T(8,128)(2,1)S(1)}, u32[]{:S(2)}, u32[]{:S(2)}) collective-permute-start(bf16[2,320,384]{2,1,0:T(8,128)(2,1)S(1)} %bitcast.109), channel_id=1, source_target_pairs={{0,3},{1,2},{2,1},{3,0},{4,7},{5,6},{6,5},{7,4},{8,11},{9,10},{10,... | collective-permute-start | bytes 1474568 | tf_op jit(solution)/shard_map/ppermute | solution.py:340
  112.0 79.0 %collective-permute-start.4 = (bf16[2,320,384]{2,1,0:T(8,128)(2,1)S(1)}, bf16[2,320,384]{2,1,0:T(8,128)(2,1)S(1)}, u32[]{:S(2)}, u32[]{:S(2)}) collective-permute-start(bf16[2,320,384]{2,1,0:T(8,128)(2,1)S(1)} %bitcast.110), channel_id=1, source_target_pairs={{0,1},{1,0},{2,3},{3,2},{4,5},{5,4},{6,7},{7,6},{8,9},{9,8},{10,11... | collective-permute-start | bytes 1474568 | tf_op jit(solution)/shard_map/ppermute | solution.py:340
  113.5 20.8 %collective-permute-start.16 = (bf16[2,320,384]{2,1,0:T(8,128)(2,1)}, bf16[2,320,384]{2,1,0:T(8,128)(2,1)S(1)}, u32[]{:S(2)}, u32[]{:S(2)}) collective-permute-start(bf16[2,320,384]{2,1,0:T(8,128)(2,1)} %bitcast.30.refs_5_), channel_id=1, source_target_pairs={{0,3},{1,2},{2,1},{3,0},{4,7},{5,6},{6,5},{7,4},{8,11},{9,10},{10,... | collective-permute-start | bytes 1474568 | tf_op jit(solution)/shard_map/ppermute | solution.py:340
  113.6 21.9 %collective-permute-start.14 = (bf16[2,320,384]{2,1,0:T(8,128)(2,1)}, bf16[2,320,384]{2,1,0:T(8,128)(2,1)}, u32[]{:S(2)}, u32[]{:S(2)}) collective-permute-start(bf16[2,320,384]{2,1,0:T(8,128)(2,1)} %bitcast.30.refs_5_), channel_id=1, source_target_pairs={{0,1},{1,0},{2,3},{3,2},{4,5},{5,4},{6,7},{7,6},{8,9},{9,8},{10,11... | collective-permute-start | bytes 1474568 | tf_op jit(solution)/shard_map/ppermute | solution.py:340
  116.5 31.8 %collective-permute-start.12 = (bf16[2,320,512]{2,1,0:T(8,128)(2,1)}, bf16[2,320,512]{2,1,0:T(8,128)(2,1)S(1)}, u32[]{:S(2)}, u32[]{:S(2)}) collective-permute-start(bf16[2,320,512]{2,1,0:T(8,128)(2,1)} %bitcast.25.refs_0_), channel_id=1, source_target_pairs={{0,3},{1,2},{2,1},{3,0},{4,7},{5,6},{6,5},{7,4},{8,11},{9,10},{10,... | collective-permute-start | bytes 1966088 | tf_op jit(solution)/shard_map/ppermute | solution.py:340
  120.4 46.3 %copy-start.4 = (bf16[640,512]{1,0:T(8,128)(2,1)}, bf16[640,512]{1,0:T(8,128)(2,1)S(1)}, u32[]{:S(2)}) copy-start(bf16[640,512]{1,0:T(8,128)(2,1)S(1)} %fusion.5) | copy-start | bytes 1966084
  134.3 1.2 copy-start.8
  134.3 16.4 %collective-permute-start.10 = (bf16[2,320,512]{2,1,0:T(8,128)(2,1)}, bf16[2,320,512]{2,1,0:T(8,128)(2,1)S(1)}, u32[]{:S(2)}, u32[]{:S(2)}) collective-permute-start(bf16[2,320,512]{2,1,0:T(8,128)(2,1)} %bitcast.25.refs_0_), channel_id=1, source_target_pairs={{0,1},{1,0},{2,3},{3,2},{4,5},{5,4},{6,7},{7,6},{8,9},{9,8},{10,11... | collective-permute-start | bytes 1966088 | tf_op jit(solution)/shard_map/ppermute | solution.py:340
  135.5 26.9 %collective-permute-start.2 = (bf16[2,320,512]{2,1,0:T(8,128)(2,1)S(1)}, bf16[2,320,512]{2,1,0:T(8,128)(2,1)S(1)}, u32[]{:S(2)}, u32[]{:S(2)}) collective-permute-start(bf16[2,320,512]{2,1,0:T(8,128)(2,1)S(1)} %bitcast.104), channel_id=1, source_target_pairs={{0,3},{1,2},{2,1},{3,0},{4,7},{5,6},{6,5},{7,4},{8,11},{9,10},{10,... | collective-permute-start | bytes 1966088 | tf_op jit(solution)/shard_map/ppermute | solution.py:340
  148.3 0.8 copy-start.6
  148.3 14.1 %collective-permute-start.17 = (bf16[320,384]{1,0:T(8,128)(2,1)S(1)}, bf16[320,384]{1,0:T(8,128)(2,1)S(1)}, u32[]{:S(2)}, u32[]{:S(2)}) collective-permute-start(bf16[320,384]{1,0:T(8,128)(2,1)S(1)} %slice_bitcast_fusion.8), channel_id=1, source_target_pairs={{0,1},{1,0},{2,3},{3,2},{4,5},{5,4},{6,7},{7,6},{8,9},{9,8},{10,11... | collective-permute-start | bytes 737288 | tf_op jit(solution)/shard_map/ppermute | solution.py:340
  150.6 17.1 %copy-start.7 = (bf16[2,320,512]{2,1,0:T(8,128)(2,1)}, bf16[2,320,512]{2,1,0:T(8,128)(2,1)S(1)}, u32[]{:S(2)}) copy-start(bf16[2,320,512]{2,1,0:T(8,128)(2,1)S(1)} %collective-permute-done.10.refs_1_) | copy-start | bytes 1966084
  150.7 37.7 %collective-permute-start = (bf16[2,320,512]{2,1,0:T(8,128)(2,1)S(1)}, bf16[2,320,512]{2,1,0:T(8,128)(2,1)S(1)}, u32[]{:S(2)}, u32[]{:S(2)}) collective-permute-start(bf16[2,320,512]{2,1,0:T(8,128)(2,1)S(1)} %bitcast.105), channel_id=1, source_target_pairs={{0,1},{1,0},{2,3},{3,2},{4,5},{5,4},{6,7},{7,6},{8,9},{9,8},{10,11... | collective-permute-start | bytes 1966088 | tf_op jit(solution)/shard_map/ppermute | solution.py:340
  150.7 33.8 %copy-start.2 = (bf16[2,320,384]{2,1,0:T(8,128)(2,1)}, bf16[2,320,384]{2,1,0:T(8,128)(2,1)S(1)}, u32[]{:S(2)}) copy-start(bf16[2,320,384]{2,1,0:T(8,128)(2,1)S(1)} %collective-permute-done.6.refs_4_) | copy-start | bytes 1474564
  150.7 17.1 %collective-permute-start.15 = (bf16[320,384]{1,0:T(8,128)(2,1)S(1)}, bf16[320,384]{1,0:T(8,128)(2,1)S(1)}, u32[]{:S(2)}, u32[]{:S(2)}) collective-permute-start(bf16[320,384]{1,0:T(8,128)(2,1)S(1)} %slice_bitcast_fusion.9), channel_id=1, source_target_pairs={{0,3},{1,2},{2,1},{3,0},{4,7},{5,6},{6,5},{7,4},{8,11},{9,10},{10,... | collective-permute-start | bytes 737288 | tf_op jit(solution)/shard_map/ppermute | solution.py:340
  162.4 22.1 %copy-start = (bf16[2,320,512]{2,1,0:T(8,128)(2,1)}, bf16[2,320,512]{2,1,0:T(8,128)(2,1)S(1)}, u32[]{:S(2)}) copy-start(bf16[2,320,512]{2,1,0:T(8,128)(2,1)S(1)} %collective-permute-done.2.refs_7_.refs_9_.refs_4_) | copy-start | bytes 1966084
  162.4 15.1 %collective-permute-start.13 = (bf16[320,512]{1,0:T(8,128)(2,1)S(1)}, bf16[320,512]{1,0:T(8,128)(2,1)}, u32[]{:S(2)}, u32[]{:S(2)}) collective-permute-start(bf16[320,512]{1,0:T(8,128)(2,1)S(1)} %slice_bitcast_fusion.4), channel_id=1, source_target_pairs={{0,1},{1,0},{2,3},{3,2},{4,5},{5,4},{6,7},{7,6},{8,9},{9,8},{10,11... | collective-permute-start | bytes 983048 | tf_op jit(solution)/shard_map/ppermute | solution.py:340
  162.4 5.4 %copy-start.12 = (bf16[320,384]{1,0:T(8,128)(2,1)}, bf16[320,384]{1,0:T(8,128)(2,1)S(1)}, u32[]{:S(2)}) copy-start(bf16[320,384]{1,0:T(8,128)(2,1)S(1)} %collective-permute-done.17.refs_8_) | copy-start | bytes 737284
  162.4 15.1 %collective-permute-start.11 = (bf16[320,512]{1,0:T(8,128)(2,1)S(1)}, bf16[320,512]{1,0:T(8,128)(2,1)}, u32[]{:S(2)}, u32[]{:S(2)}) collective-permute-start(bf16[320,512]{1,0:T(8,128)(2,1)S(1)} %slice_bitcast_fusion.5), channel_id=1, source_target_pairs={{0,3},{1,2},{2,1},{3,0},{4,7},{5,6},{6,5},{7,4},{8,11},{9,10},{10,... | collective-permute-start | bytes 983048 | tf_op jit(solution)/shard_map/ppermute | solution.py:340
  167.8 9.7 %copy-start.13 = (bf16[320,384]{1,0:T(8,128)(2,1)}, bf16[320,384]{1,0:T(8,128)(2,1)S(1)}, u32[]{:S(2)}) copy-start(bf16[320,384]{1,0:T(8,128)(2,1)S(1)} %collective-permute-done.15.refs_7_) | copy-start | bytes 737284
  167.8 23.6 %collective-permute-start.7 = (bf16[320,384]{1,0:T(8,128)(2,1)}, bf16[320,384]{1,0:T(8,128)(2,1)}, u32[]{:S(2)}, u32[]{:S(2)}) collective-permute-start(bf16[320,384]{1,0:T(8,128)(2,1)} %slice_bitcast_fusion.10), channel_id=1, source_target_pairs={{0,1},{1,0},{2,3},{3,2},{4,5},{5,4},{6,7},{7,6},{8,9},{9,8},{10,11... | collective-permute-start | bytes 737288 | tf_op jit(solution)/shard_map/ppermute | solution.py:340
  177.5 33.7 %collective-permute-start.3 = (bf16[320,512]{1,0:T(8,128)(2,1)}, bf16[320,512]{1,0:T(8,128)(2,1)}, u32[]{:S(2)}, u32[]{:S(2)}) collective-permute-start(bf16[320,512]{1,0:T(8,128)(2,1)} %slice_bitcast_fusion.6), channel_id=1, source_target_pairs={{0,1},{1,0},{2,3},{3,2},{4,5},{5,4},{6,7},{7,6},{8,9},{9,8},{10,11... | collective-permute-start | bytes 983048 | tf_op jit(solution)/shard_map/ppermute | solution.py:340
  184.5 26.7 %all-to-all-start.4 = ((bf16[4,320,256]{2,1,0:T(8,128)(2,1)}), bf16[4,320,256]{2,1,0:T(8,128)(2,1)S(1)}, u32[]{:S(2)}, u32[]{:S(2)}) async-start(bf16[4,320,256]{2,1,0:T(8,128)(2,1)} %shard_map.103), calls=%async_computation.4 | async-start | bytes 1310720 | tf_op jit(solution)/shard_map/all_to_all | solution.py:401
  188.4 136.5 %reduce-scatter.3.cloned.1.call-start = ((), (), s32[]{:S(2)}) async-start(), calls=%async_computation.9 | async-start | bytes 4587520 | tf_op jit(solution)/shard_map/reduce_scatter | solution.py:406
  188.4 15.6 %copy-start.1 = (bf16[2,320,512]{2,1,0:T(8,128)(2,1)}, bf16[2,320,512]{2,1,0:T(8,128)(2,1)S(1)}, u32[]{:S(2)}) copy-start(bf16[2,320,512]{2,1,0:T(8,128)(2,1)S(1)} %collective-permute-done.refs_6_.refs_1_) | copy-start | bytes 1966084
  188.4 22.7 %collective-permute-start.1 = (bf16[320,512]{1,0:T(8,128)(2,1)S(1)}, bf16[320,512]{1,0:T(8,128)(2,1)S(1)}, u32[]{:S(2)}, u32[]{:S(2)}) collective-permute-start(bf16[320,512]{1,0:T(8,128)(2,1)S(1)} %slice_bitcast_fusion.7), channel_id=1, source_target_pairs={{0,3},{1,2},{2,1},{3,0},{4,7},{5,6},{6,5},{7,4},{8,11},{9,10},{10,... | collective-permute-start | bytes 983048 | tf_op jit(solution)/shard_map/ppermute | solution.py:340
  191.0 13.0 %copy-start.3 = (bf16[2,320,384]{2,1,0:T(8,128)(2,1)}, bf16[2,320,384]{2,1,0:T(8,128)(2,1)S(1)}, u32[]{:S(2)}) copy-start(bf16[2,320,384]{2,1,0:T(8,128)(2,1)S(1)} %collective-permute-done.4.refs_1_) | copy-start | bytes 1474564
  191.0 13.0 %collective-permute-start.5 = (bf16[320,384]{1,0:T(8,128)(2,1)S(1)}, bf16[320,384]{1,0:T(8,128)(2,1)S(1)}, u32[]{:S(2)}, u32[]{:S(2)}) collective-permute-start(bf16[320,384]{1,0:T(8,128)(2,1)S(1)} %slice_bitcast_fusion.11), channel_id=1, source_target_pairs={{0,3},{1,2},{2,1},{3,0},{4,7},{5,6},{6,5},{7,4},{8,11},{9,10},{10,... | collective-permute-start | bytes 737288 | tf_op jit(solution)/shard_map/ppermute | solution.py:340
  211.9 0.8 copy-start.10
  224.6 122.0 %reduce-scatter.5.cloned.1.call-start = ((), (), s32[]{:S(2)}) async-start(), calls=%async_computation.10 | async-start | bytes 2621440 | tf_op jit(solution)/shard_map/reduce_scatter | solution.py:416
  235.4 12.1 %collective-permute-start.18 = (bf16[2,320,384]{2,1,0:T(8,128)(2,1)}, bf16[2,320,384]{2,1,0:T(8,128)(2,1)S(1)}, u32[]{:S(2)}, u32[]{:S(2)}) collective-permute-start(bf16[2,320,384]{2,1,0:T(8,128)(2,1)} %get-tuple-element.18), channel_id=1, source_target_pairs={{0,1},{1,0},{2,3},{3,2},{4,5},{5,4},{6,7},{7,6},{8,9},{9,8},{10,11... | collective-permute-start | bytes 1474568 | tf_op jit(solution)/shard_map/ppermute | solution.py:340
  236.4 24.3 %collective-permute-start.19 = (bf16[2,320,384]{2,1,0:T(8,128)(2,1)}, bf16[2,320,384]{2,1,0:T(8,128)(2,1)S(1)}, u32[]{:S(2)}, u32[]{:S(2)}) collective-permute-start(bf16[2,320,384]{2,1,0:T(8,128)(2,1)} %get-tuple-element.19), channel_id=1, source_target_pairs={{0,2},{1,3},{2,0},{3,1},{4,6},{5,7},{6,4},{7,5},{8,10},{9,11},{10,... | collective-permute-start | bytes 1474568 | tf_op jit(solution)/shard_map/ppermute | solution.py:340
  239.4 23.4 %collective-permute-start.20 = (bf16[2,320,384]{2,1,0:T(8,128)(2,1)}, bf16[2,320,384]{2,1,0:T(8,128)(2,1)S(1)}, u32[]{:S(2)}, u32[]{:S(2)}) collective-permute-start(bf16[2,320,384]{2,1,0:T(8,128)(2,1)} %get-tuple-element.20), channel_id=1, source_target_pairs={{0,3},{1,2},{2,1},{3,0},{4,7},{5,6},{6,5},{7,4},{8,11},{9,10},{10,... | collective-permute-start | bytes 1474568 | tf_op jit(solution)/shard_map/ppermute | solution.py:340
  247.5 15.4 %copy-start.17 = (bf16[2,320,384]{2,1,0:T(8,128)(2,1)}, bf16[2,320,384]{2,1,0:T(8,128)(2,1)S(1)}, u32[]{:S(2)}) copy-start(bf16[2,320,384]{2,1,0:T(8,128)(2,1)S(1)} %collective-permute-done.18.refs_0_) | copy-start | bytes 1474564
  260.7 2.2 copy-start.18
  262.9 0.8 copy-start.19
  269.0 65.3 %all-to-all-start.5 = ((bf16[16,40,384]{2,1,0:T(8,128)(2,1)}), bf16[16,40,384]{2,1,0:T(8,128)(2,1)S(1)}, u32[]{:S(2)}, u32[]{:S(2)}) async-start(bf16[16,40,384]{2,1,0:T(8,128)(2,1)} %bitcast.116), calls=%async_computation.5 | async-start | bytes 983040 | tf_op jit(solution)/shard_map/all_to_all | solution.py:348
  280.0 16.5 %collective-permute-start.21 = (bf16[2,320,512]{2,1,0:T(8,128)(2,1)}, bf16[2,320,512]{2,1,0:T(8,128)(2,1)S(1)}, u32[]{:S(2)}, u32[]{:S(2)}) collective-permute-start(bf16[2,320,512]{2,1,0:T(8,128)(2,1)} %get-tuple-element.21), channel_id=1, source_target_pairs={{0,1},{1,0},{2,3},{3,2},{4,5},{5,4},{6,7},{7,6},{8,9},{9,8},{10,11... | collective-permute-start | bytes 1966088 | tf_op jit(solution)/shard_map/ppermute | solution.py:340
  280.1 47.3 %collective-permute-start.22 = (bf16[2,320,512]{2,1,0:T(8,128)(2,1)}, bf16[2,320,512]{2,1,0:T(8,128)(2,1)S(1)}, u32[]{:S(2)}, u32[]{:S(2)}) collective-permute-start(bf16[2,320,512]{2,1,0:T(8,128)(2,1)} %get-tuple-element.22), channel_id=1, source_target_pairs={{0,2},{1,3},{2,0},{3,1},{4,6},{5,7},{6,4},{7,5},{8,10},{9,11},{10,... | collective-permute-start | bytes 1966088 | tf_op jit(solution)/shard_map/ppermute | solution.py:340
  281.3 46.2 %collective-permute-start.23 = (bf16[2,320,512]{2,1,0:T(8,128)(2,1)}, bf16[2,320,512]{2,1,0:T(8,128)(2,1)S(1)}, u32[]{:S(2)}, u32[]{:S(2)}) collective-permute-start(bf16[2,320,512]{2,1,0:T(8,128)(2,1)} %get-tuple-element.23), channel_id=1, source_target_pairs={{0,3},{1,2},{2,1},{3,0},{4,7},{5,6},{6,5},{7,4},{8,11},{9,10},{10,... | collective-permute-start | bytes 1966088 | tf_op jit(solution)/shard_map/ppermute | solution.py:340
  289.1 10.0 %copy-start.26 = (bf16[320,256]{1,0:T(8,128)(2,1)S(1)}, bf16[320,256]{1,0:T(8,128)(2,1)}, u32[]{:S(2)}) copy-start(bf16[320,256]{1,0:T(8,128)(2,1)} %get-tuple-element.24) | copy-start | bytes 491524
  291.3 53.3 %collective-permute-start.24 = (bf16[768,256]{1,0:T(8,128)(2,1)}, bf16[768,256]{1,0:T(8,128)(2,1)S(1)}, u32[]{:S(2)}, u32[]{:S(2)}) collective-permute-start(bf16[768,256]{1,0:T(8,128)(2,1)} %get-tuple-element.32), channel_id=1, source_target_pairs={{0,64},{64,0},{128,192},{192,128},{1,65},{65,1},{129,193},{193,129... | collective-permute-start | bytes 1179656 | tf_op jit(solution)/shard_map/ppermute | solution.py:340
  292.4 52.3 %collective-permute-start.26 = (bf16[768,256]{1,0:T(8,128)(2,1)}, bf16[768,256]{1,0:T(8,128)(2,1)}, u32[]{:S(2)}, u32[]{:S(2)}) collective-permute-start(bf16[768,256]{1,0:T(8,128)(2,1)} %get-tuple-element.33), channel_id=1, source_target_pairs={{0,192},{64,128},{128,64},{192,0},{1,193},{65,129},{129,65},{193,1... | collective-permute-start | bytes 1179656 | tf_op jit(solution)/shard_map/ppermute | solution.py:340
  296.5 30.9 %copy-start.14 = (bf16[2,320,512]{2,1,0:T(8,128)(2,1)}, bf16[2,320,512]{2,1,0:T(8,128)(2,1)S(1)}, u32[]{:S(2)}) copy-start(bf16[2,320,512]{2,1,0:T(8,128)(2,1)S(1)} %collective-permute-done.21.refs_0_) | copy-start | bytes 1966084
  296.5 48.2 %collective-permute-start.25 = (bf16[768,256]{1,0:T(8,128)(2,1)S(1)}, bf16[768,256]{1,0:T(8,128)(2,1)}, u32[]{:S(2)}, u32[]{:S(2)}) collective-permute-start(bf16[768,256]{1,0:T(8,128)(2,1)S(1)} %get-tuple-element.34), channel_id=1, source_target_pairs={{0,128},{64,192},{128,0},{192,64},{1,129},{65,193},{129,1},{193,65... | collective-permute-start | bytes 1179656 | tf_op jit(solution)/shard_map/ppermute | solution.py:340
  327.4 0.8 copy-start.15
  327.4 1.0 copy-start.16
  334.3 11.9 %copy-start.22 = (bf16[640,128]{1,0:T(8,128)(2,1)S(1)}, bf16[640,128]{1,0:T(8,128)(2,1)}, u32[]{:S(2)}) copy-start(bf16[640,128]{1,0:T(8,128)(2,1)} %copy-done.21) | copy-start | bytes 491524
  334.3 11.9 %copy-start.24 = (bf16[640,128]{1,0:T(8,128)(2,1)S(1)}, bf16[640,128]{1,0:T(8,128)(2,1)}, u32[]{:S(2)}) copy-start(bf16[640,128]{1,0:T(8,128)(2,1)} %copy-done.23) | copy-start | bytes 491524
  334.3 30.3 %all-to-all-start.6 = ((bf16[16,40,512]{2,1,0:T(8,128)(2,1)}), bf16[16,40,512]{2,1,0:T(8,128)(2,1)S(1)}, u32[]{:S(2)}, u32[]{:S(2)}) async-start(bf16[16,40,512]{2,1,0:T(8,128)(2,1)} %bitcast.114), calls=%async_computation.7 | async-start | bytes 1310720 | tf_op jit(solution)/shard_map/all_to_all | solution.py:348
  349.1 15.6 %copy-start.25 = (bf16[640,128]{1,0:T(8,128)(2,1)S(1)}, bf16[640,128]{1,0:T(8,128)(2,1)}, u32[]{:S(2)}) copy-start(bf16[640,128]{1,0:T(8,128)(2,1)} %copy-done.23) | copy-start | bytes 491524
  (3 other events, 2.1 us)
Sparse Core Ops, SparseCore 0:
  10.4 96.1 all-gather.3
  224.7 42.4 reduce-scatter.2
  269.8 35.4 reduce-scatter.4

commit v4 on v3

--- a/solution.py
+++ b/solution.py
@@ -34,6 +34,10 @@
     copy = pltpu.make_async_copy(src, dst, sem)
     copy.start()
     return copy
+
+
+def slice_of(at, size):
+    return pl.ds(at if isinstance(at, int) else pl.multiple_of(at, 128), size)
 
 
 def place(part, buf, sem):
@@ -172,7 +176,7 @@
     return call(body, out, scratch, [at, w_down] + flat(chunks), 1 + N + count * N)
 
 
-def weight_grad(chunks, acts, at, lo_col, relative=False):
+def weight_grad(chunks, acts, at, lo_col, relative=False, unroll=False):
     rows, cols = acts.shape
     units = cols // 2
     width = sum(2 * parts[0].shape[2] for parts in chunks)
@@ -192,10 +196,14 @@
 
                 def piece(c, carry, h=h, lo=lo, w=w):
                     grads = dot(x_bufs[h][j, c], a_buf[:, lo_col : lo_col + units], TN)
-                    out_buf[j, pl.ds(pl.multiple_of(lo + c * w, 128), w)] = grads.astype(BF16)
+                    out_buf[j, slice_of(lo + c * w, w)] = grads.astype(BF16)
                     return carry
 
-                lax.fori_loop(0, 2, piece, 0)
+                if unroll:
+                    for c in range(2):
+                        piece(c, 0)
+                else:
+                    lax.fori_loop(0, 2, piece, 0)
                 lo += 2 * w
             to = at_ref[0] ^ j ^ at_ref[1] if relative else at_ref[0] ^ j
             start(out_buf.at[j], out.at[to], sems.at[1 + j])
@@ -402,7 +410,7 @@
     base = project([(starts[0], (0, 1, 2, 3), x_0), (starts[1], (0, 1, 3), x_1)], w_in, at)
     hidden, acts = project([(starts[1], (2,), x_1)], w_in, at, base, grads)
 
-    part_gate = weight_grad((x_0, x_1), acts, at, 0)
+    part_gate = weight_grad((x_0, x_1), acts, at, 0, unroll=True)
     grad_gate = lax.psum_scatter(part_gate, "dp", scatter_dimension=0, tiled=True)
     grad_gate = grad_gate.astype(F32)
     leads = []
@@ -419,17 +427,19 @@
     grad_up = jnp.concatenate([direct[None], scattered.astype(F32)], axis=1)
 
     grad_tokens = []
+    hidden, grad_gate = lax.optimization_barrier((hidden, grad_gate))
     hidden_all = lax.all_gather(hidden, "dp", axis=0, tiled=False)
-    received[1], hidden_all, grad_gate = lax.optimization_barrier((received[1], hidden_all, grad_gate))
+    grad_down = down_grad((z_0, z_1), hidden_all, at)[None]
     for h in range(2):
         total = input_totals(acts, w_in, at, starts[h], received[h], order_back)
         back = exchange(total.reshape(groups, 2 * capacity, -1))
         back = back.reshape(2 * slots, -1)
+        if h == 1:
+            x_place, grad_down = lax.optimization_barrier((x_place, grad_down))
         back = dot(x_place, back, TN).astype(BF16)
         grad_tokens += [back[:rows], back[rows:]]
     grad_tokens = jnp.concatenate(grad_tokens, axis=1)
 
-    grad_down = down_grad((z_0, z_1), hidden_all, at)[None]
     return grad_tokens, grad_gate, grad_up, grad_down
 
 

time: 374 us -> 356 us (0.952)
  waiting for transfers between devices: 137 us -> 113 us
  starting transfers between devices: 93.7 us -> 114 us
  blocking collectives: 25.8 us -> 12.5 us
    ppermute x25, starting transfers between devices: 51.3 us -> 73.2 us  [swap(): return lax.ppermute(x, axis, [(i, i ^ by) for i in range(N)])]
    ppermute x25, waiting for transfers between devices: 82.7 us -> 66.1 us  [swap(): return lax.ppermute(x, axis, [(i, i ^ by) for i in range(N)])]
    all_gather x1, blocking collectives: 25.8 us -> 12.5 us  [per_device(): hidden_all = lax.all_gather(hidden, 'dp', axis=0, tiled=False)]
    all_to_all x6, waiting for transfers between devices: 54.3 us -> 47.3 us  [exchange(): return lax.all_to_all(x, 'expert', split_axis=0, concat_axis=0, tiled=True)]
  transfers between devices with their start and end apart: 37 -> 37, of which waited for: 16 -> 14; matrix products, arithmetic and copies ran while one was open for 7% -> 7% of each run, Pallas kernels for 15% -> 16%
where the time goes in v4:
time: 356 us; the launch traced here: 354 us
  starting transfers between devices  114 us (32%)
  waiting for transfers between devices  113 us (32%)
  Pallas kernels  64.5 us (18%)
  between operations  14.4 us (4%)
  other arithmetic  13.1 us (4%)
  blocking collectives  12.5 us (4%)
  matrix products  10.9 us (3%)
  local copies, waits for them, and re-layouts  10.6 us (3%)
    ppermute x25, starting transfers between devices, swap(): return lax.ppermute(x, axis, [(i, i ^ by) for i in range(N)])  73.2 us
    ppermute x25, waiting for transfers between devices, swap(): return lax.ppermute(x, axis, [(i, i ^ by) for i in range(N)])  66.1 us
    pallas_call x11, Pallas kernels, call(): pl.pallas_call(body, out_shape=outs, in_specs=[SMEM] + [ANY] * (len(args)...  64.5 us
    all_to_all x6, waiting for transfers between devices, exchange(): return lax.all_to_all(x, 'expert', split_axis=0, concat_axis=0, tiled=True)  47.3 us
    all_to_all x6, starting transfers between devices, exchange(): return lax.all_to_all(x, 'expert', split_axis=0, concat_axis=0, tiled=True)  35.9 us
    all_gather x1, blocking collectives, per_device(): hidden_all = lax.all_gather(hidden, 'dp', axis=0, tiled=False)  12.5 us
    dot_general x10, matrix products, dot(): lax.dot_general(a, b, (contract, ((), ())), preferred_element_type=F32)  10.9 us
  transfers between devices with their start and end apart: 37, of which 14 were waited for; matrix products, arithmetic and copies ran while one was open for 7% of the time, Pallas kernels for 16%

profile of v4, /device:TPU:1, one launch (start us, length us, event | category | flops | bytes accessed | tf_op | source)
XLA Modules:
  0.0 353.5 jit_solution(12711089286398113650)
XLA Ops:
  7.2 2.8 pad_maximum_fusion
  13.2 1.1 convolution_convert_fusion.1
  14.3 10.0 %all-to-all-start.1 = ((bf16[16,40,384]{2,1,0:T(8,128)(2,1)}), bf16[16,40,384]{2,1,0:T(8,128)(2,1)S(1)}, u32[]{:S(2)}, u32[]{:S(2)}) async-start(bf16[16,40,384]{2,1,0:T(8,128)(2,1)} %bitcast.13), calls=%async_computation.1 | async-start | bytes 983040 | tf_op jit(solution)/shard_map/all_to_all | solution.py:356
  25.4 1.1 fusion.8
  26.6 14.3 %all-to-all-done.1 = bf16[16,40,384]{2,1,0:T(8,128)(2,1)S(1)} async-done(((bf16[16,40,384]{2,1,0:T(8,128)(2,1)}), bf16[16,40,384]{2,1,0:T(8,128)(2,1)S(1)}, u32[]{:S(2)}, u32[]{:S(2)}) %all-to-all-start.1) | async-done | bytes 491552 | tf_op jit(solution)/shard_map/all_to_all | solution.py:356
  40.8 3.5 all-to-all-start.3
  44.3 1.2 fusion.7
  45.5 14.8 %all-to-all-done.3 = bf16[16,40,384]{2,1,0:T(8,128)(2,1)S(1)} async-done(((bf16[16,40,384]{2,1,0:T(8,128)(2,1)}), bf16[16,40,384]{2,1,0:T(8,128)(2,1)S(1)}, u32[]{:S(2)}, u32[]{:S(2)}) %all-to-all-start.3) | async-done | bytes 491552 | tf_op jit(solution)/shard_map/all_to_all | solution.py:356
  60.3 3.5 all-to-all-start.2
  63.8 1.2 convolution_convert_fusion
  65.0 18.3 %all-to-all-done.2 = bf16[16,40,512]{2,1,0:T(8,128)(2,1)S(1)} async-done(((bf16[16,40,512]{2,1,0:T(8,128)(2,1)}), bf16[16,40,512]{2,1,0:T(8,128)(2,1)S(1)}, u32[]{:S(2)}, u32[]{:S(2)}) %all-to-all-start.2) | async-done | bytes 655392 | tf_op jit(solution)/shard_map/all_to_all | solution.py:356
  83.2 4.2 %all-to-all-start = ((bf16[16,40,512]{2,1,0:T(8,128)(2,1)}), bf16[16,40,512]{2,1,0:T(8,128)(2,1)}, u32[]{:S(2)}, u32[]{:S(2)}) async-start(bf16[16,40,512]{2,1,0:T(8,128)(2,1)} %bitcast.8), calls=%async_computation | async-start | bytes 1310720 | tf_op jit(solution)/shard_map/all_to_all | solution.py:356
  88.7 14.7 %collective-permute-start.4 = (bf16[2,320,384]{2,1,0:T(8,128)(2,1)S(1)}, bf16[2,320,384]{2,1,0:T(8,128)(2,1)S(1)}, u32[]{:S(2)}, u32[]{:S(2)}) collective-permute-start(bf16[2,320,384]{2,1,0:T(8,128)(2,1)S(1)} %bitcast.110), channel_id=1, source_target_pairs={{0,1},{1,0},{2,3},{3,2},{4,5},{5,4},{6,7},{7,6},{8,9},{9,8},{10,11... | collective-permute-start | bytes 1474568 | tf_op jit(solution)/shard_map/ppermute | solution.py:348
  103.4 8.6 %collective-permute-start.6 = (bf16[2,320,384]{2,1,0:T(8,128)(2,1)S(1)}, bf16[2,320,384]{2,1,0:T(8,128)(2,1)S(1)}, u32[]{:S(2)}, u32[]{:S(2)}) collective-permute-start(bf16[2,320,384]{2,1,0:T(8,128)(2,1)S(1)} %bitcast.111), channel_id=1, source_target_pairs={{0,3},{1,2},{2,1},{3,0},{4,7},{5,6},{6,5},{7,4},{8,11},{9,10},{10,... | collective-permute-start | bytes 1474568 | tf_op jit(solution)/shard_map/ppermute | solution.py:348
  112.1 1.5 fusion.10
  114.9 1.6 fusion.6
  116.6 1.8 fusion.5
  118.4 8.7 %collective-permute-done.14.refs_6_ = bf16[2,320,384]{2,1,0:T(8,128)(2,1)S(1)} collective-permute-done((bf16[2,320,384]{2,1,0:T(8,128)(2,1)}, bf16[2,320,384]{2,1,0:T(8,128)(2,1)S(1)}, u32[]{:S(2)}, u32[]{:S(2)}) %collective-permute-start.14) | collective-permute-done | bytes 491552 | tf_op jit(solution)/shard_map/ppermute | solution.py:348
  127.1 8.8 %collective-permute-start.12 = (bf16[2,320,512]{2,1,0:T(8,128)(2,1)}, bf16[2,320,512]{2,1,0:T(8,128)(2,1)S(1)}, u32[]{:S(2)}, u32[]{:S(2)}) collective-permute-start(bf16[2,320,512]{2,1,0:T(8,128)(2,1)} %bitcast.25.refs_0_), channel_id=1, source_target_pairs={{0,3},{1,2},{2,1},{3,0},{4,7},{5,6},{6,5},{7,4},{8,11},{9,10},{10,... | collective-permute-start | bytes 1966088 | tf_op jit(solution)/shard_map/ppermute | solution.py:348
  136.0 1.0 slice_bitcast_fusion.8
  137.0 4.1 %collective-permute-done.10.refs_1_ = bf16[2,320,512]{2,1,0:T(8,128)(2,1)S(1)} collective-permute-done((bf16[2,320,512]{2,1,0:T(8,128)(2,1)}, bf16[2,320,512]{2,1,0:T(8,128)(2,1)S(1)}, u32[]{:S(2)}, u32[]{:S(2)}) %collective-permute-start.10) | collective-permute-done | bytes 655392 | tf_op jit(solution)/shard_map/ppermute | solution.py:348
  141.0 8.8 %collective-permute-start.15 = (bf16[320,384]{1,0:T(8,128)(2,1)S(1)}, bf16[320,384]{1,0:T(8,128)(2,1)S(1)}, u32[]{:S(2)}, u32[]{:S(2)}) collective-permute-start(bf16[320,384]{1,0:T(8,128)(2,1)S(1)} %slice_bitcast_fusion.9), channel_id=1, source_target_pairs={{0,3},{1,2},{2,1},{3,0},{4,7},{5,6},{6,5},{7,4},{8,11},{9,10},{10,... | collective-permute-start | bytes 737288 | tf_op jit(solution)/shard_map/ppermute | solution.py:348
  149.8 1.1 collective-permute-done.12.refs_4_
  150.9 3.0 collective-permute-start.2
  154.8 9.0 %collective-permute-start.11 = (bf16[320,512]{1,0:T(8,128)(2,1)S(1)}, bf16[320,512]{1,0:T(8,128)(2,1)}, u32[]{:S(2)}, u32[]{:S(2)}) collective-permute-start(bf16[320,512]{1,0:T(8,128)(2,1)S(1)} %slice_bitcast_fusion.5), channel_id=1, source_target_pairs={{0,3},{1,2},{2,1},{3,0},{4,7},{5,6},{6,5},{7,4},{8,11},{9,10},{10,... | collective-permute-start | bytes 983048 | tf_op jit(solution)/shard_map/ppermute | solution.py:348
  163.8 0.8 slice_bitcast_fusion.11
  165.4 3.8 %collective-permute-start.5 = (bf16[320,384]{1,0:T(8,128)(2,1)}, bf16[320,384]{1,0:T(8,128)(2,1)}, u32[]{:S(2)}, u32[]{:S(2)}) collective-permute-start(bf16[320,384]{1,0:T(8,128)(2,1)} %slice_bitcast_fusion.11), channel_id=1, source_target_pairs={{0,3},{1,2},{2,1},{3,0},{4,7},{5,6},{6,5},{7,4},{8,11},{9,10},{10,... | collective-permute-start | bytes 737288 | tf_op jit(solution)/shard_map/ppermute | solution.py:348
  169.2 8.3 %collective-permute-done.11.refs_2_ = bf16[320,512]{1,0:T(8,128)(2,1)} collective-permute-done((bf16[320,512]{1,0:T(8,128)(2,1)S(1)}, bf16[320,512]{1,0:T(8,128)(2,1)}, u32[]{:S(2)}, u32[]{:S(2)}) %collective-permute-start.11) | collective-permute-done | bytes 327712 | tf_op jit(solution)/shard_map/ppermute | solution.py:348
  177.5 2.8 collective-permute-start.1
  180.3 7.0 %shard_map.103 = bf16[4,320,256]{2,1,0:T(8,128)(2,1)} custom-call(s32[2]{0:T(128)} %pad_add_fusion.at_ref, bf16[256,1792]{1,0:T(8,128)(2,1)} %bitcast.121, bf16[2,320,512]{2,1,0:T(8,128)(2,1)} %bitcast.25.refs_0_, bf16[2,320,512]{2,1,0:T(8,128)(2,1)} %copy-done.6, bf16[320,512]{1,0:T(8,128)(2,1)} %collective-permute-done.11.refs_2_, ...), custom_call_target="tpu_custom_call" | custom-call | tf_op jit(solution)/shard_map/pallas_call | solution.py:24
  187.3 3.5 all-to-all-start.4
  191.1 1.5 collective-permute-start.7
  192.6 12.7 %collective-permute-done.7.refs_3_ = bf16[320,384]{1,0:T(8,128)(2,1)S(1)} collective-permute-done((bf16[320,384]{1,0:T(8,128)(2,1)S(1)}, bf16[320,384]{1,0:T(8,128)(2,1)S(1)}, u32[]{:S(2)}, u32[]{:S(2)}) %collective-permute-start.7) | collective-permute-done | bytes 245792 | tf_op jit(solution)/shard_map/ppermute | solution.py:348
  206.0 6.4 %shard_map.102.refs_2_ = f32[320,512]{1,0:T(8,128)} custom-call(s32[2]{0:T(128)} %pad_add_fusion.at_ref, bf16[4,1792,512]{2,1,0:T(8,128)(2,1)} %bitcast.99, bf16[2,320,384]{2,1,0:T(8,128)(2,1)} %bitcast.112, bf16[2,320,384]{2,1,0:T(8,128)(2,1)} %copy-done.2, bf16[320,384]{1,0:T(8,128)(2,1)} %collective-permute-done.5.refs_2_, bf16[320,384]{1,0:T(8,128)(2,1)} %copy-done.11, ...), custom_call_target="tpu_custom_call" | custom-call | tf_op jit(solution)/shard_map/pallas_call | solution.py:24
  213.2 0.9 copy-done.10
  214.1 3.8 %shard_map.104 = (bf16[320,256]{1,0:T(8,128)(2,1)}, bf16[320,512]{1,0:T(8,128)(2,1)}) custom-call(s32[2]{0:T(128)} %pad_add_fusion.at_ref, bf16[4,1792,512]{2,1,0:T(8,128)(2,1)} %bitcast.100, bf16[320,512]{1,0:T(8,128)(2,1)} %collective-permute-done.1.refs_0_.refs_7_.refs_2_, bf16[320,512]{1,0:T(8,128)(2,1)} %copy-done.9, f32[320,512]{1,0:T(8,128)} %shard_map.102.refs_2_, ...), custom_call_target="tpu_custom_call" | custom-call | tf_op jit(solution)/shard_map/pallas_call | solution.py:24
  217.9 5.5 %shard_map.112 = bf16[4,1024,256]{2,1,0:T(8,128)(2,1)} custom-call(s32[2]{0:T(128)} %pad_add_fusion.at_ref, bf16[320,512]{1,0:T(8,128)(2,1)} %get-tuple-element.16.a_ref, bf16[2,320,512]{2,1,0:T(8,128)(2,1)} %bitcast.108, bf16[2,320,512]{2,1,0:T(8,128)(2,1)} %copy-done, bf16[320,512]{1,0:T(8,128)(2,1)} %collective-permute-done.1.refs_0_.refs_7_.refs_2_, ...), custom_call_target="tpu_custom_call" | custom-call | tf_op jit(solution)/shard_map/pallas_call | solution.py:24
  223.4 6.5 %shard_map.107 = bf16[4,1792,256]{2,1,0:T(8,128)(2,1)} custom-call(s32[2]{0:T(128)} %pad_add_fusion.at_ref, bf16[320,512]{1,0:T(8,128)(2,1)} %get-tuple-element.16.a_ref, bf16[2,320,384]{2,1,0:T(8,128)(2,1)} %bitcast.113, bf16[2,320,384]{2,1,0:T(8,128)(2,1)} %copy-done.2, bf16[320,384]{1,0:T(8,128)(2,1)} %collective-permute-done.5.refs_2_, ...), custom_call_target="tpu_custom_call" | custom-call | tf_op jit(solution)/shard_map/pallas_call | solution.py:24
  229.9 5.3 %shard_map.105 = (bf16[2,320,384]{2,1,0:T(8,128)(2,1)}, bf16[2,320,384]{2,1,0:T(8,128)(2,1)}, bf16[2,320,384]{2,1,0:T(8,128)(2,1)}) custom-call(s32[2]{0:T(128)} %pad_add_fusion.at_ref, bf16[320,512]{1,0:T(8,128)(2,1)} %get-tuple-element.16.a_ref, bf16[4,1792,512]{2,1,0:T(8,128)(2,1)} %bitcast.101), custom_call_target="tpu_custom_call" | custom-call | tf_op jit(solution)/shard_map/pallas_call | solution.py:24
  236.4 2.8 collective-permute-start.20
  239.2 5.5 %shard_map.109 = (bf16[2,320,512]{2,1,0:T(8,128)(2,1)}, bf16[2,320,512]{2,1,0:T(8,128)(2,1)}, bf16[2,320,512]{2,1,0:T(8,128)(2,1)}) custom-call(s32[2]{0:T(128)} %pad_add_fusion.at_ref, bf16[320,512]{1,0:T(8,128)(2,1)} %get-tuple-element.16.a_ref, bf16[4,1792,512]{2,1,0:T(8,128)(2,1)} %bitcast.102), custom_call_target="tpu_custom_call" | custom-call | tf_op jit(solution)/shard_map/pallas_call | solution.py:24
  244.8 1.1 fusion.4.order_ref
  245.9 1.4 collective-permute-done.18.refs_0_
  247.3 9.8 %collective-permute-done.19.refs_1_ = bf16[2,320,384]{2,1,0:T(8,128)(2,1)S(1)} collective-permute-done((bf16[2,320,384]{2,1,0:T(8,128)(2,1)}, bf16[2,320,384]{2,1,0:T(8,128)(2,1)S(1)}, u32[]{:S(2)}, u32[]{:S(2)}) %collective-permute-start.19) | collective-permute-done | bytes 491552 | tf_op jit(solution)/shard_map/ppermute | solution.py:348
  257.8 0.8 copy-done.23
  258.6 5.3 %shard_map.106 = bf16[640,384]{1,0:T(8,128)(2,1)} custom-call(s32[2]{0:T(128)} %pad_add_fusion.at_ref, bf16[320,512]{1,0:T(8,128)(2,1)} %get-tuple-element.16.a_ref, bf16[4,1792,512]{2,1,0:T(8,128)(2,1)} %bitcast.103, bf16[640,640]{1,0:T(8,128)(2,1)} %fusion.4.order_ref, bf16[2,320,384]{2,1,0:T(8,128)(2,1)} %copy-done.21, bf16[2,320,384]{2,1,0:T(8,128)(2,1)} %copy-done.22, ...), custom_call_target="tpu_custom_call" | custom-call | tf_op jit(solution)/shard_map/pallas_call | solution.py:24
  263.9 7.6 %all-to-all-start.5 = ((bf16[16,40,384]{2,1,0:T(8,128)(2,1)}), bf16[16,40,384]{2,1,0:T(8,128)(2,1)S(1)}, u32[]{:S(2)}, u32[]{:S(2)}) async-start(bf16[16,40,384]{2,1,0:T(8,128)(2,1)} %bitcast.117), calls=%async_computation.5 | async-start | bytes 983040 | tf_op jit(solution)/shard_map/all_to_all | solution.py:356
  271.5 1.5 collective-permute-start.22
  273.1 1.6 collective-permute-start.23
  274.7 5.1 %shard_map.111 = bf16[4,768,256]{2,1,0:T(8,128)(2,1)} custom-call(s32[2]{0:T(128)} %pad_add_fusion.at_ref, bf16[320,512]{1,0:T(8,128)(2,1)} %get-tuple-element.16.a_ref, bf16[2,320,384]{2,1,0:T(8,128)(2,1)} %bitcast.114, bf16[2,320,384]{2,1,0:T(8,128)(2,1)} %copy-done.2, bf16[320,384]{1,0:T(8,128)(2,1)} %collective-permute-done.5.refs_2_, ...), custom_call_target="tpu_custom_call" | custom-call | tf_op jit(solution)/shard_map/pallas_call | solution.py:24
  279.8 2.4 slice_bitcast_fusion.2
  282.2 2.2 collective-permute-start.26
  285.5 3.8 %collective-permute-done.22.refs_1_ = bf16[2,320,512]{2,1,0:T(8,128)(2,1)S(1)} collective-permute-done((bf16[2,320,512]{2,1,0:T(8,128)(2,1)}, bf16[2,320,512]{2,1,0:T(8,128)(2,1)S(1)}, u32[]{:S(2)}, u32[]{:S(2)}) %collective-permute-start.22) | collective-permute-done | bytes 655392 | tf_op jit(solution)/shard_map/ppermute | solution.py:348
  289.3 14.8 %collective-permute-done.23.refs_2_ = bf16[2,320,512]{2,1,0:T(8,128)(2,1)S(1)} collective-permute-done((bf16[2,320,512]{2,1,0:T(8,128)(2,1)}, bf16[2,320,512]{2,1,0:T(8,128)(2,1)S(1)}, u32[]{:S(2)}, u32[]{:S(2)}) %collective-permute-start.23) | collective-permute-done | bytes 655392 | tf_op jit(solution)/shard_map/ppermute | solution.py:348
  304.1 0.8 copy-done.16
  304.9 5.8 %shard_map.110 = bf16[640,512]{1,0:T(8,128)(2,1)} custom-call(s32[2]{0:T(128)} %pad_add_fusion.at_ref, bf16[320,512]{1,0:T(8,128)(2,1)} %get-tuple-element.16.a_ref, bf16[4,1792,512]{2,1,0:T(8,128)(2,1)} %bitcast.104, bf16[640,640]{1,0:T(8,128)(2,1)} %fusion.4.order_ref, bf16[2,320,512]{2,1,0:T(8,128)(2,1)} %copy-done.14, bf16[2,320,512]{2,1,0:T(8,128)(2,1)} %copy-done.15, ...), custom_call_target="tpu_custom_call" | custom-call | tf_op jit(solution)/shard_map/pallas_call | solution.py:24
  310.8 7.2 %all-to-all-start.6 = ((bf16[16,40,512]{2,1,0:T(8,128)(2,1)}), bf16[16,40,512]{2,1,0:T(8,128)(2,1)S(1)}, u32[]{:S(2)}, u32[]{:S(2)}) async-start(bf16[16,40,512]{2,1,0:T(8,128)(2,1)} %bitcast.115), calls=%async_computation.7 | async-start | bytes 1310720 | tf_op jit(solution)/shard_map/all_to_all | solution.py:356
  318.0 1.4 fusion.17
  319.8 1.1 convert_element_type.123
  321.0 1.3 pad_maximum_fusion.1
  322.3 2.6 convert_element_type.116
  324.9 12.5 %all-gather.1 = bf16[1280,256]{1,0:T(8,128)(2,1)} all-gather(bf16[320,256]{1,0:T(8,128)(2,1)S(1)} %copy-done.25), channel_id=3, replica_groups=mesh['dp'=4,'expert'=16,'ffn'=4] {'dp'}, dimensions={0}, use_global_device_ids=true | all-gather | bytes 819200 | tf_op jit(solution)/shard_map/all_gather | solution.py:431
  337.4 8.4 %shard_map.108 = f32[256,1792]{1,0:T(8,128)} custom-call(s32[2]{0:T(128)} %pad_add_fusion.at_ref, bf16[4,320,256]{2,1,0:T(8,128)(2,1)} %bitcast.116, bf16[2,320,512]{2,1,0:T(8,128)(2,1)} %bitcast.25.refs_0_, bf16[2,320,512]{2,1,0:T(8,128)(2,1)} %copy-done.6, bf16[320,512]{1,0:T(8,128)(2,1)} %collective-permute-done.11.refs_2_, ...), custom_call_target="tpu_custom_call" | custom-call | tf_op jit(solution)/shard_map/pallas_call | solution.py:24
  346.2 0.8 pad_maximum_fusion.2
  (140 shorter events, 14.5 us)
Async XLA Ops:
  7.2 198.1 %all-gather.4.cloned.1.call-start = ((), (), s32[]{:S(2)}) async-start(), calls=%async_computation.11 | async-start | bytes 9175040 | tf_op jit(solution)/shard_map/all_gather | solution.py:372
  10.0 2.2 copy-start.27
  10.0 2.9 copy-start.24
  10.8 13.5 %copy-start.28 = (bf16[128,1792]{1,0:T(8,128)(2,1)S(1)}, bf16[128,1792]{1,0:T(8,128)(2,1)}, u32[]{:S(2)}) copy-start(bf16[128,1792]{1,0:T(8,128)(2,1)} %param.8) | copy-start | bytes 1376260
  12.3 12.7 %collective-permute-start.8 = (f32[128,4]{0,1:T(4,128)S(1)}, f32[128,4]{0,1:T(4,128)S(1)}, u32[]{:S(2)}, u32[]{:S(2)}) collective-permute-start(f32[128,4]{0,1:T(4,128)S(1)} %pad_maximum_fusion.7), channel_id=1, source_target_pairs={{0,0},{1,64},{2,128},{3,192},{64,1},{65,65},{66,129},{67,193},{128... | collective-permute-start | bytes 6152 | tf_op jit(solution)/shard_map/ppermute | solution.py:351
  13.2 50.6 %copy-start.17 = (bf16[640,128]{1,0:T(8,128)(2,1)}, bf16[640,128]{1,0:T(8,128)(2,1)S(1)}, u32[]{:S(2)}) copy-start(bf16[640,128]{1,0:T(8,128)(2,1)S(1)} %get-tuple-element.55) | copy-start | bytes 491524
  13.2 50.6 %copy-start.19 = (bf16[640,128]{1,0:T(8,128)(2,1)}, bf16[640,128]{1,0:T(8,128)(2,1)S(1)}, u32[]{:S(2)}) copy-start(bf16[640,128]{1,0:T(8,128)(2,1)S(1)} %get-tuple-element.56) | copy-start | bytes 491524
  14.3 26.5 %all-to-all-start.1 = ((bf16[16,40,384]{2,1,0:T(8,128)(2,1)}), bf16[16,40,384]{2,1,0:T(8,128)(2,1)S(1)}, u32[]{:S(2)}, u32[]{:S(2)}) async-start(bf16[16,40,384]{2,1,0:T(8,128)(2,1)} %bitcast.13), calls=%async_computation.1 | async-start | bytes 983040 | tf_op jit(solution)/shard_map/all_to_all | solution.py:356
  24.3 1.1 collective-permute-start.9
  40.8 19.4 %all-to-all-start.3 = ((bf16[16,40,384]{2,1,0:T(8,128)(2,1)}), bf16[16,40,384]{2,1,0:T(8,128)(2,1)S(1)}, u32[]{:S(2)}, u32[]{:S(2)}) async-start(bf16[16,40,384]{2,1,0:T(8,128)(2,1)} %bitcast.28), calls=%async_computation.3 | async-start | bytes 983040 | tf_op jit(solution)/shard_map/all_to_all | solution.py:356
  60.3 23.0 %all-to-all-start.2 = ((bf16[16,40,512]{2,1,0:T(8,128)(2,1)}), bf16[16,40,512]{2,1,0:T(8,128)(2,1)S(1)}, u32[]{:S(2)}, u32[]{:S(2)}) async-start(bf16[16,40,512]{2,1,0:T(8,128)(2,1)} %bitcast.23), calls=%async_computation.2 | async-start | bytes 1310720 | tf_op jit(solution)/shard_map/all_to_all | solution.py:356
  83.2 33.3 %all-to-all-start = ((bf16[16,40,512]{2,1,0:T(8,128)(2,1)}), bf16[16,40,512]{2,1,0:T(8,128)(2,1)}, u32[]{:S(2)}, u32[]{:S(2)}) async-start(bf16[16,40,512]{2,1,0:T(8,128)(2,1)} %bitcast.8), calls=%async_computation | async-start | bytes 1310720 | tf_op jit(solution)/shard_map/all_to_all | solution.py:356
  88.7 27.8 %copy-start.5 = (bf16[640,384]{1,0:T(8,128)(2,1)}, bf16[640,384]{1,0:T(8,128)(2,1)S(1)}, u32[]{:S(2)}) copy-start(bf16[640,384]{1,0:T(8,128)(2,1)S(1)} %fusion.9) | copy-start | bytes 1474564
  88.7 65.2 %collective-permute-start.4 = (bf16[2,320,384]{2,1,0:T(8,128)(2,1)S(1)}, bf16[2,320,384]{2,1,0:T(8,128)(2,1)S(1)}, u32[]{:S(2)}, u32[]{:S(2)}) collective-permute-start(bf16[2,320,384]{2,1,0:T(8,128)(2,1)S(1)} %bitcast.110), channel_id=1, source_target_pairs={{0,1},{1,0},{2,3},{3,2},{4,5},{5,4},{6,7},{7,6},{8,9},{9,8},{10,11... | collective-permute-start | bytes 1474568 | tf_op jit(solution)/shard_map/ppermute | solution.py:348
  103.4 87.6 %collective-permute-start.6 = (bf16[2,320,384]{2,1,0:T(8,128)(2,1)S(1)}, bf16[2,320,384]{2,1,0:T(8,128)(2,1)S(1)}, u32[]{:S(2)}, u32[]{:S(2)}) collective-permute-start(bf16[2,320,384]{2,1,0:T(8,128)(2,1)S(1)} %bitcast.111), channel_id=1, source_target_pairs={{0,3},{1,2},{2,1},{3,0},{4,7},{5,6},{6,5},{7,4},{8,11},{9,10},{10,... | collective-permute-start | bytes 1474568 | tf_op jit(solution)/shard_map/ppermute | solution.py:348
  113.5 13.6 %collective-permute-start.14 = (bf16[2,320,384]{2,1,0:T(8,128)(2,1)}, bf16[2,320,384]{2,1,0:T(8,128)(2,1)S(1)}, u32[]{:S(2)}, u32[]{:S(2)}) collective-permute-start(bf16[2,320,384]{2,1,0:T(8,128)(2,1)} %bitcast.30.refs_5_), channel_id=1, source_target_pairs={{0,1},{1,0},{2,3},{3,2},{4,5},{5,4},{6,7},{7,6},{8,9},{9,8},{10,11... | collective-permute-start | bytes 1474568 | tf_op jit(solution)/shard_map/ppermute | solution.py:348
  114.3 21.6 %collective-permute-start.16 = (bf16[2,320,384]{2,1,0:T(8,128)(2,1)}, bf16[2,320,384]{2,1,0:T(8,128)(2,1)}, u32[]{:S(2)}, u32[]{:S(2)}) collective-permute-start(bf16[2,320,384]{2,1,0:T(8,128)(2,1)} %bitcast.30.refs_5_), channel_id=1, source_target_pairs={{0,3},{1,2},{2,1},{3,0},{4,7},{5,6},{6,5},{7,4},{8,11},{9,10},{10,... | collective-permute-start | bytes 1474568 | tf_op jit(solution)/shard_map/ppermute | solution.py:348
  116.5 24.5 %collective-permute-start.10 = (bf16[2,320,512]{2,1,0:T(8,128)(2,1)}, bf16[2,320,512]{2,1,0:T(8,128)(2,1)S(1)}, u32[]{:S(2)}, u32[]{:S(2)}) collective-permute-start(bf16[2,320,512]{2,1,0:T(8,128)(2,1)} %bitcast.25.refs_0_), channel_id=1, source_target_pairs={{0,1},{1,0},{2,3},{3,2},{4,5},{5,4},{6,7},{7,6},{8,9},{9,8},{10,11... | collective-permute-start | bytes 1966088 | tf_op jit(solution)/shard_map/ppermute | solution.py:348
  118.4 47.0 %copy-start.4 = (bf16[640,512]{1,0:T(8,128)(2,1)}, bf16[640,512]{1,0:T(8,128)(2,1)S(1)}, u32[]{:S(2)}) copy-start(bf16[640,512]{1,0:T(8,128)(2,1)S(1)} %fusion.5) | copy-start | bytes 1966084
  127.1 8.8 %copy-start.8 = (bf16[2,320,384]{2,1,0:T(8,128)(2,1)}, bf16[2,320,384]{2,1,0:T(8,128)(2,1)S(1)}, u32[]{:S(2)}) copy-start(bf16[2,320,384]{2,1,0:T(8,128)(2,1)S(1)} %collective-permute-done.14.refs_6_) | copy-start | bytes 1474564
  127.1 23.8 %collective-permute-start.12 = (bf16[2,320,512]{2,1,0:T(8,128)(2,1)}, bf16[2,320,512]{2,1,0:T(8,128)(2,1)S(1)}, u32[]{:S(2)}, u32[]{:S(2)}) collective-permute-start(bf16[2,320,512]{2,1,0:T(8,128)(2,1)} %bitcast.25.refs_0_), channel_id=1, source_target_pairs={{0,3},{1,2},{2,1},{3,0},{4,7},{5,6},{6,5},{7,4},{8,11},{9,10},{10,... | collective-permute-start | bytes 1966088 | tf_op jit(solution)/shard_map/ppermute | solution.py:348
  135.9 18.9 %collective-permute-start = (bf16[2,320,512]{2,1,0:T(8,128)(2,1)S(1)}, bf16[2,320,512]{2,1,0:T(8,128)(2,1)S(1)}, u32[]{:S(2)}, u32[]{:S(2)}) collective-permute-start(bf16[2,320,512]{2,1,0:T(8,128)(2,1)S(1)} %bitcast.105), channel_id=1, source_target_pairs={{0,1},{1,0},{2,3},{3,2},{4,5},{5,4},{6,7},{7,6},{8,9},{9,8},{10,11... | collective-permute-start | bytes 1966088 | tf_op jit(solution)/shard_map/ppermute | solution.py:348
  141.0 8.8 %copy-start.6 = (bf16[2,320,512]{2,1,0:T(8,128)(2,1)}, bf16[2,320,512]{2,1,0:T(8,128)(2,1)S(1)}, u32[]{:S(2)}) copy-start(bf16[2,320,512]{2,1,0:T(8,128)(2,1)S(1)} %collective-permute-done.10.refs_1_) | copy-start | bytes 1966084
  141.0 22.8 %collective-permute-start.15 = (bf16[320,384]{1,0:T(8,128)(2,1)S(1)}, bf16[320,384]{1,0:T(8,128)(2,1)S(1)}, u32[]{:S(2)}, u32[]{:S(2)}) collective-permute-start(bf16[320,384]{1,0:T(8,128)(2,1)S(1)} %slice_bitcast_fusion.9), channel_id=1, source_target_pairs={{0,3},{1,2},{2,1},{3,0},{4,7},{5,6},{6,5},{7,4},{8,11},{9,10},{10,... | collective-permute-start | bytes 737288 | tf_op jit(solution)/shard_map/ppermute | solution.py:348
  150.9 14.5 %copy-start.7 = (bf16[2,320,512]{2,1,0:T(8,128)(2,1)}, bf16[2,320,512]{2,1,0:T(8,128)(2,1)S(1)}, u32[]{:S(2)}) copy-start(bf16[2,320,512]{2,1,0:T(8,128)(2,1)S(1)} %collective-permute-done.12.refs_4_) | copy-start | bytes 1966084
  150.9 40.0 %collective-permute-start.2 = (bf16[2,320,512]{2,1,0:T(8,128)(2,1)S(1)}, bf16[2,320,512]{2,1,0:T(8,128)(2,1)S(1)}, u32[]{:S(2)}, u32[]{:S(2)}) collective-permute-start(bf16[2,320,512]{2,1,0:T(8,128)(2,1)S(1)} %bitcast.106), channel_id=1, source_target_pairs={{0,3},{1,2},{2,1},{3,0},{4,7},{5,6},{6,5},{7,4},{8,11},{9,10},{10,... | collective-permute-start | bytes 1966088 | tf_op jit(solution)/shard_map/ppermute | solution.py:348
  153.9 33.4 %copy-start.2 = (bf16[2,320,384]{2,1,0:T(8,128)(2,1)}, bf16[2,320,384]{2,1,0:T(8,128)(2,1)S(1)}, u32[]{:S(2)}) copy-start(bf16[2,320,384]{2,1,0:T(8,128)(2,1)S(1)} %collective-permute-done.4.refs_1_) | copy-start | bytes 1474564
  153.9 11.5 %collective-permute-start.17 = (bf16[320,384]{1,0:T(8,128)(2,1)S(1)}, bf16[320,384]{1,0:T(8,128)(2,1)S(1)}, u32[]{:S(2)}, u32[]{:S(2)}) collective-permute-start(bf16[320,384]{1,0:T(8,128)(2,1)S(1)} %slice_bitcast_fusion.8), channel_id=1, source_target_pairs={{0,1},{1,0},{2,3},{3,2},{4,5},{5,4},{6,7},{7,6},{8,9},{9,8},{10,11... | collective-permute-start | bytes 737288 | tf_op jit(solution)/shard_map/ppermute | solution.py:348
  154.8 32.5 %copy-start = (bf16[2,320,512]{2,1,0:T(8,128)(2,1)}, bf16[2,320,512]{2,1,0:T(8,128)(2,1)S(1)}, u32[]{:S(2)}) copy-start(bf16[2,320,512]{2,1,0:T(8,128)(2,1)S(1)} %collective-permute-done.refs_6_.refs_1_) | copy-start | bytes 1966084
  154.8 22.7 %collective-permute-start.11 = (bf16[320,512]{1,0:T(8,128)(2,1)S(1)}, bf16[320,512]{1,0:T(8,128)(2,1)}, u32[]{:S(2)}, u32[]{:S(2)}) collective-permute-start(bf16[320,512]{1,0:T(8,128)(2,1)S(1)} %slice_bitcast_fusion.5), channel_id=1, source_target_pairs={{0,3},{1,2},{2,1},{3,0},{4,7},{5,6},{6,5},{7,4},{8,11},{9,10},{10,... | collective-permute-start | bytes 983048 | tf_op jit(solution)/shard_map/ppermute | solution.py:348
  163.8 5.4 %copy-start.12 = (bf16[320,384]{1,0:T(8,128)(2,1)}, bf16[320,384]{1,0:T(8,128)(2,1)S(1)}, u32[]{:S(2)}) copy-start(bf16[320,384]{1,0:T(8,128)(2,1)S(1)} %collective-permute-done.15.refs_7_) | copy-start | bytes 737284
  163.8 16.5 %collective-permute-start.13 = (bf16[320,512]{1,0:T(8,128)(2,1)S(1)}, bf16[320,512]{1,0:T(8,128)(2,1)}, u32[]{:S(2)}, u32[]{:S(2)}) collective-permute-start(bf16[320,512]{1,0:T(8,128)(2,1)S(1)} %slice_bitcast_fusion.4), channel_id=1, source_target_pairs={{0,1},{1,0},{2,3},{3,2},{4,5},{5,4},{6,7},{7,6},{8,9},{9,8},{10,11... | collective-permute-start | bytes 983048 | tf_op jit(solution)/shard_map/ppermute | solution.py:348
  165.4 12.1 %copy-start.13 = (bf16[320,384]{1,0:T(8,128)(2,1)}, bf16[320,384]{1,0:T(8,128)(2,1)S(1)}, u32[]{:S(2)}) copy-start(bf16[320,384]{1,0:T(8,128)(2,1)S(1)} %collective-permute-done.17.refs_8_) | copy-start | bytes 737284
  165.4 27.2 %collective-permute-start.5 = (bf16[320,384]{1,0:T(8,128)(2,1)}, bf16[320,384]{1,0:T(8,128)(2,1)}, u32[]{:S(2)}, u32[]{:S(2)}) collective-permute-start(bf16[320,384]{1,0:T(8,128)(2,1)} %slice_bitcast_fusion.11), channel_id=1, source_target_pairs={{0,3},{1,2},{2,1},{3,0},{4,7},{5,6},{6,5},{7,4},{8,11},{9,10},{10,... | collective-permute-start | bytes 737288 | tf_op jit(solution)/shard_map/ppermute | solution.py:348
  177.5 35.0 %collective-permute-start.1 = (bf16[320,512]{1,0:T(8,128)(2,1)}, bf16[320,512]{1,0:T(8,128)(2,1)}, u32[]{:S(2)}, u32[]{:S(2)}) collective-permute-start(bf16[320,512]{1,0:T(8,128)(2,1)} %slice_bitcast_fusion.7), channel_id=1, source_target_pairs={{0,3},{1,2},{2,1},{3,0},{4,7},{5,6},{6,5},{7,4},{8,11},{9,10},{10,... | collective-permute-start | bytes 983048 | tf_op jit(solution)/shard_map/ppermute | solution.py:348
  187.3 25.2 %all-to-all-start.4 = ((bf16[4,320,256]{2,1,0:T(8,128)(2,1)}), bf16[4,320,256]{2,1,0:T(8,128)(2,1)S(1)}, u32[]{:S(2)}, u32[]{:S(2)}) async-start(bf16[4,320,256]{2,1,0:T(8,128)(2,1)} %shard_map.103), calls=%async_computation.4 | async-start | bytes 1310720 | tf_op jit(solution)/shard_map/all_to_all | solution.py:409
  190.8 129.0 %reduce-scatter.5.cloned.1.call-start = ((), (), s32[]{:S(2)}) async-start(), calls=%async_computation.10 | async-start | bytes 2621440 | tf_op jit(solution)/shard_map/reduce_scatter | solution.py:424
  190.9 14.4 %copy-start.1 = (bf16[2,320,512]{2,1,0:T(8,128)(2,1)}, bf16[2,320,512]{2,1,0:T(8,128)(2,1)S(1)}, u32[]{:S(2)}) copy-start(bf16[2,320,512]{2,1,0:T(8,128)(2,1)S(1)} %collective-permute-done.2.refs_7_.refs_9_.refs_4_) | copy-start | bytes 1966084
  190.9 21.5 %collective-permute-start.3 = (bf16[320,512]{1,0:T(8,128)(2,1)S(1)}, bf16[320,512]{1,0:T(8,128)(2,1)S(1)}, u32[]{:S(2)}, u32[]{:S(2)}) collective-permute-start(bf16[320,512]{1,0:T(8,128)(2,1)S(1)} %slice_bitcast_fusion.6), channel_id=1, source_target_pairs={{0,1},{1,0},{2,3},{3,2},{4,5},{5,4},{6,7},{7,6},{8,9},{9,8},{10,11... | collective-permute-start | bytes 983048 | tf_op jit(solution)/shard_map/ppermute | solution.py:348
  191.0 14.3 %copy-start.3 = (bf16[2,320,384]{2,1,0:T(8,128)(2,1)}, bf16[2,320,384]{2,1,0:T(8,128)(2,1)S(1)}, u32[]{:S(2)}) copy-start(bf16[2,320,384]{2,1,0:T(8,128)(2,1)S(1)} %collective-permute-done.6.refs_4_) | copy-start | bytes 1474564
  191.1 14.2 %collective-permute-start.7 = (bf16[320,384]{1,0:T(8,128)(2,1)S(1)}, bf16[320,384]{1,0:T(8,128)(2,1)S(1)}, u32[]{:S(2)}, u32[]{:S(2)}) collective-permute-start(bf16[320,384]{1,0:T(8,128)(2,1)S(1)} %slice_bitcast_fusion.10), channel_id=1, source_target_pairs={{0,1},{1,0},{2,3},{3,2},{4,5},{5,4},{6,7},{7,6},{8,9},{9,8},{10,11... | collective-permute-start | bytes 737288 | tf_op jit(solution)/shard_map/ppermute | solution.py:348
  212.5 0.7 copy-start.9
  213.2 0.9 copy-start.10
  223.4 98.9 %reduce-scatter.3.cloned.1.call-start = ((), (), s32[]{:S(2)}) async-start(), calls=%async_computation.9 | async-start | bytes 4587520 | tf_op jit(solution)/shard_map/reduce_scatter | solution.py:414
  235.2 12.1 %collective-permute-start.18 = (bf16[2,320,384]{2,1,0:T(8,128)(2,1)}, bf16[2,320,384]{2,1,0:T(8,128)(2,1)S(1)}, u32[]{:S(2)}, u32[]{:S(2)}) collective-permute-start(bf16[2,320,384]{2,1,0:T(8,128)(2,1)} %get-tuple-element.17), channel_id=1, source_target_pairs={{0,1},{1,0},{2,3},{3,2},{4,5},{5,4},{6,7},{7,6},{8,9},{9,8},{10,11... | collective-permute-start | bytes 1474568 | tf_op jit(solution)/shard_map/ppermute | solution.py:348
  235.8 21.2 %collective-permute-start.19 = (bf16[2,320,384]{2,1,0:T(8,128)(2,1)}, bf16[2,320,384]{2,1,0:T(8,128)(2,1)S(1)}, u32[]{:S(2)}, u32[]{:S(2)}) collective-permute-start(bf16[2,320,384]{2,1,0:T(8,128)(2,1)} %get-tuple-element.18), channel_id=1, source_target_pairs={{0,2},{1,3},{2,0},{3,1},{4,6},{5,7},{6,4},{7,5},{8,10},{9,11},{10,... | collective-permute-start | bytes 1474568 | tf_op jit(solution)/shard_map/ppermute | solution.py:348
  236.4 21.4 %collective-permute-start.20 = (bf16[2,320,384]{2,1,0:T(8,128)(2,1)}, bf16[2,320,384]{2,1,0:T(8,128)(2,1)S(1)}, u32[]{:S(2)}, u32[]{:S(2)}) collective-permute-start(bf16[2,320,384]{2,1,0:T(8,128)(2,1)} %get-tuple-element.19), channel_id=1, source_target_pairs={{0,3},{1,2},{2,1},{3,0},{4,7},{5,6},{6,5},{7,4},{8,11},{9,10},{10,... | collective-permute-start | bytes 1474568 | tf_op jit(solution)/shard_map/ppermute | solution.py:348
  244.7 40.3 %collective-permute-start.21 = (bf16[2,320,512]{2,1,0:T(8,128)(2,1)}, bf16[2,320,512]{2,1,0:T(8,128)(2,1)S(1)}, u32[]{:S(2)}, u32[]{:S(2)}) collective-permute-start(bf16[2,320,512]{2,1,0:T(8,128)(2,1)} %get-tuple-element.23), channel_id=1, source_target_pairs={{0,1},{1,0},{2,3},{3,2},{4,5},{5,4},{6,7},{7,6},{8,9},{9,8},{10,11... | collective-permute-start | bytes 1966088 | tf_op jit(solution)/shard_map/ppermute | solution.py:348
  247.3 10.5 %copy-start.21 = (bf16[2,320,384]{2,1,0:T(8,128)(2,1)}, bf16[2,320,384]{2,1,0:T(8,128)(2,1)S(1)}, u32[]{:S(2)}) copy-start(bf16[2,320,384]{2,1,0:T(8,128)(2,1)S(1)} %collective-permute-done.18.refs_0_) | copy-start | bytes 1474564
  257.1 0.8 copy-start.22
  257.8 0.8 copy-start.23
  263.9 46.8 %all-to-all-start.5 = ((bf16[16,40,384]{2,1,0:T(8,128)(2,1)}), bf16[16,40,384]{2,1,0:T(8,128)(2,1)S(1)}, u32[]{:S(2)}, u32[]{:S(2)}) async-start(bf16[16,40,384]{2,1,0:T(8,128)(2,1)} %bitcast.117), calls=%async_computation.5 | async-start | bytes 983040 | tf_op jit(solution)/shard_map/all_to_all | solution.py:356
  271.5 17.7 %collective-permute-start.22 = (bf16[2,320,512]{2,1,0:T(8,128)(2,1)}, bf16[2,320,512]{2,1,0:T(8,128)(2,1)S(1)}, u32[]{:S(2)}, u32[]{:S(2)}) collective-permute-start(bf16[2,320,512]{2,1,0:T(8,128)(2,1)} %get-tuple-element.24), channel_id=1, source_target_pairs={{0,2},{1,3},{2,0},{3,1},{4,6},{5,7},{6,4},{7,5},{8,10},{9,11},{10,... | collective-permute-start | bytes 1966088 | tf_op jit(solution)/shard_map/ppermute | solution.py:348
  273.1 31.0 %collective-permute-start.23 = (bf16[2,320,512]{2,1,0:T(8,128)(2,1)}, bf16[2,320,512]{2,1,0:T(8,128)(2,1)S(1)}, u32[]{:S(2)}, u32[]{:S(2)}) collective-permute-start(bf16[2,320,512]{2,1,0:T(8,128)(2,1)} %get-tuple-element.25), channel_id=1, source_target_pairs={{0,3},{1,2},{2,1},{3,0},{4,7},{5,6},{6,5},{7,4},{8,11},{9,10},{10,... | collective-permute-start | bytes 1966088 | tf_op jit(solution)/shard_map/ppermute | solution.py:348
  279.8 5.6 %copy-start.18 = (bf16[640,128]{1,0:T(8,128)(2,1)S(1)}, bf16[640,128]{1,0:T(8,128)(2,1)}, u32[]{:S(2)}) copy-start(bf16[640,128]{1,0:T(8,128)(2,1)} %copy-done.17) | copy-start | bytes 491524
  279.8 5.6 %copy-start.20 = (bf16[640,128]{1,0:T(8,128)(2,1)S(1)}, bf16[640,128]{1,0:T(8,128)(2,1)}, u32[]{:S(2)}) copy-start(bf16[640,128]{1,0:T(8,128)(2,1)} %copy-done.19) | copy-start | bytes 491524
  282.2 35.8 %collective-permute-start.26 = (bf16[768,256]{1,0:T(8,128)(2,1)}, bf16[768,256]{1,0:T(8,128)(2,1)S(1)}, u32[]{:S(2)}, u32[]{:S(2)}) collective-permute-start(bf16[768,256]{1,0:T(8,128)(2,1)} %get-tuple-element.31), channel_id=1, source_target_pairs={{0,192},{64,128},{128,64},{192,0},{1,193},{65,129},{129,65},{193,1... | collective-permute-start | bytes 1179656 | tf_op jit(solution)/shard_map/ppermute | solution.py:348
  284.4 33.6 %collective-permute-start.25 = (bf16[768,256]{1,0:T(8,128)(2,1)}, bf16[768,256]{1,0:T(8,128)(2,1)}, u32[]{:S(2)}, u32[]{:S(2)}) collective-permute-start(bf16[768,256]{1,0:T(8,128)(2,1)} %get-tuple-element.32), channel_id=1, source_target_pairs={{0,128},{64,192},{128,0},{192,64},{1,129},{65,193},{129,1},{193,65... | collective-permute-start | bytes 1179656 | tf_op jit(solution)/shard_map/ppermute | solution.py:348
  285.0 19.1 %copy-start.14 = (bf16[2,320,512]{2,1,0:T(8,128)(2,1)}, bf16[2,320,512]{2,1,0:T(8,128)(2,1)S(1)}, u32[]{:S(2)}) copy-start(bf16[2,320,512]{2,1,0:T(8,128)(2,1)S(1)} %collective-permute-done.21.refs_0_) | copy-start | bytes 1966084
  285.0 33.0 %collective-permute-start.24 = (bf16[768,256]{1,0:T(8,128)(2,1)}, bf16[768,256]{1,0:T(8,128)(2,1)}, u32[]{:S(2)}, u32[]{:S(2)}) collective-permute-start(bf16[768,256]{1,0:T(8,128)(2,1)} %get-tuple-element.30), channel_id=1, source_target_pairs={{0,64},{64,0},{128,192},{192,128},{1,65},{65,1},{129,193},{193,129... | collective-permute-start | bytes 1179656 | tf_op jit(solution)/shard_map/ppermute | solution.py:348
  289.3 14.8 %copy-start.15 = (bf16[2,320,512]{2,1,0:T(8,128)(2,1)}, bf16[2,320,512]{2,1,0:T(8,128)(2,1)S(1)}, u32[]{:S(2)}) copy-start(bf16[2,320,512]{2,1,0:T(8,128)(2,1)S(1)} %collective-permute-done.22.refs_1_) | copy-start | bytes 1966084
  304.1 0.9 copy-start.16
  310.8 35.0 %all-to-all-start.6 = ((bf16[16,40,512]{2,1,0:T(8,128)(2,1)}), bf16[16,40,512]{2,1,0:T(8,128)(2,1)S(1)}, u32[]{:S(2)}, u32[]{:S(2)}) async-start(bf16[16,40,512]{2,1,0:T(8,128)(2,1)} %bitcast.115), calls=%async_computation.7 | async-start | bytes 1310720 | tf_op jit(solution)/shard_map/all_to_all | solution.py:356
  322.3 2.6 copy-start.25
  (2 other events, 1.4 us)
Sparse Core Ops, SparseCore 0:
  10.4 96.1 all-gather.3
  223.5 27.3 reduce-scatter.4
  253.5 61.6 reduce-scatter.2

commit v5 on v4

--- a/solution.py
+++ b/solution.py
@@ -176,7 +176,7 @@
     return call(body, out, scratch, [at, w_down] + flat(chunks), 1 + N + count * N)
 
 
-def weight_grad(chunks, acts, at, lo_col, relative=False, unroll=False):
+def weight_grad(chunks, acts, at, lo_col, unroll=False):
     rows, cols = acts.shape
     units = cols // 2
     width = sum(2 * parts[0].shape[2] for parts in chunks)
@@ -205,8 +205,7 @@
                 else:
                     lax.fori_loop(0, 2, piece, 0)
                 lo += 2 * w
-            to = at_ref[0] ^ j ^ at_ref[1] if relative else at_ref[0] ^ j
-            start(out_buf.at[j], out.at[to], sems.at[1 + j])
+            start(out_buf.at[j], out.at[at_ref[0] ^ j], sems.at[1 + j])
             return carry
 
         lax.fori_loop(0, N, step, 0)
@@ -267,12 +266,9 @@
         def step(j, carry):
             pltpu.make_async_copy(w_ref.at[0, pl.ds(offset, 2 * width)], w_buf.at[j], sems.at[1 + j]).wait()
 
-            def piece(c, carry):
-                w = w_buf[j, pl.ds(pl.multiple_of(c * width, 128), width)]
-                out_buf[j, c] = dot(a_buf[...], w, NT).astype(BF16)
-                return carry
-
-            return lax.fori_loop(0, 2, piece, carry)
+            for c in range(2):
+                out_buf[j, c] = dot(a_buf[...], w_buf[j, c * width : (c + 1) * width], NT).astype(BF16)
+            return carry
 
         lax.fori_loop(0, N - 1, step, 0)
         stores = [start(out_buf.at[j], outs[j], sems.at[j]) for j in range(N - 1)]
@@ -299,14 +295,11 @@
         for copy in copies:
             copy.wait()
 
-        def piece(c, carry):
-            total = dot(a_buf[...], w_buf[pl.ds(pl.multiple_of(c * width, 128), width)], NT)
+        for c in range(2):
+            total = dot(a_buf[...], w_buf[c * width : (c + 1) * width], NT)
             for j in range(N - 1):
                 total = total + r_buf[j, c].astype(F32)
-            t_buf[pl.ds(pl.multiple_of(c * rows, rows), rows)] = total.astype(BF16)
-            return carry
-
-        lax.fori_loop(0, 2, piece, 0)
+            t_buf[c * rows : (c + 1) * rows] = total.astype(BF16)
 
         def step(i, carry):
             block = pl.ds(i * (rows // 2), rows // 2)
@@ -342,10 +335,10 @@
     small = width // 2 - piece
     pieces, starts = (small, piece), (0, 2 * small)
     z_pieces, z_starts = (piece, small), (0, 2 * piece)
-    at = jnp.stack([lax.axis_index("ffn"), lax.axis_index("dp")]).astype(jnp.int32)
-
-    def swap(x, by, axis="ffn"):
-        return lax.ppermute(x, axis, [(i, i ^ by) for i in range(N)])
+    at = lax.axis_index("ffn").astype(jnp.int32)[None]
+
+    def swap(x, by):
+        return lax.ppermute(x, "ffn", [(i, i ^ by) for i in range(N)])
 
     def flip(x):
         return lax.ppermute(
@@ -419,16 +412,13 @@
     received = []
     for h in range(2):
         received.append([swap(leads[h][j - 1], j) for j in range(1, N)])
-    direct = weight_grad((x_0,), acts, at, gate_weight.shape[2], relative=True)
-    scattered = weight_grad((x_1,), acts, at, gate_weight.shape[2])
-    scattered = lax.psum_scatter(scattered, "dp", scatter_dimension=0, tiled=True)
-    direct = [direct[0]] + [swap(direct[j], j, "dp") for j in range(1, N)]
-    direct = sum(d.astype(F32) for d in direct)
-    grad_up = jnp.concatenate([direct[None], scattered.astype(F32)], axis=1)
+    part_up = weight_grad((x_0, x_1), acts, at, gate_weight.shape[2])
+    grad_up = lax.psum_scatter(part_up, "dp", scatter_dimension=0, tiled=True).astype(F32)
 
     grad_tokens = []
-    hidden, grad_gate = lax.optimization_barrier((hidden, grad_gate))
     hidden_all = lax.all_gather(hidden, "dp", axis=0, tiled=False)
+    received[1], hidden_all = lax.optimization_barrier((received[1], hidden_all))
+    hidden_all, grad_gate = lax.optimization_barrier((hidden_all, grad_gate))
     grad_down = down_grad((z_0, z_1), hidden_all, at)[None]
     for h in range(2):
         total = input_totals(acts, w_in, at, starts[h], received[h], order_back)

time: 356 us -> 352 us (0.989)
  waiting for transfers between devices: 113 us -> 149 us
  starting transfers between devices: 114 us -> 86.7 us
  Pallas kernels: 64.5 us -> 53.8 us
  blocking collectives: 12.5 us -> 16.2 us
    ppermute x25 -> x22, starting transfers between devices: 73.2 us -> 46.1 us  [swap(): return lax.ppermute(x, 'ffn', [(i, i ^ by) for i in range(N)])]
    ppermute x25 -> x22, waiting for transfers between devices: 66.1 us -> 92.3 us  [swap(): return lax.ppermute(x, 'ffn', [(i, i ^ by) for i in range(N)])]
    pallas_call x11 -> x10, Pallas kernels: 64.5 us -> 53.8 us  [call(): pl.pallas_call(body, out_shape=outs, in_specs=[SMEM] + [ANY] * (len(args)...]
    all_to_all x6, waiting for transfers between devices: 47.3 us -> 56.4 us  [exchange(): return lax.all_to_all(x, 'expert', split_axis=0, concat_axis=0, tiled=True)]
    all_gather x1, blocking collectives: 12.5 us -> 16.2 us  [per_device(): hidden_all = lax.all_gather(hidden, 'dp', axis=0, tiled=False)]
  transfers between devices with their start and end apart: 37 -> 34, of which waited for: 14 -> 17; matrix products, arithmetic and copies ran while one was open for 7% -> 6% of each run, Pallas kernels for 16% -> 13%
where the time goes in v5:
time: 352 us; the launch traced here: 351 us
  waiting for transfers between devices  149 us (42%)
  starting transfers between devices  86.7 us (25%)
  Pallas kernels  53.8 us (15%)
  blocking collectives  16.2 us (5%)
  between operations  14.3 us (4%)
  other arithmetic  11.1 us (3%)
  matrix products  10.9 us (3%)
  local copies, waits for them, and re-layouts  8.92 us (3%)
    ppermute x22, waiting for transfers between devices, swap(): return lax.ppermute(x, 'ffn', [(i, i ^ by) for i in range(N)])  92.3 us
    all_to_all x6, waiting for transfers between devices, exchange(): return lax.all_to_all(x, 'expert', split_axis=0, concat_axis=0, tiled=True)  56.4 us
    pallas_call x10, Pallas kernels, call(): pl.pallas_call(body, out_shape=outs, in_specs=[SMEM] + [ANY] * (len(args)...  53.8 us
    ppermute x22, starting transfers between devices, swap(): return lax.ppermute(x, 'ffn', [(i, i ^ by) for i in range(N)])  46.1 us
    all_to_all x6, starting transfers between devices, exchange(): return lax.all_to_all(x, 'expert', split_axis=0, concat_axis=0, tiled=True)  35.3 us
    all_gather x1, blocking collectives, per_device(): hidden_all = lax.all_gather(hidden, 'dp', axis=0, tiled=False)  16.2 us
    dot_general x10, matrix products, dot(): lax.dot_general(a, b, (contract, ((), ())), preferred_element_type=F32)  10.9 us
  transfers between devices with their start and end apart: 34, of which 17 were waited for; matrix products, arithmetic and copies ran while one was open for 6% of the time, Pallas kernels for 13%

profile of v5, /device:TPU:1, one launch (start us, length us, event | category | flops | bytes accessed | tf_op | source)
XLA Modules:
  0.0 350.7 jit_solution(6331936680522923847)
XLA Ops:
  7.2 2.8 pad_maximum_fusion
  13.2 1.1 convolution_convert_fusion.1
  14.3 10.0 %all-to-all-start.1 = ((bf16[16,40,384]{2,1,0:T(8,128)(2,1)}), bf16[16,40,384]{2,1,0:T(8,128)(2,1)S(1)}, u32[]{:S(2)}, u32[]{:S(2)}) async-start(bf16[16,40,384]{2,1,0:T(8,128)(2,1)} %bitcast.12), calls=%async_computation.1 | async-start | bytes 983040 | tf_op jit(solution)/shard_map/all_to_all | solution.py:349
  25.4 1.2 fusion.8
  26.6 14.2 %all-to-all-done.1 = bf16[16,40,384]{2,1,0:T(8,128)(2,1)S(1)} async-done(((bf16[16,40,384]{2,1,0:T(8,128)(2,1)}), bf16[16,40,384]{2,1,0:T(8,128)(2,1)S(1)}, u32[]{:S(2)}, u32[]{:S(2)}) %all-to-all-start.1) | async-done | bytes 491552 | tf_op jit(solution)/shard_map/all_to_all | solution.py:349
  40.8 3.5 all-to-all-start.3
  44.3 1.2 fusion.7
  45.5 14.8 %all-to-all-done.3 = bf16[16,40,384]{2,1,0:T(8,128)(2,1)S(1)} async-done(((bf16[16,40,384]{2,1,0:T(8,128)(2,1)}), bf16[16,40,384]{2,1,0:T(8,128)(2,1)S(1)}, u32[]{:S(2)}, u32[]{:S(2)}) %all-to-all-start.3) | async-done | bytes 491552 | tf_op jit(solution)/shard_map/all_to_all | solution.py:349
  60.3 3.5 all-to-all-start.2
  63.8 1.2 convolution_convert_fusion
  65.0 18.3 %all-to-all-done.2 = bf16[16,40,512]{2,1,0:T(8,128)(2,1)S(1)} async-done(((bf16[16,40,512]{2,1,0:T(8,128)(2,1)}), bf16[16,40,512]{2,1,0:T(8,128)(2,1)S(1)}, u32[]{:S(2)}, u32[]{:S(2)}) %all-to-all-start.2) | async-done | bytes 655392 | tf_op jit(solution)/shard_map/all_to_all | solution.py:349
  83.2 4.2 %all-to-all-start = ((bf16[16,40,512]{2,1,0:T(8,128)(2,1)}), bf16[16,40,512]{2,1,0:T(8,128)(2,1)}, u32[]{:S(2)}, u32[]{:S(2)}) async-start(bf16[16,40,512]{2,1,0:T(8,128)(2,1)} %bitcast.7), calls=%async_computation | async-start | bytes 1310720 | tf_op jit(solution)/shard_map/all_to_all | solution.py:349
  88.1 23.3 %collective-permute-start.6 = (bf16[2,320,384]{2,1,0:T(8,128)(2,1)S(1)}, bf16[2,320,384]{2,1,0:T(8,128)(2,1)S(1)}, u32[]{:S(2)}, u32[]{:S(2)}) collective-permute-start(bf16[2,320,384]{2,1,0:T(8,128)(2,1)S(1)} %bitcast.96), channel_id=1, source_target_pairs={{0,3},{1,2},{2,1},{3,0},{4,7},{5,6},{6,5},{7,4},{8,11},{9,10},{10,... | collective-permute-start | bytes 1474568 | tf_op jit(solution)/shard_map/ppermute | solution.py:341
  111.4 1.5 fusion.10
  113.0 1.4 collective-permute-start.14
  114.3 1.6 fusion.6
  115.9 2.1 collective-permute-start.12
  118.0 1.8 fusion.5
  119.8 13.9 %collective-permute-done.16.refs_9_ = bf16[2,320,384]{2,1,0:T(8,128)(2,1)S(1)} collective-permute-done((bf16[2,320,384]{2,1,0:T(8,128)(2,1)}, bf16[2,320,384]{2,1,0:T(8,128)(2,1)S(1)}, u32[]{:S(2)}, u32[]{:S(2)}) %collective-permute-start.16) | collective-permute-done | bytes 491552 | tf_op jit(solution)/shard_map/ppermute | solution.py:341
  133.7 1.2 collective-permute-done.14.refs_6_
  134.9 2.3 collective-permute-start.2
  137.2 1.0 slice_bitcast_fusion.5
  138.1 9.6 %collective-permute-done.12.refs_4_ = bf16[2,320,512]{2,1,0:T(8,128)(2,1)S(1)} collective-permute-done((bf16[2,320,512]{2,1,0:T(8,128)(2,1)}, bf16[2,320,512]{2,1,0:T(8,128)(2,1)S(1)}, u32[]{:S(2)}, u32[]{:S(2)}) %collective-permute-start.12) | collective-permute-done | bytes 655392 | tf_op jit(solution)/shard_map/ppermute | solution.py:341
  147.8 0.8 copy-done.6
  148.6 1.4 collective-permute-done.10.refs_1_
  150.1 3.3 collective-permute-start.15
  153.4 8.4 %collective-permute-done.2.refs_7_.refs_9_ = bf16[2,320,512]{2,1,0:T(8,128)(2,1)S(1)} collective-permute-done((bf16[2,320,512]{2,1,0:T(8,128)(2,1)S(1)}, bf16[2,320,512]{2,1,0:T(8,128)(2,1)S(1)}, u32[]{:S(2)}, u32[]{:S(2)}) %collective-permute-start.2) | collective-permute-done | bytes 655392 | tf_op jit(solution)/shard_map/ppermute | solution.py:341
  161.8 2.8 collective-permute-start.11
  165.3 0.7 slice_bitcast_fusion.2
  166.0 1.1 collective-permute-done.15.refs_7_
  167.2 9.7 %collective-permute-done.13.refs_3_ = bf16[320,512]{1,0:T(8,128)(2,1)} collective-permute-done((bf16[320,512]{1,0:T(8,128)(2,1)S(1)}, bf16[320,512]{1,0:T(8,128)(2,1)}, u32[]{:S(2)}, u32[]{:S(2)}) %collective-permute-start.13) | collective-permute-done | bytes 327712 | tf_op jit(solution)/shard_map/ppermute | solution.py:341
  176.9 6.3 %shard_map.103 = bf16[4,320,256]{2,1,0:T(8,128)(2,1)} custom-call(s32[1]{0:T(128)} %bitcast.3.at_ref, bf16[256,1792]{1,0:T(8,128)(2,1)} %bitcast.107, bf16[2,320,512]{2,1,0:T(8,128)(2,1)} %bitcast.24.refs_0_, bf16[2,320,512]{2,1,0:T(8,128)(2,1)} %copy-done.7, bf16[320,512]{1,0:T(8,128)(2,1)} %collective-permute-done.11.refs_2_, ...), custom_call_target="tpu_custom_call" | custom-call | tf_op jit(solution)/shard_map/pallas_call | solution.py:24
  183.2 3.9 %all-to-all-start.4 = ((bf16[4,320,256]{2,1,0:T(8,128)(2,1)}), bf16[4,320,256]{2,1,0:T(8,128)(2,1)S(1)}, u32[]{:S(2)}, u32[]{:S(2)}) async-start(bf16[4,320,256]{2,1,0:T(8,128)(2,1)} %shard_map.103), calls=%async_computation.4 | async-start | bytes 1310720 | tf_op jit(solution)/shard_map/all_to_all | solution.py:402
  187.2 2.6 collective-permute-start.1
  190.0 12.7 %collective-permute-done.5.refs_2_ = bf16[320,384]{1,0:T(8,128)(2,1)S(1)} collective-permute-done((bf16[320,384]{1,0:T(8,128)(2,1)S(1)}, bf16[320,384]{1,0:T(8,128)(2,1)S(1)}, u32[]{:S(2)}, u32[]{:S(2)}) %collective-permute-start.5) | collective-permute-done | bytes 245792 | tf_op jit(solution)/shard_map/ppermute | solution.py:341
  203.4 5.8 %shard_map.102.refs_2_ = f32[320,512]{1,0:T(8,128)} custom-call(s32[1]{0:T(128)} %bitcast.3.at_ref, bf16[4,1792,512]{2,1,0:T(8,128)(2,1)} %bitcast.85, bf16[2,320,384]{2,1,0:T(8,128)(2,1)} %bitcast.98, bf16[2,320,384]{2,1,0:T(8,128)(2,1)} %copy-done.3, bf16[320,384]{1,0:T(8,128)(2,1)} %copy-done.11, bf16[320,384]{1,0:T(8,128)(2,1)} %collective-permute-done.7.refs_3_, ...), custom_call_target="tpu_custom_call" | custom-call | tf_op jit(solution)/shard_map/pallas_call | solution.py:24
  210.0 0.8 copy-done.10
  210.8 3.1 shard_map.104
  213.9 5.8 %shard_map.108 = bf16[4,1792,256]{2,1,0:T(8,128)(2,1)} custom-call(s32[1]{0:T(128)} %bitcast.3.at_ref, bf16[320,512]{1,0:T(8,128)(2,1)} %get-tuple-element.20.a_ref, bf16[2,320,384]{2,1,0:T(8,128)(2,1)} %bitcast.99, bf16[2,320,384]{2,1,0:T(8,128)(2,1)} %copy-done.3, bf16[320,384]{1,0:T(8,128)(2,1)} %copy-done.11, ...), custom_call_target="tpu_custom_call" | custom-call | tf_op jit(solution)/shard_map/pallas_call | solution.py:24
  219.8 7.4 %shard_map.111 = bf16[4,1792,256]{2,1,0:T(8,128)(2,1)} custom-call(s32[1]{0:T(128)} %bitcast.3.at_ref, bf16[320,512]{1,0:T(8,128)(2,1)} %get-tuple-element.20.a_ref, bf16[2,320,384]{2,1,0:T(8,128)(2,1)} %bitcast.100, bf16[2,320,384]{2,1,0:T(8,128)(2,1)} %copy-done.3, bf16[320,384]{1,0:T(8,128)(2,1)} %copy-done.11, ...), custom_call_target="tpu_custom_call" | custom-call | tf_op jit(solution)/shard_map/pallas_call | solution.py:24
  227.2 3.9 %shard_map.105 = (bf16[2,320,384]{2,1,0:T(8,128)(2,1)}, bf16[2,320,384]{2,1,0:T(8,128)(2,1)}, bf16[2,320,384]{2,1,0:T(8,128)(2,1)}) custom-call(s32[1]{0:T(128)} %bitcast.3.at_ref, bf16[320,512]{1,0:T(8,128)(2,1)} %get-tuple-element.20.a_ref, bf16[4,1792,512]{2,1,0:T(8,128)(2,1)} %bitcast.87), custom_call_target="tpu_custom_call" | custom-call | tf_op jit(solution)/shard_map/pallas_call | solution.py:24
  231.2 1.0 collective-permute-start.18
  232.1 3.2 collective-permute-start.19
  235.4 1.1 fusion.4.order_ref
  236.5 6.7 %collective-permute-done.18.refs_0_ = bf16[2,320,384]{2,1,0:T(8,128)(2,1)S(1)} collective-permute-done((bf16[2,320,384]{2,1,0:T(8,128)(2,1)}, bf16[2,320,384]{2,1,0:T(8,128)(2,1)S(1)}, u32[]{:S(2)}, u32[]{:S(2)}) %collective-permute-start.18) | collective-permute-done | bytes 491552 | tf_op jit(solution)/shard_map/ppermute | solution.py:341
  243.2 13.1 %collective-permute-done.19.refs_1_ = bf16[2,320,384]{2,1,0:T(8,128)(2,1)S(1)} collective-permute-done((bf16[2,320,384]{2,1,0:T(8,128)(2,1)}, bf16[2,320,384]{2,1,0:T(8,128)(2,1)S(1)}, u32[]{:S(2)}, u32[]{:S(2)}) %collective-permute-start.19) | collective-permute-done | bytes 491552 | tf_op jit(solution)/shard_map/ppermute | solution.py:341
  256.4 2.2 collective-permute-done.20.refs_2_
  258.5 0.8 copy-done.23
  259.3 4.4 %shard_map.106 = bf16[640,384]{1,0:T(8,128)(2,1)} custom-call(s32[1]{0:T(128)} %bitcast.3.at_ref, bf16[320,512]{1,0:T(8,128)(2,1)} %get-tuple-element.20.a_ref, bf16[4,1792,512]{2,1,0:T(8,128)(2,1)} %bitcast.88, bf16[640,640]{1,0:T(8,128)(2,1)} %fusion.4.order_ref, bf16[2,320,384]{2,1,0:T(8,128)(2,1)} %copy-done.21, bf16[2,320,384]{2,1,0:T(8,128)(2,1)} %copy-done.22, ...), custom_call_target="tpu_custom_call" | custom-call | tf_op jit(solution)/shard_map/pallas_call | solution.py:24
  263.8 5.8 %all-to-all-start.5 = ((bf16[16,40,384]{2,1,0:T(8,128)(2,1)}), bf16[16,40,384]{2,1,0:T(8,128)(2,1)S(1)}, u32[]{:S(2)}, u32[]{:S(2)}) async-start(bf16[16,40,384]{2,1,0:T(8,128)(2,1)} %bitcast.103), calls=%async_computation.5 | async-start | bytes 983040 | tf_op jit(solution)/shard_map/all_to_all | solution.py:349
  269.6 4.3 %shard_map.107 = (bf16[2,320,512]{2,1,0:T(8,128)(2,1)}, bf16[2,320,512]{2,1,0:T(8,128)(2,1)}, bf16[2,320,512]{2,1,0:T(8,128)(2,1)}) custom-call(s32[1]{0:T(128)} %bitcast.3.at_ref, bf16[320,512]{1,0:T(8,128)(2,1)} %get-tuple-element.20.a_ref, bf16[4,1792,512]{2,1,0:T(8,128)(2,1)} %bitcast.89), custom_call_target="tpu_custom_call" | custom-call | tf_op jit(solution)/shard_map/pallas_call | solution.py:24
  274.0 1.1 collective-permute-start.22
  275.1 2.7 collective-permute-start.23
  277.8 16.2 %all-gather.1 = bf16[1280,256]{1,0:T(8,128)(2,1)} all-gather(bf16[320,256]{1,0:T(8,128)(2,1)S(1)} %copy-done.25), channel_id=3, replica_groups=mesh['dp'=4,'expert'=16,'ffn'=4] {'dp'}, dimensions={0}, use_global_device_ids=true | all-gather | bytes 819200 | tf_op jit(solution)/shard_map/all_gather | solution.py:419
  294.0 10.0 %collective-permute-done.22.refs_1_ = bf16[2,320,512]{2,1,0:T(8,128)(2,1)S(1)} collective-permute-done((bf16[2,320,512]{2,1,0:T(8,128)(2,1)}, bf16[2,320,512]{2,1,0:T(8,128)(2,1)S(1)}, u32[]{:S(2)}, u32[]{:S(2)}) %collective-permute-start.22) | collective-permute-done | bytes 655392 | tf_op jit(solution)/shard_map/ppermute | solution.py:341
  304.0 2.2 collective-permute-done.23.refs_2_
  306.3 0.8 copy-done.16
  307.1 5.0 %shard_map.110 = bf16[640,512]{1,0:T(8,128)(2,1)} custom-call(s32[1]{0:T(128)} %bitcast.3.at_ref, bf16[320,512]{1,0:T(8,128)(2,1)} %get-tuple-element.20.a_ref, bf16[4,1792,512]{2,1,0:T(8,128)(2,1)} %bitcast.90, bf16[640,640]{1,0:T(8,128)(2,1)} %fusion.4.order_ref, bf16[2,320,512]{2,1,0:T(8,128)(2,1)} %copy-done.14, bf16[2,320,512]{2,1,0:T(8,128)(2,1)} %copy-done.15, ...), custom_call_target="tpu_custom_call" | custom-call | tf_op jit(solution)/shard_map/pallas_call | solution.py:24
  312.1 8.4 %all-to-all-start.6 = ((bf16[16,40,512]{2,1,0:T(8,128)(2,1)}), bf16[16,40,512]{2,1,0:T(8,128)(2,1)S(1)}, u32[]{:S(2)}, u32[]{:S(2)}) async-start(bf16[16,40,512]{2,1,0:T(8,128)(2,1)} %bitcast.101), calls=%async_computation.7 | async-start | bytes 1310720 | tf_op jit(solution)/shard_map/all_to_all | solution.py:349
  321.0 2.5 convert_element_type.101
  323.5 7.7 %shard_map.109 = f32[256,1792]{1,0:T(8,128)} custom-call(s32[1]{0:T(128)} %bitcast.3.at_ref, bf16[4,320,256]{2,1,0:T(8,128)(2,1)} %bitcast.102, bf16[2,320,512]{2,1,0:T(8,128)(2,1)} %bitcast.24.refs_0_, bf16[2,320,512]{2,1,0:T(8,128)(2,1)} %copy-done.7, bf16[320,512]{1,0:T(8,128)(2,1)} %collective-permute-done.11.refs_2_, ...), custom_call_target="tpu_custom_call" | custom-call | tf_op jit(solution)/shard_map/pallas_call | solution.py:24
  331.3 9.1 %all-to-all-done.6 = bf16[16,40,512]{2,1,0:T(8,128)(2,1)S(1)} async-done(((bf16[16,40,512]{2,1,0:T(8,128)(2,1)}), bf16[16,40,512]{2,1,0:T(8,128)(2,1)S(1)}, u32[]{:S(2)}, u32[]{:S(2)}) %all-to-all-start.6) | async-done | bytes 655392 | tf_op jit(solution)/shard_map/all_to_all | solution.py:349
  340.8 0.8 pad_maximum_fusion.1
  341.6 2.5 convert_element_type.103
  (129 shorter events, 8.7 us)
Async XLA Ops:
  7.2 195.6 %all-gather.4.cloned.1.call-start = ((), (), s32[]{:S(2)}) async-start(), calls=%async_computation.11 | async-start | bytes 9175040 | tf_op jit(solution)/shard_map/all_gather | solution.py:365
  10.0 0.7 copy-start.26
  10.0 2.2 copy-start.27
  10.0 2.9 copy-start.24
  10.8 13.5 %copy-start.28 = (bf16[128,1792]{1,0:T(8,128)(2,1)S(1)}, bf16[128,1792]{1,0:T(8,128)(2,1)}, u32[]{:S(2)}) copy-start(bf16[128,1792]{1,0:T(8,128)(2,1)} %param.8) | copy-start | bytes 1376260
  12.3 12.7 %collective-permute-start.8 = (f32[128,4]{0,1:T(4,128)S(1)}, f32[128,4]{0,1:T(4,128)S(1)}, u32[]{:S(2)}, u32[]{:S(2)}) collective-permute-start(f32[128,4]{0,1:T(4,128)S(1)} %pad_maximum_fusion.6), channel_id=1, source_target_pairs={{0,0},{1,64},{2,128},{3,192},{64,1},{65,65},{66,129},{67,193},{128... | collective-permute-start | bytes 6152 | tf_op jit(solution)/shard_map/ppermute | solution.py:344
  13.2 50.6 %copy-start.17 = (bf16[640,128]{1,0:T(8,128)(2,1)}, bf16[640,128]{1,0:T(8,128)(2,1)S(1)}, u32[]{:S(2)}) copy-start(bf16[640,128]{1,0:T(8,128)(2,1)S(1)} %get-tuple-element.60) | copy-start | bytes 491524
  13.2 50.6 %copy-start.19 = (bf16[640,128]{1,0:T(8,128)(2,1)}, bf16[640,128]{1,0:T(8,128)(2,1)S(1)}, u32[]{:S(2)}) copy-start(bf16[640,128]{1,0:T(8,128)(2,1)S(1)} %get-tuple-element.61) | copy-start | bytes 491524
  14.3 26.5 %all-to-all-start.1 = ((bf16[16,40,384]{2,1,0:T(8,128)(2,1)}), bf16[16,40,384]{2,1,0:T(8,128)(2,1)S(1)}, u32[]{:S(2)}, u32[]{:S(2)}) async-start(bf16[16,40,384]{2,1,0:T(8,128)(2,1)} %bitcast.12), calls=%async_computation.1 | async-start | bytes 983040 | tf_op jit(solution)/shard_map/all_to_all | solution.py:349
  24.3 1.1 collective-permute-start.9
  40.8 19.4 %all-to-all-start.3 = ((bf16[16,40,384]{2,1,0:T(8,128)(2,1)}), bf16[16,40,384]{2,1,0:T(8,128)(2,1)S(1)}, u32[]{:S(2)}, u32[]{:S(2)}) async-start(bf16[16,40,384]{2,1,0:T(8,128)(2,1)} %bitcast.27), calls=%async_computation.3 | async-start | bytes 983040 | tf_op jit(solution)/shard_map/all_to_all | solution.py:349
  60.3 23.0 %all-to-all-start.2 = ((bf16[16,40,512]{2,1,0:T(8,128)(2,1)}), bf16[16,40,512]{2,1,0:T(8,128)(2,1)S(1)}, u32[]{:S(2)}, u32[]{:S(2)}) async-start(bf16[16,40,512]{2,1,0:T(8,128)(2,1)} %bitcast.22), calls=%async_computation.2 | async-start | bytes 1310720 | tf_op jit(solution)/shard_map/all_to_all | solution.py:349
  83.2 34.8 %all-to-all-start = ((bf16[16,40,512]{2,1,0:T(8,128)(2,1)}), bf16[16,40,512]{2,1,0:T(8,128)(2,1)}, u32[]{:S(2)}, u32[]{:S(2)}) async-start(bf16[16,40,512]{2,1,0:T(8,128)(2,1)} %bitcast.7), calls=%async_computation | async-start | bytes 1310720 | tf_op jit(solution)/shard_map/all_to_all | solution.py:349
  88.1 27.8 %copy-start.5 = (bf16[640,384]{1,0:T(8,128)(2,1)}, bf16[640,384]{1,0:T(8,128)(2,1)S(1)}, u32[]{:S(2)}) copy-start(bf16[640,384]{1,0:T(8,128)(2,1)S(1)} %fusion.9) | copy-start | bytes 1474564
  88.1 62.0 %collective-permute-start.6 = (bf16[2,320,384]{2,1,0:T(8,128)(2,1)S(1)}, bf16[2,320,384]{2,1,0:T(8,128)(2,1)S(1)}, u32[]{:S(2)}, u32[]{:S(2)}) collective-permute-start(bf16[2,320,384]{2,1,0:T(8,128)(2,1)S(1)} %bitcast.96), channel_id=1, source_target_pairs={{0,3},{1,2},{2,1},{3,0},{4,7},{5,6},{6,5},{7,4},{8,11},{9,10},{10,... | collective-permute-start | bytes 1474568 | tf_op jit(solution)/shard_map/ppermute | solution.py:341
  111.4 78.4 %collective-permute-start.4 = (bf16[2,320,384]{2,1,0:T(8,128)(2,1)S(1)}, bf16[2,320,384]{2,1,0:T(8,128)(2,1)S(1)}, u32[]{:S(2)}, u32[]{:S(2)}) collective-permute-start(bf16[2,320,384]{2,1,0:T(8,128)(2,1)S(1)} %bitcast.97), channel_id=1, source_target_pairs={{0,1},{1,0},{2,3},{3,2},{4,5},{5,4},{6,7},{7,6},{8,9},{9,8},{10,11... | collective-permute-start | bytes 1474568 | tf_op jit(solution)/shard_map/ppermute | solution.py:341
  112.9 20.8 %collective-permute-start.16 = (bf16[2,320,384]{2,1,0:T(8,128)(2,1)}, bf16[2,320,384]{2,1,0:T(8,128)(2,1)S(1)}, u32[]{:S(2)}, u32[]{:S(2)}) collective-permute-start(bf16[2,320,384]{2,1,0:T(8,128)(2,1)} %bitcast.29.refs_5_), channel_id=1, source_target_pairs={{0,3},{1,2},{2,1},{3,0},{4,7},{5,6},{6,5},{7,4},{8,11},{9,10},{10,... | collective-permute-start | bytes 1474568 | tf_op jit(solution)/shard_map/ppermute | solution.py:341
  113.0 21.9 %collective-permute-start.14 = (bf16[2,320,384]{2,1,0:T(8,128)(2,1)}, bf16[2,320,384]{2,1,0:T(8,128)(2,1)}, u32[]{:S(2)}, u32[]{:S(2)}) collective-permute-start(bf16[2,320,384]{2,1,0:T(8,128)(2,1)} %bitcast.29.refs_5_), channel_id=1, source_target_pairs={{0,1},{1,0},{2,3},{3,2},{4,5},{5,4},{6,7},{7,6},{8,9},{9,8},{10,11... | collective-permute-start | bytes 1474568 | tf_op jit(solution)/shard_map/ppermute | solution.py:341
  115.9 31.8 %collective-permute-start.12 = (bf16[2,320,512]{2,1,0:T(8,128)(2,1)}, bf16[2,320,512]{2,1,0:T(8,128)(2,1)S(1)}, u32[]{:S(2)}, u32[]{:S(2)}) collective-permute-start(bf16[2,320,512]{2,1,0:T(8,128)(2,1)} %bitcast.24.refs_0_), channel_id=1, source_target_pairs={{0,3},{1,2},{2,1},{3,0},{4,7},{5,6},{6,5},{7,4},{8,11},{9,10},{10,... | collective-permute-start | bytes 1966088 | tf_op jit(solution)/shard_map/ppermute | solution.py:341
  119.8 46.2 %copy-start.4 = (bf16[640,512]{1,0:T(8,128)(2,1)}, bf16[640,512]{1,0:T(8,128)(2,1)S(1)}, u32[]{:S(2)}) copy-start(bf16[640,512]{1,0:T(8,128)(2,1)S(1)} %fusion.5) | copy-start | bytes 1966084
  133.7 1.2 copy-start.8
  133.7 16.4 %collective-permute-start.10 = (bf16[2,320,512]{2,1,0:T(8,128)(2,1)}, bf16[2,320,512]{2,1,0:T(8,128)(2,1)S(1)}, u32[]{:S(2)}, u32[]{:S(2)}) collective-permute-start(bf16[2,320,512]{2,1,0:T(8,128)(2,1)} %bitcast.24.refs_0_), channel_id=1, source_target_pairs={{0,1},{1,0},{2,3},{3,2},{4,5},{5,4},{6,7},{7,6},{8,9},{9,8},{10,11... | collective-permute-start | bytes 1966088 | tf_op jit(solution)/shard_map/ppermute | solution.py:341
  134.9 26.9 %collective-permute-start.2 = (bf16[2,320,512]{2,1,0:T(8,128)(2,1)S(1)}, bf16[2,320,512]{2,1,0:T(8,128)(2,1)S(1)}, u32[]{:S(2)}, u32[]{:S(2)}) collective-permute-start(bf16[2,320,512]{2,1,0:T(8,128)(2,1)S(1)} %bitcast.91), channel_id=1, source_target_pairs={{0,3},{1,2},{2,1},{3,0},{4,7},{5,6},{6,5},{7,4},{8,11},{9,10},{10,... | collective-permute-start | bytes 1966088 | tf_op jit(solution)/shard_map/ppermute | solution.py:341
  147.7 0.9 copy-start.6
  147.7 14.1 %collective-permute-start.17 = (bf16[320,384]{1,0:T(8,128)(2,1)S(1)}, bf16[320,384]{1,0:T(8,128)(2,1)S(1)}, u32[]{:S(2)}, u32[]{:S(2)}) collective-permute-start(bf16[320,384]{1,0:T(8,128)(2,1)S(1)} %slice_bitcast_fusion.4), channel_id=1, source_target_pairs={{0,1},{1,0},{2,3},{3,2},{4,5},{5,4},{6,7},{7,6},{8,9},{9,8},{10,11... | collective-permute-start | bytes 737288 | tf_op jit(solution)/shard_map/ppermute | solution.py:341
  150.1 17.1 %copy-start.7 = (bf16[2,320,512]{2,1,0:T(8,128)(2,1)}, bf16[2,320,512]{2,1,0:T(8,128)(2,1)S(1)}, u32[]{:S(2)}) copy-start(bf16[2,320,512]{2,1,0:T(8,128)(2,1)S(1)} %collective-permute-done.10.refs_1_) | copy-start | bytes 1966084
  150.1 37.1 %collective-permute-start = (bf16[2,320,512]{2,1,0:T(8,128)(2,1)S(1)}, bf16[2,320,512]{2,1,0:T(8,128)(2,1)S(1)}, u32[]{:S(2)}, u32[]{:S(2)}) collective-permute-start(bf16[2,320,512]{2,1,0:T(8,128)(2,1)S(1)} %bitcast.92), channel_id=1, source_target_pairs={{0,1},{1,0},{2,3},{3,2},{4,5},{5,4},{6,7},{7,6},{8,9},{9,8},{10,11... | collective-permute-start | bytes 1966088 | tf_op jit(solution)/shard_map/ppermute | solution.py:341
  150.1 33.1 %copy-start.2 = (bf16[2,320,384]{2,1,0:T(8,128)(2,1)}, bf16[2,320,384]{2,1,0:T(8,128)(2,1)S(1)}, u32[]{:S(2)}) copy-start(bf16[2,320,384]{2,1,0:T(8,128)(2,1)S(1)} %collective-permute-done.6.refs_4_) | copy-start | bytes 1474564
  150.1 17.1 %collective-permute-start.15 = (bf16[320,384]{1,0:T(8,128)(2,1)S(1)}, bf16[320,384]{1,0:T(8,128)(2,1)S(1)}, u32[]{:S(2)}, u32[]{:S(2)}) collective-permute-start(bf16[320,384]{1,0:T(8,128)(2,1)S(1)} %slice_bitcast_fusion.5), channel_id=1, source_target_pairs={{0,3},{1,2},{2,1},{3,0},{4,7},{5,6},{6,5},{7,4},{8,11},{9,10},{10,... | collective-permute-start | bytes 737288 | tf_op jit(solution)/shard_map/ppermute | solution.py:341
  161.8 21.4 %copy-start = (bf16[2,320,512]{2,1,0:T(8,128)(2,1)}, bf16[2,320,512]{2,1,0:T(8,128)(2,1)S(1)}, u32[]{:S(2)}) copy-start(bf16[2,320,512]{2,1,0:T(8,128)(2,1)S(1)} %collective-permute-done.2.refs_7_.refs_9_) | copy-start | bytes 1966084
  161.8 15.1 %collective-permute-start.13 = (bf16[320,512]{1,0:T(8,128)(2,1)S(1)}, bf16[320,512]{1,0:T(8,128)(2,1)}, u32[]{:S(2)}, u32[]{:S(2)}) collective-permute-start(bf16[320,512]{1,0:T(8,128)(2,1)S(1)} %slice_bitcast_fusion), channel_id=1, source_target_pairs={{0,1},{1,0},{2,3},{3,2},{4,5},{5,4},{6,7},{7,6},{8,9},{9,8},{10,11... | collective-permute-start | bytes 983048 | tf_op jit(solution)/shard_map/ppermute | solution.py:341
  161.8 5.4 %copy-start.12 = (bf16[320,384]{1,0:T(8,128)(2,1)}, bf16[320,384]{1,0:T(8,128)(2,1)S(1)}, u32[]{:S(2)}) copy-start(bf16[320,384]{1,0:T(8,128)(2,1)S(1)} %collective-permute-done.17.refs_8_) | copy-start | bytes 737284
  161.8 15.1 %collective-permute-start.11 = (bf16[320,512]{1,0:T(8,128)(2,1)S(1)}, bf16[320,512]{1,0:T(8,128)(2,1)}, u32[]{:S(2)}, u32[]{:S(2)}) collective-permute-start(bf16[320,512]{1,0:T(8,128)(2,1)S(1)} %slice_bitcast_fusion.1), channel_id=1, source_target_pairs={{0,3},{1,2},{2,1},{3,0},{4,7},{5,6},{6,5},{7,4},{8,11},{9,10},{10,... | collective-permute-start | bytes 983048 | tf_op jit(solution)/shard_map/ppermute | solution.py:341
  167.2 9.7 %copy-start.13 = (bf16[320,384]{1,0:T(8,128)(2,1)}, bf16[320,384]{1,0:T(8,128)(2,1)S(1)}, u32[]{:S(2)}) copy-start(bf16[320,384]{1,0:T(8,128)(2,1)S(1)} %collective-permute-done.15.refs_7_) | copy-start | bytes 737284
  167.2 22.9 %collective-permute-start.7 = (bf16[320,384]{1,0:T(8,128)(2,1)}, bf16[320,384]{1,0:T(8,128)(2,1)}, u32[]{:S(2)}, u32[]{:S(2)}) collective-permute-start(bf16[320,384]{1,0:T(8,128)(2,1)} %slice_bitcast_fusion.6), channel_id=1, source_target_pairs={{0,1},{1,0},{2,3},{3,2},{4,5},{5,4},{6,7},{7,6},{8,9},{9,8},{10,11... | collective-permute-start | bytes 737288 | tf_op jit(solution)/shard_map/ppermute | solution.py:341
  176.9 32.3 %collective-permute-start.3 = (bf16[320,512]{1,0:T(8,128)(2,1)}, bf16[320,512]{1,0:T(8,128)(2,1)}, u32[]{:S(2)}, u32[]{:S(2)}) collective-permute-start(bf16[320,512]{1,0:T(8,128)(2,1)} %slice_bitcast_fusion.2), channel_id=1, source_target_pairs={{0,1},{1,0},{2,3},{3,2},{4,5},{5,4},{6,7},{7,6},{8,9},{9,8},{10,11... | collective-permute-start | bytes 983048 | tf_op jit(solution)/shard_map/ppermute | solution.py:341
  183.2 26.0 %all-to-all-start.4 = ((bf16[4,320,256]{2,1,0:T(8,128)(2,1)}), bf16[4,320,256]{2,1,0:T(8,128)(2,1)S(1)}, u32[]{:S(2)}, u32[]{:S(2)}) async-start(bf16[4,320,256]{2,1,0:T(8,128)(2,1)} %shard_map.103), calls=%async_computation.4 | async-start | bytes 1310720 | tf_op jit(solution)/shard_map/all_to_all | solution.py:402
  187.1 133.9 %reduce-scatter.3.cloned.1.call-start = ((), (), s32[]{:S(2)}) async-start(), calls=%async_computation.9 | async-start | bytes 4587520 | tf_op jit(solution)/shard_map/reduce_scatter | solution.py:407
  187.1 15.6 %copy-start.1 = (bf16[2,320,512]{2,1,0:T(8,128)(2,1)}, bf16[2,320,512]{2,1,0:T(8,128)(2,1)S(1)}, u32[]{:S(2)}) copy-start(bf16[2,320,512]{2,1,0:T(8,128)(2,1)S(1)} %collective-permute-done.refs_6_) | copy-start | bytes 1966084
  187.2 22.1 %collective-permute-start.1 = (bf16[320,512]{1,0:T(8,128)(2,1)S(1)}, bf16[320,512]{1,0:T(8,128)(2,1)S(1)}, u32[]{:S(2)}, u32[]{:S(2)}) collective-permute-start(bf16[320,512]{1,0:T(8,128)(2,1)S(1)} %slice_bitcast_fusion.3), channel_id=1, source_target_pairs={{0,3},{1,2},{2,1},{3,0},{4,7},{5,6},{6,5},{7,4},{8,11},{9,10},{10,... | collective-permute-start | bytes 983048 | tf_op jit(solution)/shard_map/ppermute | solution.py:341
  189.8 13.0 %copy-start.3 = (bf16[2,320,384]{2,1,0:T(8,128)(2,1)}, bf16[2,320,384]{2,1,0:T(8,128)(2,1)S(1)}, u32[]{:S(2)}) copy-start(bf16[2,320,384]{2,1,0:T(8,128)(2,1)S(1)} %collective-permute-done.4.refs_1_) | copy-start | bytes 1474564
  189.8 12.9 %collective-permute-start.5 = (bf16[320,384]{1,0:T(8,128)(2,1)S(1)}, bf16[320,384]{1,0:T(8,128)(2,1)S(1)}, u32[]{:S(2)}, u32[]{:S(2)}) collective-permute-start(bf16[320,384]{1,0:T(8,128)(2,1)S(1)} %slice_bitcast_fusion.7), channel_id=1, source_target_pairs={{0,3},{1,2},{2,1},{3,0},{4,7},{5,6},{6,5},{7,4},{8,11},{9,10},{10,... | collective-permute-start | bytes 737288 | tf_op jit(solution)/shard_map/ppermute | solution.py:341
  202.7 0.7 copy-start.11
  209.2 0.7 copy-start.9
  210.0 0.8 copy-start.10
  219.8 121.9 %reduce-scatter.5.cloned.1.call-start = ((), (), s32[]{:S(2)}) async-start(), calls=%async_computation.10 | async-start | bytes 4587520 | tf_op jit(solution)/shard_map/reduce_scatter | solution.py:416
  231.2 12.1 %collective-permute-start.18 = (bf16[2,320,384]{2,1,0:T(8,128)(2,1)}, bf16[2,320,384]{2,1,0:T(8,128)(2,1)S(1)}, u32[]{:S(2)}, u32[]{:S(2)}) collective-permute-start(bf16[2,320,384]{2,1,0:T(8,128)(2,1)} %get-tuple-element.21), channel_id=1, source_target_pairs={{0,1},{1,0},{2,3},{3,2},{4,5},{5,4},{6,7},{7,6},{8,9},{9,8},{10,11... | collective-permute-start | bytes 1474568 | tf_op jit(solution)/shard_map/ppermute | solution.py:341
  232.1 24.2 %collective-permute-start.19 = (bf16[2,320,384]{2,1,0:T(8,128)(2,1)}, bf16[2,320,384]{2,1,0:T(8,128)(2,1)S(1)}, u32[]{:S(2)}, u32[]{:S(2)}) collective-permute-start(bf16[2,320,384]{2,1,0:T(8,128)(2,1)} %get-tuple-element.22), channel_id=1, source_target_pairs={{0,2},{1,3},{2,0},{3,1},{4,6},{5,7},{6,4},{7,5},{8,10},{9,11},{10,... | collective-permute-start | bytes 1474568 | tf_op jit(solution)/shard_map/ppermute | solution.py:341
  235.4 23.2 %collective-permute-start.20 = (bf16[2,320,384]{2,1,0:T(8,128)(2,1)}, bf16[2,320,384]{2,1,0:T(8,128)(2,1)S(1)}, u32[]{:S(2)}, u32[]{:S(2)}) collective-permute-start(bf16[2,320,384]{2,1,0:T(8,128)(2,1)} %get-tuple-element.23), channel_id=1, source_target_pairs={{0,3},{1,2},{2,1},{3,0},{4,7},{5,6},{6,5},{7,4},{8,11},{9,10},{10,... | collective-permute-start | bytes 1474568 | tf_op jit(solution)/shard_map/ppermute | solution.py:341
  243.2 15.3 %copy-start.21 = (bf16[2,320,384]{2,1,0:T(8,128)(2,1)}, bf16[2,320,384]{2,1,0:T(8,128)(2,1)S(1)}, u32[]{:S(2)}) copy-start(bf16[2,320,384]{2,1,0:T(8,128)(2,1)S(1)} %collective-permute-done.18.refs_0_) | copy-start | bytes 1474564
  256.4 2.2 copy-start.22
  258.5 0.8 copy-start.23
  263.8 48.4 %all-to-all-start.5 = ((bf16[16,40,384]{2,1,0:T(8,128)(2,1)}), bf16[16,40,384]{2,1,0:T(8,128)(2,1)S(1)}, u32[]{:S(2)}, u32[]{:S(2)}) async-start(bf16[16,40,384]{2,1,0:T(8,128)(2,1)} %bitcast.103), calls=%async_computation.5 | async-start | bytes 983040 | tf_op jit(solution)/shard_map/all_to_all | solution.py:349
  269.6 8.3 %copy-start.25 = (bf16[320,256]{1,0:T(8,128)(2,1)S(1)}, bf16[320,256]{1,0:T(8,128)(2,1)}, u32[]{:S(2)}) copy-start(bf16[320,256]{1,0:T(8,128)(2,1)} %get-tuple-element.27) | copy-start | bytes 491524
  273.9 20.1 %collective-permute-start.21 = (bf16[2,320,512]{2,1,0:T(8,128)(2,1)}, bf16[2,320,512]{2,1,0:T(8,128)(2,1)S(1)}, u32[]{:S(2)}, u32[]{:S(2)}) collective-permute-start(bf16[2,320,512]{2,1,0:T(8,128)(2,1)} %get-tuple-element.24), channel_id=1, source_target_pairs={{0,1},{1,0},{2,3},{3,2},{4,5},{5,4},{6,7},{7,6},{8,9},{9,8},{10,11... | collective-permute-start | bytes 1966088 | tf_op jit(solution)/shard_map/ppermute | solution.py:341
  274.0 30.0 %collective-permute-start.22 = (bf16[2,320,512]{2,1,0:T(8,128)(2,1)}, bf16[2,320,512]{2,1,0:T(8,128)(2,1)S(1)}, u32[]{:S(2)}, u32[]{:S(2)}) collective-permute-start(bf16[2,320,512]{2,1,0:T(8,128)(2,1)} %get-tuple-element.25), channel_id=1, source_target_pairs={{0,2},{1,3},{2,0},{3,1},{4,6},{5,7},{6,4},{7,5},{8,10},{9,11},{10,... | collective-permute-start | bytes 1966088 | tf_op jit(solution)/shard_map/ppermute | solution.py:341
  275.1 31.1 %collective-permute-start.23 = (bf16[2,320,512]{2,1,0:T(8,128)(2,1)}, bf16[2,320,512]{2,1,0:T(8,128)(2,1)S(1)}, u32[]{:S(2)}, u32[]{:S(2)}) collective-permute-start(bf16[2,320,512]{2,1,0:T(8,128)(2,1)} %get-tuple-element.26), channel_id=1, source_target_pairs={{0,3},{1,2},{2,1},{3,0},{4,7},{5,6},{6,5},{7,4},{8,11},{9,10},{10,... | collective-permute-start | bytes 1966088 | tf_op jit(solution)/shard_map/ppermute | solution.py:341
  294.0 12.3 %copy-start.14 = (bf16[2,320,512]{2,1,0:T(8,128)(2,1)}, bf16[2,320,512]{2,1,0:T(8,128)(2,1)S(1)}, u32[]{:S(2)}) copy-start(bf16[2,320,512]{2,1,0:T(8,128)(2,1)S(1)} %collective-permute-done.21.refs_0_) | copy-start | bytes 1966084
  304.0 2.2 copy-start.15
  306.3 0.9 copy-start.16
  307.1 13.4 %copy-start.18 = (bf16[640,128]{1,0:T(8,128)(2,1)S(1)}, bf16[640,128]{1,0:T(8,128)(2,1)}, u32[]{:S(2)}) copy-start(bf16[640,128]{1,0:T(8,128)(2,1)} %copy-done.17) | copy-start | bytes 491524
  307.1 13.4 %copy-start.20 = (bf16[640,128]{1,0:T(8,128)(2,1)S(1)}, bf16[640,128]{1,0:T(8,128)(2,1)}, u32[]{:S(2)}) copy-start(bf16[640,128]{1,0:T(8,128)(2,1)} %copy-done.19) | copy-start | bytes 491524
  312.1 28.3 %all-to-all-start.6 = ((bf16[16,40,512]{2,1,0:T(8,128)(2,1)}), bf16[16,40,512]{2,1,0:T(8,128)(2,1)S(1)}, u32[]{:S(2)}, u32[]{:S(2)}) async-start(bf16[16,40,512]{2,1,0:T(8,128)(2,1)} %bitcast.101), calls=%async_computation.7 | async-start | bytes 1310720 | tf_op jit(solution)/shard_map/all_to_all | solution.py:349
Sparse Core Ops, SparseCore 0:
  10.4 96.1 all-gather.3
  219.9 42.5 reduce-scatter.2
  265.0 50.1 reduce-scatter.4
